TPU v7x, 32 devices: a whole 2x2x4 slice. The times are simulated.
32 devices in a mesh: groups: 2 (over y), dp: 2 (over x), expert: 8 (over z, core).
Axes of the slice: x: 2, y: 2, z: 4, core: 2. Of those that a mesh axis runs over, the one named last changes fastest.
Arguments:
- tokens: bfloat16 [4096, 2048], P(('groups', 'dp', 'expert')), parts along dimension 0, may hold values from -6 to 6
- routes: int32 [4096, 4], P(('groups', 'dp', 'expert')), parts along dimension 0, may hold values from 0 to 7, all different within a row; in each aligned block of 128 rows (0 to 127, 128 to 255, ...) at most 128 rows name the same one
- w_gate: bfloat16 [16, 2048, 512], P(('groups', 'expert')), parts along dimension 0, may hold values from -0.125 to 0.125
- w_up: bfloat16 [16, 2048, 512], P(('groups', 'expert')), parts along dimension 0, may hold values from -0.125 to 0.125
Outputs:
- r_factor: float32 [16, 512, 512], P(('groups', 'expert'), 'dp'), parts along dimension 0
There are 2 independent parts, one for each index of `groups`. A program takes and returns all parts, laid end to end along the dimension named above; each array names one. Nothing has to cross between parts.
Inputs may be any that keep to these rules, and one draw needn't show every extreme that they name: `routes`: each row names 4 different experts. In each aligned block of 128 rows (the tokens of one device) no expert is named by more than 128 rows, and in some block some expert is named by exactly 128 rows.
All inputs are finite; a program needn't handle non-finite values.
Results may differ from a plain program's by a relative error of at most 0.0027.
Values may be sent and summed in bfloat16 or wider, within the bound.
No kernel may reach another device: no remote copies, remote signals or barrier semaphores. Data moves between devices by JAX's collectives and lax.ppermute only.
A program may use at most 64 MiB of HBM per device.

v0:
```python
import functools

import jax
import jax.numpy as jnp
from jax import lax
from jax.experimental import pallas as pl
from jax.experimental.pallas import tpu as pltpu
from jax.sharding import PartitionSpec as P


RIDGE = 0.05
CORES = 2
CHIPS_DENSE = 4


def hidden_kernel(me_ref, gate_ref, up_ref, *refs, at, top):
    hidden_ref = refs[-1]
    count = len(refs) // 2
    pieces, names = refs[:count], refs[count:-1]
    hw = gate_ref.shape[1]
    width = 256
    member = []
    for name in names:
        hit = (name[at * top : (at + 1) * top, :] == me_ref[0]).astype(jnp.float32)
        member.append(jnp.max(hit.T, axis=1, keepdims=True))
    member = jnp.concatenate(member, axis=0)
    x = jnp.concatenate([piece[...] for piece in pieces], axis=0)

    def step(i, carry):
        columns = pl.ds(pl.multiple_of(i * width, width), width)
        gate = jnp.dot(x, gate_ref[:, columns], preferred_element_type=jnp.float32)
        up = jnp.dot(x, up_ref[:, columns], preferred_element_type=jnp.float32)
        value = gate / (1.0 + jnp.exp(-gate)) * up
        hidden_ref[:, columns] = jnp.where(member > 0, value, 0.0).astype(jnp.bfloat16)
        return carry

    lax.fori_loop(0, hw // width, step, 0)


def hidden_of(me, pieces, names, at, top, gate_w, up_w):
    rows = sum(piece.shape[0] for piece in pieces)
    model, hw = gate_w.shape
    return pl.pallas_call(
        functools.partial(hidden_kernel, at=at, top=top),
        in_specs=[pl.BlockSpec(memory_space=pltpu.SMEM)]
        + [pl.BlockSpec(memory_space=pltpu.VMEM)] * (2 + 2 * len(pieces)),
        out_specs=pl.BlockSpec(memory_space=pltpu.VMEM),
        out_shape=jax.ShapeDtypeStruct((rows, hw), jnp.bfloat16),
        compiler_params=pltpu.CompilerParams(vmem_limit_bytes=24 << 20),
        cost_estimate=pl.CostEstimate(
            flops=2 * rows * model * 2 * hw,
            bytes_accessed=2 * (rows * model + 2 * model * hw) + 2 * rows * hw,
            transcendentals=rows * hw,
        ),
        name="hidden",
    )(me, gate_w, up_w, *pieces, *names)


def gram_of(refs):
    total = None
    for ref in refs:
        h = ref[...]
        part = lax.dot_general(h, h, (((0,), (0,)), ((), ())), preferred_element_type=jnp.float32)
        total = part if total is None else total + part
    return total


def gram_kernel(*refs):
    refs[-1][...] = gram_of(refs[:-1])


def partial_gram(hiddens):
    rows = sum(hidden.shape[0] for hidden in hiddens)
    hw = hiddens[0].shape[1]
    return pl.pallas_call(
        gram_kernel,
        in_specs=[pl.BlockSpec(memory_space=pltpu.VMEM)] * len(hiddens),
        out_specs=pl.BlockSpec(memory_space=pltpu.VMEM),
        out_shape=jax.ShapeDtypeStruct((hw, hw), jnp.float32),
        compiler_params=pltpu.CompilerParams(vmem_limit_bytes=24 << 20),
        cost_estimate=pl.CostEstimate(
            flops=2 * rows * hw * hw,
            bytes_accessed=2 * rows * hw + 4 * hw * hw,
            transcendentals=0,
        ),
        name="partial_gram",
    )(*hiddens)


def between_chips(pairs):
    return [(s * CORES + c, d * CORES + c) for s, d in pairs for c in range(CORES)]


def gathered(tokens, routes, gate_w, up_w):
    me = lax.axis_index("expert").astype(jnp.int32).reshape(1)
    data_ranks = lax.axis_size("dp")
    top = routes.shape[1]
    move = lambda x, pairs: lax.ppermute(x, "expert", between_chips(pairs))
    swap = lambda x: lax.ppermute(x, "expert", [(e, e ^ 1) for e in range(CHIPS_DENSE * CORES)])
    turn = lambda x, s: lax.ppermute(x, "dp", [(r, (r + s) % data_ranks) for r in range(data_ranks)])
    ring = lambda s: [(z, (z + s) % CHIPS_DENSE) for z in range(CHIPS_DENSE)]

    names = routes.T
    above = move(tokens, ring(-1))
    below = move(tokens, ring(1))
    on_down = move(above, [(2, 1), (1, 0)])
    on_up = move(below, [(1, 2), (2, 3)])
    moved = []
    for pairs in [ring(-1), ring(1), ring(2)]:
        moved.append(move(names, pairs))
    moved = jnp.concatenate(moved, axis=0)
    other_names = swap(names)
    other_moved = swap(moved)

    hiddens = []
    for slot, own in enumerate([tokens, above, below]):
        other = swap(own)
        who, at = ((names, other_names), 0) if slot == 0 else ((moved, other_moved), slot - 1)
        hidden = hidden_of(me, (own, other), who, at, top, gate_w, up_w)
        hiddens.append([hidden] + [turn(hidden, s) for s in range(1, data_ranks)])
    early = partial_gram(sum(hiddens, []))

    last = on_up + on_down
    other = swap(last)
    late = []
    for piece, who in ((last, moved), (other, other_moved)):
        hidden = hidden_of(me, (piece,), (who,), 2, top, gate_w, up_w)
        late += [hidden] + [turn(hidden, s) for s in range(1, data_ranks)]
    return early, late


def packed_grams(tokens, routes, gate_w, up_w, capacity):
    owners = lax.axis_size("expert")
    experts = owners
    model_width = tokens.shape[1]
    tok_rows, top_count = routes.shape
    assigned = routes.reshape(-1)
    onehot = (assigned[:, None] == jnp.arange(experts, dtype=jnp.int32)[None, :]).astype(jnp.int32)
    position = jnp.sum(jnp.cumsum(onehot, axis=0) * onehot, axis=1) - 1
    target = assigned * capacity + position
    anchor = jnp.arange(tok_rows * top_count, dtype=jnp.int32) // top_count
    source_row = jnp.zeros((experts * capacity,), jnp.int32).at[target].set(anchor)
    filled = jnp.zeros((experts * capacity,), jnp.int32).at[target].set(1)
    outbox = jnp.where(filled[:, None] > 0, tokens[source_row], jnp.zeros((), tokens.dtype))
    outbox = outbox.reshape(experts, capacity, model_width)
    arrived = lax.all_to_all(outbox, "expert", split_axis=0, concat_axis=0, tiled=True)
    flattened = arrived.reshape(-1, model_width)
    gate_proj = jnp.dot(flattened, gate_w, preferred_element_type=jnp.float32)
    up_proj = jnp.dot(flattened, up_w, preferred_element_type=jnp.float32)
    hidden = (jax.nn.silu(gate_proj) * up_proj).astype(jnp.bfloat16)
    return lax.dot_general(hidden, hidden, (((0,), (0,)), ((), ())), preferred_element_type=jnp.float32)


def body(tokens, routes, w_gate, w_up):
    owners = lax.axis_size("expert")
    data_ranks = lax.axis_size("dp")
    experts = w_gate.shape[0] * owners
    tok_rows, top_count = routes.shape
    capacity = min(tok_rows, 2 * tok_rows * top_count // experts)
    gate_w, up_w = w_gate[0], w_up[0]
    if tok_rows * owners <= experts * capacity and owners == CHIPS_DENSE * CORES:
        early, late = gathered(tokens, routes, gate_w, up_w)
    else:
        gram = packed_grams(tokens, routes, gate_w, up_w, capacity)
        early, late = gram, []
        for s in range(1, data_ranks):
            early = early + lax.ppermute(gram, "dp", [(r, (r + s) % data_ranks) for r in range(data_ranks)])
    rows_mean = data_ranks * tok_rows * top_count
    return factor_rows(early, late, rows_mean, data_ranks)[None]


def over_lanes(column, width):
    return jnp.concatenate([column] * (width // column.shape[1]), axis=1)


def row_of(x, k):
    return jnp.broadcast_to(x[k : k + 1, :], x.shape)


def lane_of(x, at):
    return jnp.take_along_axis(x, jnp.full(x.shape, at, jnp.int32), axis=1, mode="promise_in_bounds")


PRODUCTS = ((0, 0), (0, 1), (1, 0), (0, 2), (2, 0), (1, 1))


def three_parts(x):
    high = x.astype(jnp.bfloat16).astype(jnp.float32)
    rest = x - high
    middle = rest.astype(jnp.bfloat16).astype(jnp.float32)
    return high, middle, rest - middle


def outer_of_few(a, b):
    left, right = three_parts(a), three_parts(b)
    left = jnp.concatenate([left[i] for i, _ in PRODUCTS], axis=0)
    right = jnp.concatenate([right[j] for _, j in PRODUCTS], axis=0).astype(jnp.bfloat16)
    return jnp.dot(left.T.astype(jnp.bfloat16), right, preferred_element_type=jnp.float32)


def outer_of_many(a, b):
    left, right = three_parts(a.T), three_parts(b)
    left = jnp.concatenate([left[i].astype(jnp.bfloat16) for i, _ in PRODUCTS], axis=1)
    right = jnp.concatenate([right[j].astype(jnp.bfloat16) for _, j in PRODUCTS], axis=0)
    return jnp.dot(left, right, preferred_element_type=jnp.float32)


def factor_panel(rows, column, sublane):
    group, width = rows[0].shape
    count = len(rows)
    extract = lambda u: {t: [column(rows[t], u, j) for j in range(group)] for t in range(u, count)}
    current, done = extract(0), []
    for s in range(count):
        ahead = extract(s + 1) if s + 1 < count else {}
        factor = jnp.zeros_like(rows[s])
        for k in range(group):
            pivot = current[s][k]
            scale = lax.rsqrt(row_of(pivot, k))
            lower = {t: current[t][k] * scale for t in range(s, count)}
            if k + 1 < group:
                current[s][k + 1] = current[s][k + 1] - pivot * row_of(pivot, k + 1) * (scale * scale)
            upper = row_of(rows[s], k) * over_lanes(scale, width)
            factor = jnp.where(sublane == k, upper, factor)
            for j in range(k + 1, group):
                entry = row_of(lower[s], j)
                for t in range(s, count):
                    if (t, j) != (s, k + 1):
                        current[t][j] = current[t][j] - lower[t] * entry
            for j in range(group if ahead else 0):
                entry = row_of(lower[s + 1], j)
                for t in range(s + 1, count):
                    ahead[t][j] = ahead[t][j] - lower[t] * entry
            for t in range(s if k + 1 < group else s + 1, count):
                rows[t] = rows[t] - over_lanes(lower[t], width) * upper
        done.append(factor)
        current = ahead
    return done


def factor_kernel(rank_ref, early_ref, *refs, rows_mean):
    late_refs, (my_rows_ref, out_ref, rest_ref) = refs[:-3], refs[-3:]
    size = early_ref.shape[0]
    block, group, groups = 128, 8, 4
    panel = group * groups
    row = lax.broadcasted_iota(jnp.int32, (size, size), 0)
    col = lax.broadcasted_iota(jnp.int32, (size, size), 1)
    gram = early_ref[...]
    if late_refs:
        gram = gram + gram_of(late_refs)
    rest_ref[...] = gram / rows_mean + jnp.where(row == col, RIDGE, 0.0)
    for base in range(0, size, block):
        width = size - base
        end = base + block
        if base:
            out_ref[base:end, :base] = jnp.zeros((block, base), jnp.float32)
        sublane = lax.broadcasted_iota(jnp.int32, (group, width), 0)
        lane = lax.broadcasted_iota(jnp.int32, (group, width), 1)
        panel_lane = lax.broadcasted_iota(jnp.int32, (panel, block), 1)

        def step(p, carry):
            first = panel * p
            at = [pl.ds(pl.multiple_of(base + first + group * t, group), group) for t in range(groups)]
            rows = [rest_ref[at[t], base:] for t in range(groups)]
            column = lambda x, u, j: lane_of(x[:, :block], first + group * u + j)
            done = factor_panel(rows, column, sublane)
            for t in range(groups):
                out_ref[at[t], base:] = jnp.where(lane >= sublane + first + group * t, done[t], 0.0)
            done = jnp.concatenate(done, axis=0)

            @pl.when(p + 1 < block // panel)
            def _():
                below = jnp.where(panel_lane >= first + panel, done[:, :block], 0.0)
                rest_ref[base:end, base:] -= outer_of_few(below, done)

            return carry

        lax.fori_loop(0, block // panel, step, 0)
        for to in range(end, size, block):
            right = out_ref[base:end, to:]
            rest_ref[to : to + block, to:] -= outer_of_many(right[:, :block], right)
    count = my_rows_ref.shape[0]
    my_rows_ref[...] = out_ref[pl.ds(pl.multiple_of(rank_ref[0] * count, count), count), :]


def factor_rows(early, late, rows_mean, data_ranks):
    size = early.shape[0]
    rank = lax.axis_index("dp").astype(jnp.int32).reshape(1)
    return pl.pallas_call(
        functools.partial(factor_kernel, rows_mean=rows_mean),
        in_specs=[pl.BlockSpec(memory_space=pltpu.SMEM)] + [pl.BlockSpec(memory_space=pltpu.VMEM)] * (1 + len(late)),
        out_specs=pl.BlockSpec(memory_space=pltpu.VMEM),
        out_shape=jax.ShapeDtypeStruct((size // data_ranks, size), jnp.float32),
        scratch_shapes=[pltpu.VMEM((size, size), jnp.float32)] * 2,
        compiler_params=pltpu.CompilerParams(vmem_limit_bytes=24 << 20),
        name="factor",
    )(rank, early, *late)


def solution(mesh):
    in_specs = (
        P(("groups", "dp", "expert"), None),
        P(("groups", "dp", "expert"), None),
        P(("groups", "expert"), None, None),
        P(("groups", "expert"), None, None),
    )
    out_specs = P(("groups", "expert"), "dp", None)
    return jax.shard_map(body, mesh=mesh, in_specs=in_specs, out_specs=out_specs, check_vma=False)
```

profile of v0, /device:TPU:0, one launch (start us, length us, event | category | flops | bytes accessed | tf_op | source)
XLA Modules:
  0.0 96.8 jit_solution(146745441510299291)
XLA Ops:
  0.0 3.1 %collective-permute-start.10 = (bf16[128,2048]{1,0:T(8,128)(2,1)}, bf16[128,2048]{1,0:T(8,128)(2,1)S(1)}, u32[]{:S(2)}, u32[]{:S(2)}) collective-permute-start(bf16[128,2048]{1,0:T(8,128)(2,1)} %refs_0_.1), channel_id=1, source_target_pairs={{0,2},{1,3},{2,4},{3,5},{4,6},{5,7},{6,0},{7,1},{8,10},{9,11},{10,... | collective-permute-start | bytes 1572872 | tf_op jit(solution)/shard_map/ppermute | solution.py:98
  3.1 2.0 %collective-permute-start.3 = (bf16[128,2048]{1,0:T(8,128)(2,1)}, bf16[128,2048]{1,0:T(8,128)(2,1)S(1)}, u32[]{:S(2)}, u32[]{:S(2)}) collective-permute-start(bf16[128,2048]{1,0:T(8,128)(2,1)} %refs_0_.1), channel_id=1, source_target_pairs={{0,6},{1,7},{2,0},{3,1},{4,2},{5,3},{6,4},{7,5},{8,14},{9,15},{10,... | collective-permute-start | bytes 1572872 | tf_op jit(solution)/shard_map/ppermute | solution.py:98
  5.1 13.0 %collective-permute-done.10.refs_0_ = bf16[128,2048]{1,0:T(8,128)(2,1)S(1)} collective-permute-done((bf16[128,2048]{1,0:T(8,128)(2,1)}, bf16[128,2048]{1,0:T(8,128)(2,1)S(1)}, u32[]{:S(2)}, u32[]{:S(2)}) %collective-permute-start.10) | collective-permute-done | bytes 524320 | tf_op jit(solution)/shard_map/ppermute | solution.py:98
  18.8 9.1 %collective-permute-done.3.refs_0_ = bf16[128,2048]{1,0:T(8,128)(2,1)S(1)} collective-permute-done((bf16[128,2048]{1,0:T(8,128)(2,1)}, bf16[128,2048]{1,0:T(8,128)(2,1)S(1)}, u32[]{:S(2)}, u32[]{:S(2)}) %collective-permute-start.3) | collective-permute-done | bytes 524320 | tf_op jit(solution)/shard_map/ppermute | solution.py:98
  27.9 1.3 %collective-permute-start.14 = (bf16[128,2048]{1,0:T(8,128)(2,1)S(1)}, bf16[128,2048]{1,0:T(8,128)(2,1)S(1)}, u32[]{:S(2)}, u32[]{:S(2)}) collective-permute-start(bf16[128,2048]{1,0:T(8,128)(2,1)S(1)} %collective-permute-done.3.refs_0_), channel_id=1, source_target_pairs={{4,2},{5,3},{2,0},{3,1},{12,10},{13,11},{10,8},{11,9},{20,18},{21,... | collective-permute-start | bytes 1572872 | tf_op jit(solution)/shard_map/ppermute | solution.py:98
  29.7 5.9 %collective-permute-start.7 = (s32[4,128]{1,0:T(4,128)}, s32[4,128]{1,0:T(4,128)S(1)}, u32[]{:S(2)}, u32[]{:S(2)}) collective-permute-start(s32[4,128]{1,0:T(4,128)} %bitcast.16), channel_id=1, source_target_pairs={{0,4},{1,5},{2,6},{3,7},{4,0},{5,1},{6,2},{7,3},{8,12},{9,13},{10,... | collective-permute-start | bytes 6152 | tf_op jit(solution)/shard_map/ppermute | solution.py:98
  35.7 8.6 %collective-permute-done.7 = s32[4,128]{1,0:T(4,128)S(1)} collective-permute-done((s32[4,128]{1,0:T(4,128)}, s32[4,128]{1,0:T(4,128)S(1)}, u32[]{:S(2)}, u32[]{:S(2)}) %collective-permute-start.7) | collective-permute-done | bytes 2080 | tf_op jit(solution)/shard_map/ppermute | solution.py:98
  45.1 3.8 %collective-permute-start.5 = (s32[4,128]{1,0:T(4,128)}, s32[4,128]{1,0:T(4,128)S(1)}, u32[]{:S(2)}, u32[]{:S(2)}) collective-permute-start(s32[4,128]{1,0:T(4,128)} %bitcast.18), channel_id=1, source_target_pairs={{0,6},{1,7},{2,0},{3,1},{4,2},{5,3},{6,4},{7,5},{8,14},{9,15},{10,... | collective-permute-start | bytes 6152 | tf_op jit(solution)/shard_map/ppermute | solution.py:98
  48.9 1.2 %add.3.refs_0_ = bf16[128,2048]{1,0:T(8,128)(2,1)S(1)} add(bf16[128,2048]{1,0:T(8,128)(2,1)S(1)} %collective-permute-done.13, bf16[128,2048]{1,0:T(8,128)(2,1)} %copy-done.4) | non-fusion elementwise | flops 262144 | bytes 1572864 | tf_op jit(solution)/shard_map/add | solution.py:123
  51.7 1.6 %copy-done = bf16[1,2048,512]{2,1,0:T(8,128)(2,1)S(1)} copy-done((bf16[1,2048,512]{2,1,0:T(8,128)(2,1)S(1)}, bf16[1,2048,512]{2,1,0:T(8,128)(2,1)}, u32[]{:S(2)}) %copy-start) | copy-done | bytes 2097176
  53.3 1.6 %copy-done.1 = bf16[1,2048,512]{2,1,0:T(8,128)(2,1)S(1)} copy-done((bf16[1,2048,512]{2,1,0:T(8,128)(2,1)S(1)}, bf16[1,2048,512]{2,1,0:T(8,128)(2,1)}, u32[]{:S(2)}) %copy-start.1) | copy-done | bytes 2097176
  56.6 1.7 %hidden.5.refs_0_ = bf16[256,512]{1,0:T(8,128)(2,1)S(1)} custom-call(s32[1]{0:T(128)} %bitcast.1.me_ref, bf16[2048,512]{1,0:T(8,128)(2,1)S(1)} %bitcast.6, bf16[2048,512]{1,0:T(8,128)(2,1)S(1)} %bitcast.11, bf16[128,2048]{1,0:T(8,128)(2,1)S(1)} %copy-done.2, bf16[128,2048]{1,0:T(8,128)(2,1)S(1)} %collective-permute-done.refs_1_, s32[4,128]{1,0:T(4,128)S(1)} %bitcast.20, ...), custom_call_target="tpu_custom_call" | custom-call | flops 1073741824 | bytes 5505024 | tf_op jit(solution)/shard_map/hidden/pallas_call | solution.py:43
  58.3 1.6 %collective-permute-start.2 = (bf16[256,512]{1,0:T(8,128)(2,1)S(1)}, bf16[256,512]{1,0:T(8,128)(2,1)S(1)}, u32[]{:S(2)}, u32[]{:S(2)}) collective-permute-start(bf16[256,512]{1,0:T(8,128)(2,1)S(1)} %hidden.5.refs_0_), channel_id=1, source_target_pairs={{0,8},{8,0},{1,9},{9,1},{2,10},{10,2},{3,11},{11,3},{4,12},{12,4},... | collective-permute-start | bytes 786440 | tf_op jit(solution)/shard_map/ppermute | solution.py:100
  59.9 1.7 %hidden.7.refs_4_ = bf16[256,512]{1,0:T(8,128)(2,1)S(1)} custom-call(s32[1]{0:T(128)} %bitcast.1.me_ref, bf16[2048,512]{1,0:T(8,128)(2,1)S(1)} %bitcast.7, bf16[2048,512]{1,0:T(8,128)(2,1)S(1)} %bitcast.12, bf16[128,2048]{1,0:T(8,128)(2,1)S(1)} %collective-permute-done.10.refs_0_, bf16[128,2048]{1,0:T(8,128)(2,1)S(1)} %collective-permute-done.11.refs_1_, ...), custom_call_target="tpu_custom_call" | custom-call | flops 1073741824 | bytes 5505024 | tf_op jit(solution)/shard_map/hidden/pallas_call | solution.py:43
  62.2 1.7 %hidden.6.refs_2_ = bf16[256,512]{1,0:T(8,128)(2,1)S(1)} custom-call(s32[1]{0:T(128)} %bitcast.1.me_ref, bf16[2048,512]{1,0:T(8,128)(2,1)S(1)} %bitcast.8, bf16[2048,512]{1,0:T(8,128)(2,1)S(1)} %bitcast.13, bf16[128,2048]{1,0:T(8,128)(2,1)S(1)} %collective-permute-done.3.refs_0_, bf16[128,2048]{1,0:T(8,128)(2,1)S(1)} %collective-permute-done.4.refs_1_, ...), custom_call_target="tpu_custom_call" | custom-call | flops 1073741824 | bytes 5505024 | tf_op jit(solution)/shard_map/hidden/pallas_call | solution.py:43
  63.9 1.6 %collective-permute-start.9 = (bf16[256,512]{1,0:T(8,128)(2,1)S(1)}, bf16[256,512]{1,0:T(8,128)(2,1)S(1)}, u32[]{:S(2)}, u32[]{:S(2)}) collective-permute-start(bf16[256,512]{1,0:T(8,128)(2,1)S(1)} %hidden.6.refs_2_), channel_id=1, source_target_pairs={{0,8},{8,0},{1,9},{9,1},{2,10},{10,2},{3,11},{11,3},{4,12},{12,4},... | collective-permute-start | bytes 786440 | tf_op jit(solution)/shard_map/ppermute | solution.py:100
  65.5 1.1 %hidden.8.refs_0_ = bf16[128,512]{1,0:T(8,128)(2,1)S(1)} custom-call(s32[1]{0:T(128)} %bitcast.1.me_ref, bf16[2048,512]{1,0:T(8,128)(2,1)S(1)} %bitcast.9, bf16[2048,512]{1,0:T(8,128)(2,1)S(1)} %bitcast.14, bf16[128,2048]{1,0:T(8,128)(2,1)S(1)} %add.3.refs_0_, s32[12,128]{1,0:T(8,128)S(1)} %pad_add_fusion.refs_2_.refs_1_), custom_call_target="tpu_custom_call" | custom-call | flops 536870912 | bytes 4849664 | tf_op jit(solution)/shard_map/hidden/pallas_call | solution.py:43
  67.2 1.1 %hidden.9.refs_2_ = bf16[128,512]{1,0:T(8,128)(2,1)S(1)} custom-call(s32[1]{0:T(128)} %bitcast.1.me_ref, bf16[2048,512]{1,0:T(8,128)(2,1)S(1)} %bitcast.10, bf16[2048,512]{1,0:T(8,128)(2,1)S(1)} %bitcast.15, bf16[128,2048]{1,0:T(8,128)(2,1)S(1)} %collective-permute-done.16.refs_0_, s32[12,128]{1,0:T(8,128)S(1)} %collective-permute-done.8.refs_3_.refs_1_), custom_call_target="tpu_custom_call" | custom-call | flops 536870912 | bytes 4849664 | tf_op jit(solution)/shard_map/hidden/pallas_call | solution.py:43
  68.4 1.6 %collective-permute-start.17 = (bf16[128,512]{1,0:T(8,128)(2,1)S(1)}, bf16[128,512]{1,0:T(8,128)(2,1)S(1)}, u32[]{:S(2)}, u32[]{:S(2)}) collective-permute-start(bf16[128,512]{1,0:T(8,128)(2,1)S(1)} %hidden.9.refs_2_), channel_id=1, source_target_pairs={{0,8},{8,0},{1,9},{9,1},{2,10},{10,2},{3,11},{11,3},{4,12},{12,4},... | collective-permute-start | bytes 393224 | tf_op jit(solution)/shard_map/ppermute | solution.py:100
  69.9 3.2 %collective-permute-done.12.refs_5_ = bf16[256,512]{1,0:T(8,128)(2,1)S(1)} collective-permute-done((bf16[256,512]{1,0:T(8,128)(2,1)S(1)}, bf16[256,512]{1,0:T(8,128)(2,1)S(1)}, u32[]{:S(2)}, u32[]{:S(2)}) %collective-permute-start.12) | collective-permute-done | bytes 262176 | tf_op jit(solution)/shard_map/ppermute | solution.py:100
  73.2 5.6 %collective-permute-done.9.refs_3_ = bf16[256,512]{1,0:T(8,128)(2,1)S(1)} collective-permute-done((bf16[256,512]{1,0:T(8,128)(2,1)S(1)}, bf16[256,512]{1,0:T(8,128)(2,1)S(1)}, u32[]{:S(2)}, u32[]{:S(2)}) %collective-permute-start.9) | collective-permute-done | bytes 262176 | tf_op jit(solution)/shard_map/ppermute | solution.py:100
  79.8 1.8 %collective-permute-done.15.refs_1_ = bf16[128,512]{1,0:T(8,128)(2,1)S(1)} collective-permute-done((bf16[128,512]{1,0:T(8,128)(2,1)S(1)}, bf16[128,512]{1,0:T(8,128)(2,1)S(1)}, u32[]{:S(2)}, u32[]{:S(2)}) %collective-permute-start.15) | collective-permute-done | bytes 131104 | tf_op jit(solution)/shard_map/ppermute | solution.py:100
  81.6 2.2 %collective-permute-done.17.refs_3_ = bf16[128,512]{1,0:T(8,128)(2,1)S(1)} collective-permute-done((bf16[128,512]{1,0:T(8,128)(2,1)S(1)}, bf16[128,512]{1,0:T(8,128)(2,1)S(1)}, u32[]{:S(2)}, u32[]{:S(2)}) %collective-permute-start.17) | collective-permute-done | bytes 131104 | tf_op jit(solution)/shard_map/ppermute | solution.py:100
  83.8 13.0 %factor.1 = f32[256,512]{1,0:T(8,128)} custom-call(s32[1]{0:T(128)} %bitcast.rank_ref, f32[512,512]{1,0:T(8,128)S(1)} %partial_gram.1.early_ref, bf16[128,512]{1,0:T(8,128)(2,1)S(1)} %hidden.8.refs_0_, bf16[128,512]{1,0:T(8,128)(2,1)S(1)} %collective-permute-done.15.refs_1_, bf16[128,512]{1,0:T(8,128)(2,1)S(1)} %hidden.9.refs_2_, ...), custom_call_target="tpu_custom_call" | custom-call | tf_op jit(solution)/shard_map/factor/pallas_call | solution.py:288
  (31 shorter events, 7.6 us)
Async XLA Ops:
  0.0 18.1 %collective-permute-start.10 = (bf16[128,2048]{1,0:T(8,128)(2,1)}, bf16[128,2048]{1,0:T(8,128)(2,1)S(1)}, u32[]{:S(2)}, u32[]{:S(2)}) collective-permute-start(bf16[128,2048]{1,0:T(8,128)(2,1)} %refs_0_.1), channel_id=1, source_target_pairs={{0,2},{1,3},{2,4},{3,5},{4,6},{5,7},{6,0},{7,1},{8,10},{9,11},{10,... | collective-permute-start | bytes 1572872 | tf_op jit(solution)/shard_map/ppermute | solution.py:98
  3.1 24.8 %collective-permute-start.3 = (bf16[128,2048]{1,0:T(8,128)(2,1)}, bf16[128,2048]{1,0:T(8,128)(2,1)S(1)}, u32[]{:S(2)}, u32[]{:S(2)}) collective-permute-start(bf16[128,2048]{1,0:T(8,128)(2,1)} %refs_0_.1), channel_id=1, source_target_pairs={{0,6},{1,7},{2,0},{3,1},{4,2},{5,3},{6,4},{7,5},{8,14},{9,15},{10,... | collective-permute-start | bytes 1572872 | tf_op jit(solution)/shard_map/ppermute | solution.py:98
  18.1 26.2 %collective-permute-start.13 = (bf16[128,2048]{1,0:T(8,128)(2,1)S(1)}, bf16[128,2048]{1,0:T(8,128)(2,1)S(1)}, u32[]{:S(2)}, u32[]{:S(2)}) collective-permute-start(bf16[128,2048]{1,0:T(8,128)(2,1)S(1)} %collective-permute-done.10.refs_0_), channel_id=1, source_target_pairs={{2,4},{3,5},{4,6},{5,7},{10,12},{11,13},{12,14},{13,15},{18,20},{1... | collective-permute-start | bytes 1572872 | tf_op jit(solution)/shard_map/ppermute | solution.py:98
  27.9 16.4 %collective-permute-start.14 = (bf16[128,2048]{1,0:T(8,128)(2,1)S(1)}, bf16[128,2048]{1,0:T(8,128)(2,1)S(1)}, u32[]{:S(2)}, u32[]{:S(2)}) collective-permute-start(bf16[128,2048]{1,0:T(8,128)(2,1)S(1)} %collective-permute-done.3.refs_0_), channel_id=1, source_target_pairs={{4,2},{5,3},{2,0},{3,1},{12,10},{13,11},{10,8},{11,9},{20,18},{21,... | collective-permute-start | bytes 1572872 | tf_op jit(solution)/shard_map/ppermute | solution.py:98
  29.2 22.5 %collective-permute-start = (bf16[128,2048]{1,0:T(8,128)(2,1)}, bf16[128,2048]{1,0:T(8,128)(2,1)S(1)}, u32[]{:S(2)}, u32[]{:S(2)}) collective-permute-start(bf16[128,2048]{1,0:T(8,128)(2,1)} %refs_0_.1), channel_id=1, source_target_pairs={{0,1},{1,0},{2,3},{3,2},{4,5},{5,4},{6,7},{7,6},{8,9},{9,8},{10,11... | collective-permute-start | bytes 1572872 | tf_op jit(solution)/shard_map/ppermute | solution.py:99
  29.3 30.6 %collective-permute-start.11 = (bf16[128,2048]{1,0:T(8,128)(2,1)S(1)}, bf16[128,2048]{1,0:T(8,128)(2,1)S(1)}, u32[]{:S(2)}, u32[]{:S(2)}) collective-permute-start(bf16[128,2048]{1,0:T(8,128)(2,1)S(1)} %collective-permute-done.10.refs_0_), channel_id=1, source_target_pairs={{0,1},{1,0},{2,3},{3,2},{4,5},{5,4},{6,7},{7,6},{8,9},{9,8},{10,11... | collective-permute-start | bytes 1572872 | tf_op jit(solution)/shard_map/ppermute | solution.py:99
  29.7 14.5 %collective-permute-start.7 = (s32[4,128]{1,0:T(4,128)}, s32[4,128]{1,0:T(4,128)S(1)}, u32[]{:S(2)}, u32[]{:S(2)}) collective-permute-start(s32[4,128]{1,0:T(4,128)} %bitcast.16), channel_id=1, source_target_pairs={{0,4},{1,5},{2,6},{3,7},{4,0},{5,1},{6,2},{7,3},{8,12},{9,13},{10,... | collective-permute-start | bytes 6152 | tf_op jit(solution)/shard_map/ppermute | solution.py:98
  44.3 17.9 %collective-permute-start.4 = (bf16[128,2048]{1,0:T(8,128)(2,1)S(1)}, bf16[128,2048]{1,0:T(8,128)(2,1)S(1)}, u32[]{:S(2)}, u32[]{:S(2)}) collective-permute-start(bf16[128,2048]{1,0:T(8,128)(2,1)S(1)} %collective-permute-done.3.refs_0_), channel_id=1, source_target_pairs={{0,1},{1,0},{2,3},{3,2},{4,5},{5,4},{6,7},{7,6},{8,9},{9,8},{10,11... | collective-permute-start | bytes 1572872 | tf_op jit(solution)/shard_map/ppermute | solution.py:99
  44.3 5.8 %collective-permute-start.6 = (s32[4,128]{1,0:T(4,128)}, s32[4,128]{1,0:T(4,128)S(1)}, u32[]{:S(2)}, u32[]{:S(2)}) collective-permute-start(s32[4,128]{1,0:T(4,128)} %bitcast.17), channel_id=1, source_target_pairs={{0,2},{1,3},{2,4},{3,5},{4,6},{5,7},{6,0},{7,1},{8,10},{9,11},{10,... | collective-permute-start | bytes 6152 | tf_op jit(solution)/shard_map/ppermute | solution.py:98
  44.3 0.8 copy-start.4
  45.1 5.3 %collective-permute-start.5 = (s32[4,128]{1,0:T(4,128)}, s32[4,128]{1,0:T(4,128)S(1)}, u32[]{:S(2)}, u32[]{:S(2)}) collective-permute-start(s32[4,128]{1,0:T(4,128)} %bitcast.18), channel_id=1, source_target_pairs={{0,6},{1,7},{2,0},{3,1},{4,2},{5,3},{6,4},{7,5},{8,14},{9,15},{10,... | collective-permute-start | bytes 6152 | tf_op jit(solution)/shard_map/ppermute | solution.py:98
  50.1 1.4 %collective-permute-start.1 = (s32[4,128]{1,0:T(4,128)}, s32[4,128]{1,0:T(4,128)S(1)}, u32[]{:S(2)}, u32[]{:S(2)}) collective-permute-start(s32[4,128]{1,0:T(4,128)} %bitcast.19), channel_id=1, source_target_pairs={{0,1},{1,0},{2,3},{3,2},{4,5},{5,4},{6,7},{7,6},{8,9},{9,8},{10,11... | collective-permute-start | bytes 6152 | tf_op jit(solution)/shard_map/ppermute | solution.py:99
  50.4 16.8 %collective-permute-start.16 = (bf16[128,2048]{1,0:T(8,128)(2,1)S(1)}, bf16[128,2048]{1,0:T(8,128)(2,1)S(1)}, u32[]{:S(2)}, u32[]{:S(2)}) collective-permute-start(bf16[128,2048]{1,0:T(8,128)(2,1)S(1)} %add.3.refs_0_), channel_id=1, source_target_pairs={{0,1},{1,0},{2,3},{3,2},{4,5},{5,4},{6,7},{7,6},{8,9},{9,8},{10,11... | collective-permute-start | bytes 1572872 | tf_op jit(solution)/shard_map/ppermute | solution.py:99
  51.5 8.4 %collective-permute-start.8 = (s32[12,128]{1,0:T(8,128)S(1)}, s32[12,128]{1,0:T(8,128)S(1)}, u32[]{:S(2)}, u32[]{:S(2)}) collective-permute-start(s32[12,128]{1,0:T(8,128)S(1)} %pad_add_fusion.refs_2_.refs_1_), channel_id=1, source_target_pairs={{0,1},{1,0},{2,3},{3,2},{4,5},{5,4},{6,7},{7,6},{8,9},{9,8},{10,11... | collective-permute-start | bytes 18440 | tf_op jit(solution)/shard_map/ppermute | solution.py:99
  51.7 1.6 %copy-start = (bf16[1,2048,512]{2,1,0:T(8,128)(2,1)S(1)}, bf16[1,2048,512]{2,1,0:T(8,128)(2,1)}, u32[]{:S(2)}) copy-start(bf16[1,2048,512]{2,1,0:T(8,128)(2,1)} %param.6) | copy-start | bytes 6291460
  53.3 1.6 %copy-start.1 = (bf16[1,2048,512]{2,1,0:T(8,128)(2,1)S(1)}, bf16[1,2048,512]{2,1,0:T(8,128)(2,1)}, u32[]{:S(2)}) copy-start(bf16[1,2048,512]{2,1,0:T(8,128)(2,1)} %param.7) | copy-start | bytes 6291460
  54.9 1.0 %copy-start.2 = (bf16[128,2048]{1,0:T(8,128)(2,1)S(1)}, bf16[128,2048]{1,0:T(8,128)(2,1)}, u32[]{:S(2)}) copy-start(bf16[128,2048]{1,0:T(8,128)(2,1)} %refs_0_.1) | copy-start | bytes 1572868
  55.9 0.7 copy-start.3
  58.3 11.6 %collective-permute-start.2 = (bf16[256,512]{1,0:T(8,128)(2,1)S(1)}, bf16[256,512]{1,0:T(8,128)(2,1)S(1)}, u32[]{:S(2)}, u32[]{:S(2)}) collective-permute-start(bf16[256,512]{1,0:T(8,128)(2,1)S(1)} %hidden.5.refs_0_), channel_id=1, source_target_pairs={{0,8},{8,0},{1,9},{9,1},{2,10},{10,2},{3,11},{11,3},{4,12},{12,4},... | collective-permute-start | bytes 786440 | tf_op jit(solution)/shard_map/ppermute | solution.py:100
  61.6 11.6 %collective-permute-start.12 = (bf16[256,512]{1,0:T(8,128)(2,1)S(1)}, bf16[256,512]{1,0:T(8,128)(2,1)S(1)}, u32[]{:S(2)}, u32[]{:S(2)}) collective-permute-start(bf16[256,512]{1,0:T(8,128)(2,1)S(1)} %hidden.7.refs_4_), channel_id=1, source_target_pairs={{0,8},{8,0},{1,9},{9,1},{2,10},{10,2},{3,11},{11,3},{4,12},{12,4},... | collective-permute-start | bytes 786440 | tf_op jit(solution)/shard_map/ppermute | solution.py:100
  63.9 14.9 %collective-permute-start.9 = (bf16[256,512]{1,0:T(8,128)(2,1)S(1)}, bf16[256,512]{1,0:T(8,128)(2,1)S(1)}, u32[]{:S(2)}, u32[]{:S(2)}) collective-permute-start(bf16[256,512]{1,0:T(8,128)(2,1)S(1)} %hidden.6.refs_2_), channel_id=1, source_target_pairs={{0,8},{8,0},{1,9},{9,1},{2,10},{10,2},{3,11},{11,3},{4,12},{12,4},... | collective-permute-start | bytes 786440 | tf_op jit(solution)/shard_map/ppermute | solution.py:100
  66.6 15.0 %collective-permute-start.15 = (bf16[128,512]{1,0:T(8,128)(2,1)S(1)}, bf16[128,512]{1,0:T(8,128)(2,1)S(1)}, u32[]{:S(2)}, u32[]{:S(2)}) collective-permute-start(bf16[128,512]{1,0:T(8,128)(2,1)S(1)} %hidden.8.refs_0_), channel_id=1, source_target_pairs={{0,8},{8,0},{1,9},{9,1},{2,10},{10,2},{3,11},{11,3},{4,12},{12,4},... | collective-permute-start | bytes 393224 | tf_op jit(solution)/shard_map/ppermute | solution.py:100
  68.4 15.4 %collective-permute-start.17 = (bf16[128,512]{1,0:T(8,128)(2,1)S(1)}, bf16[128,512]{1,0:T(8,128)(2,1)S(1)}, u32[]{:S(2)}, u32[]{:S(2)}) collective-permute-start(bf16[128,512]{1,0:T(8,128)(2,1)S(1)} %hidden.9.refs_2_), channel_id=1, source_target_pairs={{0,8},{8,0},{1,9},{9,1},{2,10},{10,2},{3,11},{11,3},{4,12},{12,4},... | collective-permute-start | bytes 393224 | tf_op jit(solution)/shard_map/ppermute | solution.py:100
where the time goes:
time: 97.1 us; the launch traced here: 96.8 us
  waiting for transfers between devices  44.7 us (46%)
  starting transfers between devices  23.7 us (24%)
  Pallas kernels  21.5 us (22%)
  local copies, waits for them, and re-layouts  5.69 us (6%)
  other arithmetic  1.17 us (1%)
    ppermute x7, waiting for transfers between devices, gathered(): move = lambda x, pairs: lax.ppermute(x, 'expert', between_chips(pairs))  31 us
    ppermute x7, starting transfers between devices, gathered(): move = lambda x, pairs: lax.ppermute(x, 'expert', between_chips(pairs))  16.8 us
    pallas_call x1, Pallas kernels, factor_rows(): pl.pallas_call(functools.partial(factor_kernel, rows_mean=rows_mean), in_...  13 us
    ppermute x5, waiting for transfers between devices, gathered(): lax.ppermute(x, 'dp', [(r, (r + s) % data_ranks) for r in range(data_rank...  12.9 us
    pallas_call x5, Pallas kernels, hidden_of(): pl.pallas_call(functools.partial(hidden_kernel, at=at, top=top), in_specs...  7.41 us
    ppermute x5, starting transfers between devices, gathered(): lax.ppermute(x, 'dp', [(r, (r + s) % data_ranks) for r in range(data_rank...  5.87 us
    unnamed x10, local copies, waits for them, and re-layouts  5.69 us
  transfers between devices with their start and end apart: 18, of which 9 were waited for; matrix products, arithmetic and copies ran while one was open for 1% of the time, Pallas kernels for 9%

commit v1 on v0

--- a/solution.py
+++ b/solution.py
@@ -102,9 +102,14 @@
 
     names = routes.T
     above = move(tokens, ring(-1))
-    below = move(tokens, ring(1))
+    half = tokens.shape[0] // 2
+    below, on_up = [], []
+    for i in range(2):
+        below.append(move(tokens[i * half : (i + 1) * half], ring(1)))
     on_down = move(above, [(2, 1), (1, 0)])
-    on_up = move(below, [(1, 2), (2, 3)])
+    for i in range(2):
+        on_up.append(move(below[i], [(1, 2), (2, 3)]))
+    below = jnp.concatenate(below, axis=0)
     moved = []
     for pairs in [ring(-1), ring(1), ring(2)]:
         moved.append(move(names, pairs))
@@ -120,7 +125,7 @@
         hiddens.append([hidden] + [turn(hidden, s) for s in range(1, data_ranks)])
     early = partial_gram(sum(hiddens, []))
 
-    last = on_up + on_down
+    last = jnp.concatenate(on_up, axis=0) + on_down
     other = swap(last)
     late = []
     for piece, who in ((last, moved), (other, other_moved)):

time: 97.1 us -> 86 us (0.89)
  waiting for transfers between devices: 44.7 us -> 36.2 us
  starting transfers between devices: 23.7 us -> 20.4 us
  Pallas kernels: 21.5 us -> 23.3 us
  local copies, waits for them, and re-layouts: 5.69 us -> 4.45 us
    ppermute x7 -> x9, waiting for transfers between devices: 31 us -> 25.4 us  [gathered(): move = lambda x, pairs: lax.ppermute(x, 'expert', between_chips(pairs))]
    unnamed x10 -> x9, local copies, waits for them, and re-layouts: 5.69 us -> 1.62 us
    ppermute x7 -> x9, starting transfers between devices: 16.8 us -> 12.9 us  [gathered(): move = lambda x, pairs: lax.ppermute(x, 'expert', between_chips(pairs))]
    ppermute x5, waiting for transfers between devices: 12.9 us -> 10.8 us  [gathered(): lax.ppermute(x, 'dp', [(r, (r + s) % data_ranks) for r in range(data_rank...]
    slice x0 -> x1, local copies, waits for them, and re-layouts: none -> 1.86 us  [gathered(): below.append(move(tokens[i * half:(i + 1) * half], ring(1)))]
    pallas_call x1, Pallas kernels: 1 us -> 2.1 us  [partial_gram(): pl.pallas_call(gram_kernel, in_specs=[pl.BlockSpec(memory_space=pltpu.VME...]
  transfers between devices with their start and end apart: 18 -> 20, of which waited for: 9 -> 9; matrix products, arithmetic and copies ran while one was open for 1% -> 5% of each run, Pallas kernels for 9% -> 12%
where the time goes in v1:
time: 86 us; the launch traced here: 85.7 us
  waiting for transfers between devices  36.2 us (42%)
  Pallas kernels  23.3 us (27%)
  starting transfers between devices  20.4 us (24%)
  local copies, waits for them, and re-layouts  4.45 us (5%)
  other arithmetic  1.18 us (1%)
    ppermute x9, waiting for transfers between devices, gathered(): move = lambda x, pairs: lax.ppermute(x, 'expert', between_chips(pairs))  25.4 us
    pallas_call x1, Pallas kernels, factor_rows(): pl.pallas_call(functools.partial(factor_kernel, rows_mean=rows_mean), in_...  13 us
    ppermute x9, starting transfers between devices, gathered(): move = lambda x, pairs: lax.ppermute(x, 'expert', between_chips(pairs))  12.9 us
    ppermute x5, waiting for transfers between devices, gathered(): lax.ppermute(x, 'dp', [(r, (r + s) % data_ranks) for r in range(data_rank...  10.8 us
    pallas_call x5, Pallas kernels, hidden_of(): pl.pallas_call(functools.partial(hidden_kernel, at=at, top=top), in_specs...  8.12 us
    ppermute x5, starting transfers between devices, gathered(): lax.ppermute(x, 'dp', [(r, (r + s) % data_ranks) for r in range(data_rank...  5.8 us
    pallas_call x1, Pallas kernels, partial_gram(): pl.pallas_call(gram_kernel, in_specs=[pl.BlockSpec(memory_space=pltpu.VME...  2.1 us
    slice x1, local copies, waits for them, and re-layouts, gathered(): below.append(move(tokens[i * half:(i + 1) * half], ring(1)))  1.86 us
  transfers between devices with their start and end apart: 20, of which 9 were waited for; matrix products, arithmetic and copies ran while one was open for 5% of the time, Pallas kernels for 12%

profile of v1, /device:TPU:0, one launch (start us, length us, event | category | flops | bytes accessed | tf_op | source)
XLA Modules:
  0.0 85.7 jit_solution(10570315962374819185)
XLA Ops:
  0.0 5.1 %collective-permute-start.3 = (bf16[128,2048]{1,0:T(8,128)(2,1)}, bf16[128,2048]{1,0:T(8,128)(2,1)S(1)}, u32[]{:S(2)}, u32[]{:S(2)}) collective-permute-start(bf16[128,2048]{1,0:T(8,128)(2,1)} %refs_0_.1), channel_id=1, source_target_pairs={{0,6},{1,7},{2,0},{3,1},{4,2},{5,3},{6,4},{7,5},{8,14},{9,15},{10,... | collective-permute-start | bytes 1572872 | tf_op jit(solution)/shard_map/ppermute | solution.py:98
  5.1 1.9 %fusion = (bf16[64,2048]{1,0:T(8,128)(2,1)}, bf16[64,2048]{1,0:T(8,128)(2,1)}) fusion(bf16[128,2048]{1,0:T(8,128)(2,1)} %refs_0_.1), kind=kLoop, calls=%fused_computation.4 | loop fusion | bytes 1048576 | tf_op jit(solution)/shard_map/slice | solution.py:108
  7.3 10.5 %collective-permute-done.3.refs_0_ = bf16[128,2048]{1,0:T(8,128)(2,1)S(1)} collective-permute-done((bf16[128,2048]{1,0:T(8,128)(2,1)}, bf16[128,2048]{1,0:T(8,128)(2,1)S(1)}, u32[]{:S(2)}, u32[]{:S(2)}) %collective-permute-start.3) | collective-permute-done | bytes 524320 | tf_op jit(solution)/shard_map/ppermute | solution.py:98
  17.8 1.3 %collective-permute-start.16 = (bf16[128,2048]{1,0:T(8,128)(2,1)S(1)}, bf16[128,2048]{1,0:T(8,128)(2,1)}, u32[]{:S(2)}, u32[]{:S(2)}) collective-permute-start(bf16[128,2048]{1,0:T(8,128)(2,1)S(1)} %collective-permute-done.3.refs_0_), channel_id=1, source_target_pairs={{4,2},{5,3},{2,0},{3,1},{12,10},{13,11},{10,8},{11,9},{20,18},{21,... | collective-permute-start | bytes 1572872 | tf_op jit(solution)/shard_map/ppermute | solution.py:98
  19.1 2.2 %collective-permute-start.7 = (s32[4,128]{1,0:T(4,128)}, s32[4,128]{1,0:T(4,128)S(1)}, u32[]{:S(2)}, u32[]{:S(2)}) collective-permute-start(s32[4,128]{1,0:T(4,128)} %bitcast.16), channel_id=1, source_target_pairs={{0,4},{1,5},{2,6},{3,7},{4,0},{5,1},{6,2},{7,3},{8,12},{9,13},{10,... | collective-permute-start | bytes 6152 | tf_op jit(solution)/shard_map/ppermute | solution.py:98
  21.3 2.7 %collective-permute-start.6 = (s32[4,128]{1,0:T(4,128)}, s32[4,128]{1,0:T(4,128)S(1)}, u32[]{:S(2)}, u32[]{:S(2)}) collective-permute-start(s32[4,128]{1,0:T(4,128)} %bitcast.17), channel_id=1, source_target_pairs={{0,2},{1,3},{2,4},{3,5},{4,6},{5,7},{6,0},{7,1},{8,10},{9,11},{10,... | collective-permute-start | bytes 6152 | tf_op jit(solution)/shard_map/ppermute | solution.py:98
  25.1 3.7 %collective-permute-done.10 = bf16[64,2048]{1,0:T(8,128)(2,1)S(1)} collective-permute-done((bf16[64,2048]{1,0:T(8,128)(2,1)}, bf16[64,2048]{1,0:T(8,128)(2,1)S(1)}, u32[]{:S(2)}, u32[]{:S(2)}) %collective-permute-start.10) | collective-permute-done | bytes 262176 | tf_op jit(solution)/shard_map/ppermute | solution.py:98
  30.5 9.6 %collective-permute-done.7 = s32[4,128]{1,0:T(4,128)S(1)} collective-permute-done((s32[4,128]{1,0:T(4,128)}, s32[4,128]{1,0:T(4,128)S(1)}, u32[]{:S(2)}, u32[]{:S(2)}) %collective-permute-start.7) | collective-permute-done | bytes 2080 | tf_op jit(solution)/shard_map/ppermute | solution.py:98
  40.7 1.2 %maximum_add_fusion.refs_0_ = bf16[128,2048]{1,0:T(8,128)(2,1)S(1)} fusion(bf16[128,2048]{1,0:T(8,128)(2,1)} %collective-permute-done.16, bf16[64,2048]{1,0:T(8,128)(2,1)S(1)} %collective-permute-done.15, bf16[64,2048]{1,0:T(8,128)(2,1)S(1)} %collective-permute-done.14), kind=kLoop, calls=%fused_computation | loop fusion | flops 1572864 | bytes 1572864 | tf_op jit(solution)/shard_map/add | solution.py:128
  42.4 1.2 %collective-permute-done.5 = s32[4,128]{1,0:T(4,128)S(1)} collective-permute-done((s32[4,128]{1,0:T(4,128)S(1)}, s32[4,128]{1,0:T(4,128)S(1)}, u32[]{:S(2)}, u32[]{:S(2)}) %collective-permute-start.5) | collective-permute-done | bytes 2080 | tf_op jit(solution)/shard_map/ppermute | solution.py:98
  44.2 1.6 %copy-done.1 = bf16[1,2048,512]{2,1,0:T(8,128)(2,1)S(1)} copy-done((bf16[1,2048,512]{2,1,0:T(8,128)(2,1)S(1)}, bf16[1,2048,512]{2,1,0:T(8,128)(2,1)}, u32[]{:S(2)}) %copy-start.1) | copy-done | bytes 2097176
  45.8 1.7 %hidden.5.refs_0_ = bf16[256,512]{1,0:T(8,128)(2,1)S(1)} custom-call(s32[1]{0:T(128)} %bitcast.1.me_ref, bf16[2048,512]{1,0:T(8,128)(2,1)S(1)} %bitcast.6, bf16[2048,512]{1,0:T(8,128)(2,1)S(1)} %bitcast.11, bf16[128,2048]{1,0:T(8,128)(2,1)S(1)} %copy-done.2, bf16[128,2048]{1,0:T(8,128)(2,1)S(1)} %collective-permute-done.refs_1_, s32[4,128]{1,0:T(4,128)S(1)} %bitcast.20, ...), custom_call_target="tpu_custom_call" | custom-call | flops 1073741824 | bytes 5505024 | tf_op jit(solution)/shard_map/hidden/pallas_call | solution.py:43
  47.5 1.6 %collective-permute-start.2 = (bf16[256,512]{1,0:T(8,128)(2,1)S(1)}, bf16[256,512]{1,0:T(8,128)(2,1)}, u32[]{:S(2)}, u32[]{:S(2)}) collective-permute-start(bf16[256,512]{1,0:T(8,128)(2,1)S(1)} %hidden.5.refs_0_), channel_id=1, source_target_pairs={{0,8},{8,0},{1,9},{9,1},{2,10},{10,2},{3,11},{11,3},{4,12},{12,4},... | collective-permute-start | bytes 786440 | tf_op jit(solution)/shard_map/ppermute | solution.py:100
  49.1 1.7 %hidden.7.refs_4_ = bf16[256,512]{1,0:T(8,128)(2,1)S(1)} custom-call(s32[1]{0:T(128)} %bitcast.1.me_ref, bf16[2048,512]{1,0:T(8,128)(2,1)S(1)} %bitcast.7, bf16[2048,512]{1,0:T(8,128)(2,1)S(1)} %bitcast.12, bf16[128,2048]{1,0:T(8,128)(2,1)S(1)} %constant_dynamic-update-slice_fusion.refs_0_, bf16[128,2048]{1,0:T(8,128)(2,1)S(1)} %collective-permute-done.12.refs_1_, ...), custom_call_target="tpu_custom_call" | custom-call | flops 1073741824 | bytes 5505024 | tf_op jit(solution)/shard_map/hidden/pallas_call | solution.py:43
  51.4 2.4 %hidden.6.refs_2_ = bf16[256,512]{1,0:T(8,128)(2,1)} custom-call(s32[1]{0:T(128)} %bitcast.1.me_ref, bf16[2048,512]{1,0:T(8,128)(2,1)S(1)} %bitcast.8, bf16[2048,512]{1,0:T(8,128)(2,1)S(1)} %bitcast.13, bf16[128,2048]{1,0:T(8,128)(2,1)S(1)} %collective-permute-done.3.refs_0_, bf16[128,2048]{1,0:T(8,128)(2,1)S(1)} %collective-permute-done.4.refs_1_, ...), custom_call_target="tpu_custom_call" | custom-call | flops 1073741824 | bytes 5505024 | tf_op jit(solution)/shard_map/hidden/pallas_call | solution.py:43
  53.9 1.5 %collective-permute-start.9 = (bf16[256,512]{1,0:T(8,128)(2,1)}, bf16[256,512]{1,0:T(8,128)(2,1)S(1)}, u32[]{:S(2)}, u32[]{:S(2)}) collective-permute-start(bf16[256,512]{1,0:T(8,128)(2,1)} %hidden.6.refs_2_), channel_id=1, source_target_pairs={{0,8},{8,0},{1,9},{9,1},{2,10},{10,2},{3,11},{11,3},{4,12},{12,4},... | collective-permute-start | bytes 786440 | tf_op jit(solution)/shard_map/ppermute | solution.py:100
  55.4 1.1 %hidden.8.refs_0_ = bf16[128,512]{1,0:T(8,128)(2,1)S(1)} custom-call(s32[1]{0:T(128)} %bitcast.1.me_ref, bf16[2048,512]{1,0:T(8,128)(2,1)S(1)} %bitcast.9, bf16[2048,512]{1,0:T(8,128)(2,1)S(1)} %bitcast.14, bf16[128,2048]{1,0:T(8,128)(2,1)S(1)} %maximum_add_fusion.refs_0_, s32[12,128]{1,0:T(8,128)S(1)} %pad_add_fusion.refs_2_.refs_1_), custom_call_target="tpu_custom_call" | custom-call | flops 536870912 | bytes 4849664 | tf_op jit(solution)/shard_map/hidden/pallas_call | solution.py:43
  57.1 1.1 %hidden.9.refs_2_ = bf16[128,512]{1,0:T(8,128)(2,1)S(1)} custom-call(s32[1]{0:T(128)} %bitcast.1.me_ref, bf16[2048,512]{1,0:T(8,128)(2,1)S(1)} %bitcast.10, bf16[2048,512]{1,0:T(8,128)(2,1)S(1)} %bitcast.15, bf16[128,2048]{1,0:T(8,128)(2,1)S(1)} %collective-permute-done.18.refs_0_, s32[12,128]{1,0:T(8,128)S(1)} %collective-permute-done.8.refs_3_.refs_1_), custom_call_target="tpu_custom_call" | custom-call | flops 536870912 | bytes 4849664 | tf_op jit(solution)/shard_map/hidden/pallas_call | solution.py:43
  58.2 1.6 %collective-permute-start.19 = (bf16[128,512]{1,0:T(8,128)(2,1)S(1)}, bf16[128,512]{1,0:T(8,128)(2,1)S(1)}, u32[]{:S(2)}, u32[]{:S(2)}) collective-permute-start(bf16[128,512]{1,0:T(8,128)(2,1)S(1)} %hidden.9.refs_2_), channel_id=1, source_target_pairs={{0,8},{8,0},{1,9},{9,1},{2,10},{10,2},{3,11},{11,3},{4,12},{12,4},... | collective-permute-start | bytes 393224 | tf_op jit(solution)/shard_map/ppermute | solution.py:100
  59.8 2.7 %collective-permute-done.13.refs_5_ = bf16[256,512]{1,0:T(8,128)(2,1)} collective-permute-done((bf16[256,512]{1,0:T(8,128)(2,1)S(1)}, bf16[256,512]{1,0:T(8,128)(2,1)}, u32[]{:S(2)}, u32[]{:S(2)}) %collective-permute-start.13) | collective-permute-done | bytes 262176 | tf_op jit(solution)/shard_map/ppermute | solution.py:100
  62.5 5.5 %collective-permute-done.9.refs_3_ = bf16[256,512]{1,0:T(8,128)(2,1)S(1)} collective-permute-done((bf16[256,512]{1,0:T(8,128)(2,1)}, bf16[256,512]{1,0:T(8,128)(2,1)S(1)}, u32[]{:S(2)}, u32[]{:S(2)}) %collective-permute-start.9) | collective-permute-done | bytes 262176 | tf_op jit(solution)/shard_map/ppermute | solution.py:100
  68.0 2.1 %partial_gram.1.early_ref = f32[512,512]{1,0:T(8,128)S(1)} custom-call(bf16[256,512]{1,0:T(8,128)(2,1)S(1)} %hidden.5.refs_0_, bf16[256,512]{1,0:T(8,128)(2,1)} %collective-permute-done.2.refs_1_, bf16[256,512]{1,0:T(8,128)(2,1)} %hidden.6.refs_2_, bf16[256,512]{1,0:T(8,128)(2,1)S(1)} %collective-permute-done.9.refs_3_, bf16[256,512]{1,0:T(8,128)(2,1)S(1)} %hidden.7.refs_4_, ...), custom_call_target="tpu_custom_call" | custom-call | flops 805306368 | bytes 2621440 | tf_op jit(solution)/shard_map/partial_gram/pallas_call | solution.py:75
  70.8 1.9 %collective-permute-done.19.refs_3_ = bf16[128,512]{1,0:T(8,128)(2,1)S(1)} collective-permute-done((bf16[128,512]{1,0:T(8,128)(2,1)S(1)}, bf16[128,512]{1,0:T(8,128)(2,1)S(1)}, u32[]{:S(2)}, u32[]{:S(2)}) %collective-permute-start.19) | collective-permute-done | bytes 131104 | tf_op jit(solution)/shard_map/ppermute | solution.py:100
  72.7 13.0 %factor.1 = f32[256,512]{1,0:T(8,128)} custom-call(s32[1]{0:T(128)} %bitcast.rank_ref, f32[512,512]{1,0:T(8,128)S(1)} %partial_gram.1.early_ref, bf16[128,512]{1,0:T(8,128)(2,1)S(1)} %hidden.8.refs_0_, bf16[128,512]{1,0:T(8,128)(2,1)S(1)} %collective-permute-done.17.refs_1_, bf16[128,512]{1,0:T(8,128)(2,1)S(1)} %hidden.9.refs_2_, ...), custom_call_target="tpu_custom_call" | custom-call | tf_op jit(solution)/shard_map/factor/pallas_call | solution.py:293
  (36 shorter events, 6.6 us)
Async XLA Ops:
  0.0 40.1 %copy-start.2 = (bf16[128,2048]{1,0:T(8,128)(2,1)S(1)}, bf16[128,2048]{1,0:T(8,128)(2,1)}, u32[]{:S(2)}) copy-start(bf16[128,2048]{1,0:T(8,128)(2,1)} %refs_0_.1) | copy-start | bytes 1572868
  0.0 40.0 %copy-start.3 = (s32[128,4]{0,1:T(4,128)S(1)}, s32[128,4]{0,1:T(4,128)}, u32[]{:S(2)}) copy-start(s32[128,4]{0,1:T(4,128)} %param.5) | copy-start | bytes 6148
  0.0 44.2 %copy-start = (bf16[1,2048,512]{2,1,0:T(8,128)(2,1)S(1)}, bf16[1,2048,512]{2,1,0:T(8,128)(2,1)}, u32[]{:S(2)}) copy-start(bf16[1,2048,512]{2,1,0:T(8,128)(2,1)} %param.6) | copy-start | bytes 6291460
  0.0 17.8 %collective-permute-start.3 = (bf16[128,2048]{1,0:T(8,128)(2,1)}, bf16[128,2048]{1,0:T(8,128)(2,1)S(1)}, u32[]{:S(2)}, u32[]{:S(2)}) collective-permute-start(bf16[128,2048]{1,0:T(8,128)(2,1)} %refs_0_.1), channel_id=1, source_target_pairs={{0,6},{1,7},{2,0},{3,1},{4,2},{5,3},{6,4},{7,5},{8,14},{9,15},{10,... | collective-permute-start | bytes 1572872 | tf_op jit(solution)/shard_map/ppermute | solution.py:98
  7.0 17.4 %collective-permute-start.11 = (bf16[64,2048]{1,0:T(8,128)(2,1)}, bf16[64,2048]{1,0:T(8,128)(2,1)}, u32[]{:S(2)}, u32[]{:S(2)}) collective-permute-start(bf16[64,2048]{1,0:T(8,128)(2,1)} %get-tuple-element.5), channel_id=1, source_target_pairs={{0,2},{1,3},{2,4},{3,5},{4,6},{5,7},{6,0},{7,1},{8,10},{9,11},{10,... | collective-permute-start | bytes 786440 | tf_op jit(solution)/shard_map/ppermute | solution.py:98
  7.0 21.8 %collective-permute-start.10 = (bf16[64,2048]{1,0:T(8,128)(2,1)}, bf16[64,2048]{1,0:T(8,128)(2,1)S(1)}, u32[]{:S(2)}, u32[]{:S(2)}) collective-permute-start(bf16[64,2048]{1,0:T(8,128)(2,1)} %get-tuple-element.6), channel_id=1, source_target_pairs={{0,2},{1,3},{2,4},{3,5},{4,6},{5,7},{6,0},{7,1},{8,10},{9,11},{10,... | collective-permute-start | bytes 786440 | tf_op jit(solution)/shard_map/ppermute | solution.py:98
  17.8 22.8 %collective-permute-start.16 = (bf16[128,2048]{1,0:T(8,128)(2,1)S(1)}, bf16[128,2048]{1,0:T(8,128)(2,1)}, u32[]{:S(2)}, u32[]{:S(2)}) collective-permute-start(bf16[128,2048]{1,0:T(8,128)(2,1)S(1)} %collective-permute-done.3.refs_0_), channel_id=1, source_target_pairs={{4,2},{5,3},{2,0},{3,1},{12,10},{13,11},{10,8},{11,9},{20,18},{21,... | collective-permute-start | bytes 1572872 | tf_op jit(solution)/shard_map/ppermute | solution.py:98
  19.1 20.9 %collective-permute-start.7 = (s32[4,128]{1,0:T(4,128)}, s32[4,128]{1,0:T(4,128)S(1)}, u32[]{:S(2)}, u32[]{:S(2)}) collective-permute-start(s32[4,128]{1,0:T(4,128)} %bitcast.16), channel_id=1, source_target_pairs={{0,4},{1,5},{2,6},{3,7},{4,0},{5,1},{6,2},{7,3},{8,12},{9,13},{10,... | collective-permute-start | bytes 6152 | tf_op jit(solution)/shard_map/ppermute | solution.py:98
  21.3 20.6 %collective-permute-start.6 = (s32[4,128]{1,0:T(4,128)}, s32[4,128]{1,0:T(4,128)S(1)}, u32[]{:S(2)}, u32[]{:S(2)}) collective-permute-start(s32[4,128]{1,0:T(4,128)} %bitcast.17), channel_id=1, source_target_pairs={{0,2},{1,3},{2,4},{3,5},{4,6},{5,7},{6,0},{7,1},{8,10},{9,11},{10,... | collective-permute-start | bytes 6152 | tf_op jit(solution)/shard_map/ppermute | solution.py:98
  24.4 15.6 %collective-permute-start.15 = (bf16[64,2048]{1,0:T(8,128)(2,1)}, bf16[64,2048]{1,0:T(8,128)(2,1)S(1)}, u32[]{:S(2)}, u32[]{:S(2)}) collective-permute-start(bf16[64,2048]{1,0:T(8,128)(2,1)} %collective-permute-done.11), channel_id=1, source_target_pairs={{2,4},{3,5},{4,6},{5,7},{10,12},{11,13},{12,14},{13,15},{18,20},{1... | collective-permute-start | bytes 786440 | tf_op jit(solution)/shard_map/ppermute | solution.py:98
  28.8 11.3 %collective-permute-start.14 = (bf16[64,2048]{1,0:T(8,128)(2,1)S(1)}, bf16[64,2048]{1,0:T(8,128)(2,1)S(1)}, u32[]{:S(2)}, u32[]{:S(2)}) collective-permute-start(bf16[64,2048]{1,0:T(8,128)(2,1)S(1)} %collective-permute-done.10), channel_id=1, source_target_pairs={{2,4},{3,5},{4,6},{5,7},{10,12},{11,13},{12,14},{13,15},{18,20},{1... | collective-permute-start | bytes 786440 | tf_op jit(solution)/shard_map/ppermute | solution.py:98
  40.0 3.6 %collective-permute-start.5 = (s32[4,128]{1,0:T(4,128)S(1)}, s32[4,128]{1,0:T(4,128)S(1)}, u32[]{:S(2)}, u32[]{:S(2)}) collective-permute-start(s32[4,128]{1,0:T(4,128)S(1)} %bitcast.18), channel_id=1, source_target_pairs={{0,6},{1,7},{2,0},{3,1},{4,2},{5,3},{6,4},{7,5},{8,14},{9,15},{10,... | collective-permute-start | bytes 6152 | tf_op jit(solution)/shard_map/ppermute | solution.py:98
  40.1 4.2 %collective-permute-start = (bf16[128,2048]{1,0:T(8,128)(2,1)S(1)}, bf16[128,2048]{1,0:T(8,128)(2,1)S(1)}, u32[]{:S(2)}, u32[]{:S(2)}) collective-permute-start(bf16[128,2048]{1,0:T(8,128)(2,1)S(1)} %copy-done.2), channel_id=1, source_target_pairs={{0,1},{1,0},{2,3},{3,2},{4,5},{5,4},{6,7},{7,6},{8,9},{9,8},{10,11... | collective-permute-start | bytes 1572872 | tf_op jit(solution)/shard_map/ppermute | solution.py:99
  40.2 9.0 %collective-permute-start.12 = (bf16[128,2048]{1,0:T(8,128)(2,1)S(1)}, bf16[128,2048]{1,0:T(8,128)(2,1)S(1)}, u32[]{:S(2)}, u32[]{:S(2)}) collective-permute-start(bf16[128,2048]{1,0:T(8,128)(2,1)S(1)} %constant_dynamic-update-slice_fusion.refs_0_), channel_id=1, source_target_pairs={{0,1},{1,0},{2,3},{3,2},{4,5},{5,4},{6,7},{7,6},{8,9},{9,8},{10,11... | collective-permute-start | bytes 1572872 | tf_op jit(solution)/shard_map/ppermute | solution.py:99
  40.6 10.8 %collective-permute-start.4 = (bf16[128,2048]{1,0:T(8,128)(2,1)S(1)}, bf16[128,2048]{1,0:T(8,128)(2,1)S(1)}, u32[]{:S(2)}, u32[]{:S(2)}) collective-permute-start(bf16[128,2048]{1,0:T(8,128)(2,1)S(1)} %collective-permute-done.3.refs_0_), channel_id=1, source_target_pairs={{0,1},{1,0},{2,3},{3,2},{4,5},{5,4},{6,7},{7,6},{8,9},{9,8},{10,11... | collective-permute-start | bytes 1572872 | tf_op jit(solution)/shard_map/ppermute | solution.py:99
  41.9 1.7 %collective-permute-start.1 = (s32[4,128]{1,0:T(4,128)S(1)}, s32[4,128]{1,0:T(4,128)S(1)}, u32[]{:S(2)}, u32[]{:S(2)}) collective-permute-start(s32[4,128]{1,0:T(4,128)S(1)} %bitcast.19), channel_id=1, source_target_pairs={{0,1},{1,0},{2,3},{3,2},{4,5},{5,4},{6,7},{7,6},{8,9},{9,8},{10,11... | collective-permute-start | bytes 6152 | tf_op jit(solution)/shard_map/ppermute | solution.py:99
  43.6 13.5 %collective-permute-start.18 = (bf16[128,2048]{1,0:T(8,128)(2,1)S(1)}, bf16[128,2048]{1,0:T(8,128)(2,1)S(1)}, u32[]{:S(2)}, u32[]{:S(2)}) collective-permute-start(bf16[128,2048]{1,0:T(8,128)(2,1)S(1)} %maximum_add_fusion.refs_0_), channel_id=1, source_target_pairs={{0,1},{1,0},{2,3},{3,2},{4,5},{5,4},{6,7},{7,6},{8,9},{9,8},{10,11... | collective-permute-start | bytes 1572872 | tf_op jit(solution)/shard_map/ppermute | solution.py:99
  43.7 5.4 %collective-permute-start.8 = (s32[12,128]{1,0:T(8,128)S(1)}, s32[12,128]{1,0:T(8,128)S(1)}, u32[]{:S(2)}, u32[]{:S(2)}) collective-permute-start(s32[12,128]{1,0:T(8,128)S(1)} %pad_add_fusion.refs_2_.refs_1_), channel_id=1, source_target_pairs={{0,1},{1,0},{2,3},{3,2},{4,5},{5,4},{6,7},{7,6},{8,9},{9,8},{10,11... | collective-permute-start | bytes 18440 | tf_op jit(solution)/shard_map/ppermute | solution.py:99
  44.2 1.6 %copy-start.1 = (bf16[1,2048,512]{2,1,0:T(8,128)(2,1)S(1)}, bf16[1,2048,512]{2,1,0:T(8,128)(2,1)}, u32[]{:S(2)}) copy-start(bf16[1,2048,512]{2,1,0:T(8,128)(2,1)} %param.7) | copy-start | bytes 6291460
  47.5 12.3 %collective-permute-start.2 = (bf16[256,512]{1,0:T(8,128)(2,1)S(1)}, bf16[256,512]{1,0:T(8,128)(2,1)}, u32[]{:S(2)}, u32[]{:S(2)}) collective-permute-start(bf16[256,512]{1,0:T(8,128)(2,1)S(1)} %hidden.5.refs_0_), channel_id=1, source_target_pairs={{0,8},{8,0},{1,9},{9,1},{2,10},{10,2},{3,11},{11,3},{4,12},{12,4},... | collective-permute-start | bytes 786440 | tf_op jit(solution)/shard_map/ppermute | solution.py:100
  50.8 11.7 %collective-permute-start.13 = (bf16[256,512]{1,0:T(8,128)(2,1)S(1)}, bf16[256,512]{1,0:T(8,128)(2,1)}, u32[]{:S(2)}, u32[]{:S(2)}) collective-permute-start(bf16[256,512]{1,0:T(8,128)(2,1)S(1)} %hidden.7.refs_4_), channel_id=1, source_target_pairs={{0,8},{8,0},{1,9},{9,1},{2,10},{10,2},{3,11},{11,3},{4,12},{12,4},... | collective-permute-start | bytes 786440 | tf_op jit(solution)/shard_map/ppermute | solution.py:100
  53.9 14.2 %collective-permute-start.9 = (bf16[256,512]{1,0:T(8,128)(2,1)}, bf16[256,512]{1,0:T(8,128)(2,1)S(1)}, u32[]{:S(2)}, u32[]{:S(2)}) collective-permute-start(bf16[256,512]{1,0:T(8,128)(2,1)} %hidden.6.refs_2_), channel_id=1, source_target_pairs={{0,8},{8,0},{1,9},{9,1},{2,10},{10,2},{3,11},{11,3},{4,12},{12,4},... | collective-permute-start | bytes 786440 | tf_op jit(solution)/shard_map/ppermute | solution.py:100
  56.5 14.3 %collective-permute-start.17 = (bf16[128,512]{1,0:T(8,128)(2,1)S(1)}, bf16[128,512]{1,0:T(8,128)(2,1)S(1)}, u32[]{:S(2)}, u32[]{:S(2)}) collective-permute-start(bf16[128,512]{1,0:T(8,128)(2,1)S(1)} %hidden.8.refs_0_), channel_id=1, source_target_pairs={{0,8},{8,0},{1,9},{9,1},{2,10},{10,2},{3,11},{11,3},{4,12},{12,4},... | collective-permute-start | bytes 393224 | tf_op jit(solution)/shard_map/ppermute | solution.py:100
  58.2 14.5 %collective-permute-start.19 = (bf16[128,512]{1,0:T(8,128)(2,1)S(1)}, bf16[128,512]{1,0:T(8,128)(2,1)S(1)}, u32[]{:S(2)}, u32[]{:S(2)}) collective-permute-start(bf16[128,512]{1,0:T(8,128)(2,1)S(1)} %hidden.9.refs_2_), channel_id=1, source_target_pairs={{0,8},{8,0},{1,9},{9,1},{2,10},{10,2},{3,11},{11,3},{4,12},{12,4},... | collective-permute-start | bytes 393224 | tf_op jit(solution)/shard_map/ppermute | solution.py:100

commit v2 on v1

--- a/solution.py
+++ b/solution.py
@@ -57,12 +57,8 @@
 
 
 def gram_of(refs):
-    total = None
-    for ref in refs:
-        h = ref[...]
-        part = lax.dot_general(h, h, (((0,), (0,)), ((), ())), preferred_element_type=jnp.float32)
-        total = part if total is None else total + part
-    return total
+    h = jnp.concatenate([ref[...] for ref in refs], axis=0)
+    return lax.dot_general(h, h, (((0,), (0,)), ((), ())), preferred_element_type=jnp.float32)
 
 
 def gram_kernel(*refs):
@@ -180,10 +176,6 @@
 
 def row_of(x, k):
     return jnp.broadcast_to(x[k : k + 1, :], x.shape)
-
-
-def lane_of(x, at):
-    return jnp.take_along_axis(x, jnp.full(x.shape, at, jnp.int32), axis=1, mode="promise_in_bounds")
 
 
 PRODUCTS = ((0, 0), (0, 1), (1, 0), (0, 2), (2, 0), (1, 1))
@@ -260,26 +252,17 @@
             out_ref[base:end, :base] = jnp.zeros((block, base), jnp.float32)
         sublane = lax.broadcasted_iota(jnp.int32, (group, width), 0)
         lane = lax.broadcasted_iota(jnp.int32, (group, width), 1)
-        panel_lane = lax.broadcasted_iota(jnp.int32, (panel, block), 1)
-
-        def step(p, carry):
-            first = panel * p
-            at = [pl.ds(pl.multiple_of(base + first + group * t, group), group) for t in range(groups)]
+        column = lambda x, at: jnp.broadcast_to(x[:, at : at + 1], (group, block))
+        for first in range(0, block, panel):
+            at = [slice(base + first + group * t, base + first + group * (t + 1)) for t in range(groups)]
             rows = [rest_ref[at[t], base:] for t in range(groups)]
-            column = lambda x, u, j: lane_of(x[:, :block], first + group * u + j)
-            done = factor_panel(rows, column, sublane)
+            done = factor_panel(rows, lambda x, u, j: column(x, first + group * u + j), sublane)
             for t in range(groups):
                 out_ref[at[t], base:] = jnp.where(lane >= sublane + first + group * t, done[t], 0.0)
-            done = jnp.concatenate(done, axis=0)
-
-            @pl.when(p + 1 < block // panel)
-            def _():
-                below = jnp.where(panel_lane >= first + panel, done[:, :block], 0.0)
-                rest_ref[base:end, base:] -= outer_of_few(below, done)
-
-            return carry
-
-        lax.fori_loop(0, block // panel, step, 0)
+            after = first + panel
+            if after < block:
+                done = jnp.concatenate(done, axis=0)
+                rest_ref[base + after : end, base:] -= outer_of_few(done[:, :block], done)[after:, :]
         for to in range(end, size, block):
             right = out_ref[base:end, to:]
             rest_ref[to : to + block, to:] -= outer_of_many(right[:, :block], right)

time: 86 us -> 85.6 us (level)
  no operation moved by 1% of the time
where the time goes in v2:
time: 85.6 us; the launch traced here: 85.4 us
  waiting for transfers between devices  36.1 us (42%)
  Pallas kernels  23.1 us (27%)
  starting transfers between devices  20.4 us (24%)
  local copies, waits for them, and re-layouts  4.45 us (5%)
  other arithmetic  1.18 us (1%)
    ppermute x9, waiting for transfers between devices, gathered(): move = lambda x, pairs: lax.ppermute(x, 'expert', between_chips(pairs))  25.4 us
    ppermute x9, starting transfers between devices, gathered(): move = lambda x, pairs: lax.ppermute(x, 'expert', between_chips(pairs))  12.9 us
    pallas_call x1, Pallas kernels, factor_rows(): pl.pallas_call(functools.partial(factor_kernel, rows_mean=rows_mean), in_...  12.6 us
    ppermute x5, waiting for transfers between devices, gathered(): lax.ppermute(x, 'dp', [(r, (r + s) % data_ranks) for r in range(data_rank...  10.6 us
    pallas_call x5, Pallas kernels, hidden_of(): pl.pallas_call(functools.partial(hidden_kernel, at=at, top=top), in_specs...  8.3 us
    ppermute x5, starting transfers between devices, gathered(): lax.ppermute(x, 'dp', [(r, (r + s) % data_ranks) for r in range(data_rank...  5.8 us
    pallas_call x1, Pallas kernels, partial_gram(): pl.pallas_call(gram_kernel, in_specs=[pl.BlockSpec(memory_space=pltpu.VME...  2.11 us
    slice x1, local copies, waits for them, and re-layouts, gathered(): below.append(move(tokens[i * half:(i + 1) * half], ring(1)))  1.86 us
  transfers between devices with their start and end apart: 20, of which 9 were waited for; matrix products, arithmetic and copies ran while one was open for 5% of the time, Pallas kernels for 12%

profile of v2, /device:TPU:0, one launch (start us, length us, event | category | flops | bytes accessed | tf_op | source)
XLA Modules:
  0.0 85.4 jit_solution(13946185160728975983)
XLA Ops:
  0.0 5.1 %collective-permute-start.3 = (bf16[128,2048]{1,0:T(8,128)(2,1)}, bf16[128,2048]{1,0:T(8,128)(2,1)S(1)}, u32[]{:S(2)}, u32[]{:S(2)}) collective-permute-start(bf16[128,2048]{1,0:T(8,128)(2,1)} %refs_0_.1), channel_id=1, source_target_pairs={{0,6},{1,7},{2,0},{3,1},{4,2},{5,3},{6,4},{7,5},{8,14},{9,15},{10,... | collective-permute-start | bytes 1572872 | tf_op jit(solution)/shard_map/ppermute | solution.py:94
  5.1 1.9 %fusion = (bf16[64,2048]{1,0:T(8,128)(2,1)}, bf16[64,2048]{1,0:T(8,128)(2,1)}) fusion(bf16[128,2048]{1,0:T(8,128)(2,1)} %refs_0_.1), kind=kLoop, calls=%fused_computation.4 | loop fusion | bytes 1048576 | tf_op jit(solution)/shard_map/slice | solution.py:104
  7.3 10.5 %collective-permute-done.3.refs_0_ = bf16[128,2048]{1,0:T(8,128)(2,1)S(1)} collective-permute-done((bf16[128,2048]{1,0:T(8,128)(2,1)}, bf16[128,2048]{1,0:T(8,128)(2,1)S(1)}, u32[]{:S(2)}, u32[]{:S(2)}) %collective-permute-start.3) | collective-permute-done | bytes 524320 | tf_op jit(solution)/shard_map/ppermute | solution.py:94
  17.8 1.3 %collective-permute-start.16 = (bf16[128,2048]{1,0:T(8,128)(2,1)S(1)}, bf16[128,2048]{1,0:T(8,128)(2,1)}, u32[]{:S(2)}, u32[]{:S(2)}) collective-permute-start(bf16[128,2048]{1,0:T(8,128)(2,1)S(1)} %collective-permute-done.3.refs_0_), channel_id=1, source_target_pairs={{4,2},{5,3},{2,0},{3,1},{12,10},{13,11},{10,8},{11,9},{20,18},{21,... | collective-permute-start | bytes 1572872 | tf_op jit(solution)/shard_map/ppermute | solution.py:94
  19.1 2.2 %collective-permute-start.7 = (s32[4,128]{1,0:T(4,128)}, s32[4,128]{1,0:T(4,128)S(1)}, u32[]{:S(2)}, u32[]{:S(2)}) collective-permute-start(s32[4,128]{1,0:T(4,128)} %bitcast.16), channel_id=1, source_target_pairs={{0,4},{1,5},{2,6},{3,7},{4,0},{5,1},{6,2},{7,3},{8,12},{9,13},{10,... | collective-permute-start | bytes 6152 | tf_op jit(solution)/shard_map/ppermute | solution.py:94
  21.3 2.7 %collective-permute-start.6 = (s32[4,128]{1,0:T(4,128)}, s32[4,128]{1,0:T(4,128)S(1)}, u32[]{:S(2)}, u32[]{:S(2)}) collective-permute-start(s32[4,128]{1,0:T(4,128)} %bitcast.17), channel_id=1, source_target_pairs={{0,2},{1,3},{2,4},{3,5},{4,6},{5,7},{6,0},{7,1},{8,10},{9,11},{10,... | collective-permute-start | bytes 6152 | tf_op jit(solution)/shard_map/ppermute | solution.py:94
  25.1 3.7 %collective-permute-done.10 = bf16[64,2048]{1,0:T(8,128)(2,1)S(1)} collective-permute-done((bf16[64,2048]{1,0:T(8,128)(2,1)}, bf16[64,2048]{1,0:T(8,128)(2,1)S(1)}, u32[]{:S(2)}, u32[]{:S(2)}) %collective-permute-start.10) | collective-permute-done | bytes 262176 | tf_op jit(solution)/shard_map/ppermute | solution.py:94
  30.5 9.6 %collective-permute-done.7 = s32[4,128]{1,0:T(4,128)S(1)} collective-permute-done((s32[4,128]{1,0:T(4,128)}, s32[4,128]{1,0:T(4,128)S(1)}, u32[]{:S(2)}, u32[]{:S(2)}) %collective-permute-start.7) | collective-permute-done | bytes 2080 | tf_op jit(solution)/shard_map/ppermute | solution.py:94
  40.7 1.2 %maximum_add_fusion.refs_0_ = bf16[128,2048]{1,0:T(8,128)(2,1)S(1)} fusion(bf16[128,2048]{1,0:T(8,128)(2,1)} %collective-permute-done.16, bf16[64,2048]{1,0:T(8,128)(2,1)S(1)} %collective-permute-done.15, bf16[64,2048]{1,0:T(8,128)(2,1)S(1)} %collective-permute-done.14), kind=kLoop, calls=%fused_computation | loop fusion | flops 1572864 | bytes 1572864 | tf_op jit(solution)/shard_map/add | solution.py:124
  42.4 1.2 %collective-permute-done.5 = s32[4,128]{1,0:T(4,128)S(1)} collective-permute-done((s32[4,128]{1,0:T(4,128)S(1)}, s32[4,128]{1,0:T(4,128)S(1)}, u32[]{:S(2)}, u32[]{:S(2)}) %collective-permute-start.5) | collective-permute-done | bytes 2080 | tf_op jit(solution)/shard_map/ppermute | solution.py:94
  44.2 1.6 %copy-done.1 = bf16[1,2048,512]{2,1,0:T(8,128)(2,1)S(1)} copy-done((bf16[1,2048,512]{2,1,0:T(8,128)(2,1)S(1)}, bf16[1,2048,512]{2,1,0:T(8,128)(2,1)}, u32[]{:S(2)}) %copy-start.1) | copy-done | bytes 2097176
  45.8 1.7 %hidden.5.refs_0_ = bf16[256,512]{1,0:T(8,128)(2,1)S(1)} custom-call(s32[1]{0:T(128)} %bitcast.1.me_ref, bf16[2048,512]{1,0:T(8,128)(2,1)S(1)} %bitcast.6, bf16[2048,512]{1,0:T(8,128)(2,1)S(1)} %bitcast.11, bf16[128,2048]{1,0:T(8,128)(2,1)S(1)} %copy-done.2, bf16[128,2048]{1,0:T(8,128)(2,1)S(1)} %collective-permute-done.refs_1_, s32[4,128]{1,0:T(4,128)S(1)} %bitcast.20, ...), custom_call_target="tpu_custom_call" | custom-call | flops 1073741824 | bytes 5505024 | tf_op jit(solution)/shard_map/hidden/pallas_call | solution.py:43
  47.5 1.6 %collective-permute-start.2 = (bf16[256,512]{1,0:T(8,128)(2,1)S(1)}, bf16[256,512]{1,0:T(8,128)(2,1)}, u32[]{:S(2)}, u32[]{:S(2)}) collective-permute-start(bf16[256,512]{1,0:T(8,128)(2,1)S(1)} %hidden.5.refs_0_), channel_id=1, source_target_pairs={{0,8},{8,0},{1,9},{9,1},{2,10},{10,2},{3,11},{11,3},{4,12},{12,4},... | collective-permute-start | bytes 786440 | tf_op jit(solution)/shard_map/ppermute | solution.py:96
  49.1 1.7 %hidden.7.refs_4_ = bf16[256,512]{1,0:T(8,128)(2,1)S(1)} custom-call(s32[1]{0:T(128)} %bitcast.1.me_ref, bf16[2048,512]{1,0:T(8,128)(2,1)S(1)} %bitcast.7, bf16[2048,512]{1,0:T(8,128)(2,1)S(1)} %bitcast.12, bf16[128,2048]{1,0:T(8,128)(2,1)S(1)} %constant_dynamic-update-slice_fusion.refs_0_, bf16[128,2048]{1,0:T(8,128)(2,1)S(1)} %collective-permute-done.12.refs_1_, ...), custom_call_target="tpu_custom_call" | custom-call | flops 1073741824 | bytes 5505024 | tf_op jit(solution)/shard_map/hidden/pallas_call | solution.py:43
  51.4 2.4 %hidden.6.refs_2_ = bf16[256,512]{1,0:T(8,128)(2,1)} custom-call(s32[1]{0:T(128)} %bitcast.1.me_ref, bf16[2048,512]{1,0:T(8,128)(2,1)S(1)} %bitcast.8, bf16[2048,512]{1,0:T(8,128)(2,1)S(1)} %bitcast.13, bf16[128,2048]{1,0:T(8,128)(2,1)S(1)} %collective-permute-done.3.refs_0_, bf16[128,2048]{1,0:T(8,128)(2,1)S(1)} %collective-permute-done.4.refs_1_, ...), custom_call_target="tpu_custom_call" | custom-call | flops 1073741824 | bytes 5505024 | tf_op jit(solution)/shard_map/hidden/pallas_call | solution.py:43
  53.9 1.5 %collective-permute-start.9 = (bf16[256,512]{1,0:T(8,128)(2,1)}, bf16[256,512]{1,0:T(8,128)(2,1)S(1)}, u32[]{:S(2)}, u32[]{:S(2)}) collective-permute-start(bf16[256,512]{1,0:T(8,128)(2,1)} %hidden.6.refs_2_), channel_id=1, source_target_pairs={{0,8},{8,0},{1,9},{9,1},{2,10},{10,2},{3,11},{11,3},{4,12},{12,4},... | collective-permute-start | bytes 786440 | tf_op jit(solution)/shard_map/ppermute | solution.py:96
  55.3 1.1 %hidden.8.refs_0_ = bf16[128,512]{1,0:T(8,128)(2,1)S(1)} custom-call(s32[1]{0:T(128)} %bitcast.1.me_ref, bf16[2048,512]{1,0:T(8,128)(2,1)S(1)} %bitcast.9, bf16[2048,512]{1,0:T(8,128)(2,1)S(1)} %bitcast.14, bf16[128,2048]{1,0:T(8,128)(2,1)S(1)} %maximum_add_fusion.refs_0_, s32[12,128]{1,0:T(8,128)S(1)} %pad_add_fusion.refs_2_.refs_1_), custom_call_target="tpu_custom_call" | custom-call | flops 536870912 | bytes 4849664 | tf_op jit(solution)/shard_map/hidden/pallas_call | solution.py:43
  57.1 1.3 %hidden.9.refs_2_ = bf16[128,512]{1,0:T(8,128)(2,1)S(1)} custom-call(s32[1]{0:T(128)} %bitcast.1.me_ref, bf16[2048,512]{1,0:T(8,128)(2,1)S(1)} %bitcast.10, bf16[2048,512]{1,0:T(8,128)(2,1)S(1)} %bitcast.15, bf16[128,2048]{1,0:T(8,128)(2,1)S(1)} %collective-permute-done.18.refs_0_, s32[12,128]{1,0:T(8,128)S(1)} %collective-permute-done.8.refs_3_.refs_1_), custom_call_target="tpu_custom_call" | custom-call | flops 536870912 | bytes 4849664 | tf_op jit(solution)/shard_map/hidden/pallas_call | solution.py:43
  58.4 1.6 %collective-permute-start.19 = (bf16[128,512]{1,0:T(8,128)(2,1)S(1)}, bf16[128,512]{1,0:T(8,128)(2,1)S(1)}, u32[]{:S(2)}, u32[]{:S(2)}) collective-permute-start(bf16[128,512]{1,0:T(8,128)(2,1)S(1)} %hidden.9.refs_2_), channel_id=1, source_target_pairs={{0,8},{8,0},{1,9},{9,1},{2,10},{10,2},{3,11},{11,3},{4,12},{12,4},... | collective-permute-start | bytes 393224 | tf_op jit(solution)/shard_map/ppermute | solution.py:96
  60.0 2.5 %collective-permute-done.13.refs_5_ = bf16[256,512]{1,0:T(8,128)(2,1)} collective-permute-done((bf16[256,512]{1,0:T(8,128)(2,1)S(1)}, bf16[256,512]{1,0:T(8,128)(2,1)}, u32[]{:S(2)}, u32[]{:S(2)}) %collective-permute-start.13) | collective-permute-done | bytes 262176 | tf_op jit(solution)/shard_map/ppermute | solution.py:96
  62.5 5.5 %collective-permute-done.9.refs_3_ = bf16[256,512]{1,0:T(8,128)(2,1)S(1)} collective-permute-done((bf16[256,512]{1,0:T(8,128)(2,1)}, bf16[256,512]{1,0:T(8,128)(2,1)S(1)}, u32[]{:S(2)}, u32[]{:S(2)}) %collective-permute-start.9) | collective-permute-done | bytes 262176 | tf_op jit(solution)/shard_map/ppermute | solution.py:96
  68.0 2.1 %partial_gram.1.early_ref = f32[512,512]{1,0:T(8,128)S(1)} custom-call(bf16[256,512]{1,0:T(8,128)(2,1)S(1)} %hidden.5.refs_0_, bf16[256,512]{1,0:T(8,128)(2,1)} %collective-permute-done.2.refs_1_, bf16[256,512]{1,0:T(8,128)(2,1)} %hidden.6.refs_2_, bf16[256,512]{1,0:T(8,128)(2,1)S(1)} %collective-permute-done.9.refs_3_, bf16[256,512]{1,0:T(8,128)(2,1)S(1)} %hidden.7.refs_4_, ...), custom_call_target="tpu_custom_call" | custom-call | flops 805306368 | bytes 2621440 | tf_op jit(solution)/shard_map/partial_gram/pallas_call | solution.py:71
  70.8 1.9 %collective-permute-done.19.refs_3_ = bf16[128,512]{1,0:T(8,128)(2,1)S(1)} collective-permute-done((bf16[128,512]{1,0:T(8,128)(2,1)S(1)}, bf16[128,512]{1,0:T(8,128)(2,1)S(1)}, u32[]{:S(2)}, u32[]{:S(2)}) %collective-permute-start.19) | collective-permute-done | bytes 131104 | tf_op jit(solution)/shard_map/ppermute | solution.py:96
  72.7 12.6 %factor.1 = f32[256,512]{1,0:T(8,128)} custom-call(s32[1]{0:T(128)} %bitcast.rank_ref, f32[512,512]{1,0:T(8,128)S(1)} %partial_gram.1.early_ref, bf16[128,512]{1,0:T(8,128)(2,1)S(1)} %hidden.8.refs_0_, bf16[128,512]{1,0:T(8,128)(2,1)S(1)} %collective-permute-done.17.refs_1_, bf16[128,512]{1,0:T(8,128)(2,1)S(1)} %hidden.9.refs_2_, ...), custom_call_target="tpu_custom_call" | custom-call | tf_op jit(solution)/shard_map/factor/pallas_call | solution.py:276
  (36 shorter events, 6.6 us)
Async XLA Ops:
  0.0 40.1 %copy-start.2 = (bf16[128,2048]{1,0:T(8,128)(2,1)S(1)}, bf16[128,2048]{1,0:T(8,128)(2,1)}, u32[]{:S(2)}) copy-start(bf16[128,2048]{1,0:T(8,128)(2,1)} %refs_0_.1) | copy-start | bytes 1572868
  0.0 40.0 %copy-start.3 = (s32[128,4]{0,1:T(4,128)S(1)}, s32[128,4]{0,1:T(4,128)}, u32[]{:S(2)}) copy-start(s32[128,4]{0,1:T(4,128)} %param.5) | copy-start | bytes 6148
  0.0 44.2 %copy-start = (bf16[1,2048,512]{2,1,0:T(8,128)(2,1)S(1)}, bf16[1,2048,512]{2,1,0:T(8,128)(2,1)}, u32[]{:S(2)}) copy-start(bf16[1,2048,512]{2,1,0:T(8,128)(2,1)} %param.6) | copy-start | bytes 6291460
  0.0 17.8 %collective-permute-start.3 = (bf16[128,2048]{1,0:T(8,128)(2,1)}, bf16[128,2048]{1,0:T(8,128)(2,1)S(1)}, u32[]{:S(2)}, u32[]{:S(2)}) collective-permute-start(bf16[128,2048]{1,0:T(8,128)(2,1)} %refs_0_.1), channel_id=1, source_target_pairs={{0,6},{1,7},{2,0},{3,1},{4,2},{5,3},{6,4},{7,5},{8,14},{9,15},{10,... | collective-permute-start | bytes 1572872 | tf_op jit(solution)/shard_map/ppermute | solution.py:94
  7.0 17.4 %collective-permute-start.11 = (bf16[64,2048]{1,0:T(8,128)(2,1)}, bf16[64,2048]{1,0:T(8,128)(2,1)}, u32[]{:S(2)}, u32[]{:S(2)}) collective-permute-start(bf16[64,2048]{1,0:T(8,128)(2,1)} %get-tuple-element.5), channel_id=1, source_target_pairs={{0,2},{1,3},{2,4},{3,5},{4,6},{5,7},{6,0},{7,1},{8,10},{9,11},{10,... | collective-permute-start | bytes 786440 | tf_op jit(solution)/shard_map/ppermute | solution.py:94
  7.0 21.8 %collective-permute-start.10 = (bf16[64,2048]{1,0:T(8,128)(2,1)}, bf16[64,2048]{1,0:T(8,128)(2,1)S(1)}, u32[]{:S(2)}, u32[]{:S(2)}) collective-permute-start(bf16[64,2048]{1,0:T(8,128)(2,1)} %get-tuple-element.6), channel_id=1, source_target_pairs={{0,2},{1,3},{2,4},{3,5},{4,6},{5,7},{6,0},{7,1},{8,10},{9,11},{10,... | collective-permute-start | bytes 786440 | tf_op jit(solution)/shard_map/ppermute | solution.py:94
  17.8 22.8 %collective-permute-start.16 = (bf16[128,2048]{1,0:T(8,128)(2,1)S(1)}, bf16[128,2048]{1,0:T(8,128)(2,1)}, u32[]{:S(2)}, u32[]{:S(2)}) collective-permute-start(bf16[128,2048]{1,0:T(8,128)(2,1)S(1)} %collective-permute-done.3.refs_0_), channel_id=1, source_target_pairs={{4,2},{5,3},{2,0},{3,1},{12,10},{13,11},{10,8},{11,9},{20,18},{21,... | collective-permute-start | bytes 1572872 | tf_op jit(solution)/shard_map/ppermute | solution.py:94
  19.1 20.9 %collective-permute-start.7 = (s32[4,128]{1,0:T(4,128)}, s32[4,128]{1,0:T(4,128)S(1)}, u32[]{:S(2)}, u32[]{:S(2)}) collective-permute-start(s32[4,128]{1,0:T(4,128)} %bitcast.16), channel_id=1, source_target_pairs={{0,4},{1,5},{2,6},{3,7},{4,0},{5,1},{6,2},{7,3},{8,12},{9,13},{10,... | collective-permute-start | bytes 6152 | tf_op jit(solution)/shard_map/ppermute | solution.py:94
  21.3 20.6 %collective-permute-start.6 = (s32[4,128]{1,0:T(4,128)}, s32[4,128]{1,0:T(4,128)S(1)}, u32[]{:S(2)}, u32[]{:S(2)}) collective-permute-start(s32[4,128]{1,0:T(4,128)} %bitcast.17), channel_id=1, source_target_pairs={{0,2},{1,3},{2,4},{3,5},{4,6},{5,7},{6,0},{7,1},{8,10},{9,11},{10,... | collective-permute-start | bytes 6152 | tf_op jit(solution)/shard_map/ppermute | solution.py:94
  24.4 15.6 %collective-permute-start.15 = (bf16[64,2048]{1,0:T(8,128)(2,1)}, bf16[64,2048]{1,0:T(8,128)(2,1)S(1)}, u32[]{:S(2)}, u32[]{:S(2)}) collective-permute-start(bf16[64,2048]{1,0:T(8,128)(2,1)} %collective-permute-done.11), channel_id=1, source_target_pairs={{2,4},{3,5},{4,6},{5,7},{10,12},{11,13},{12,14},{13,15},{18,20},{1... | collective-permute-start | bytes 786440 | tf_op jit(solution)/shard_map/ppermute | solution.py:94
  28.8 11.3 %collective-permute-start.14 = (bf16[64,2048]{1,0:T(8,128)(2,1)S(1)}, bf16[64,2048]{1,0:T(8,128)(2,1)S(1)}, u32[]{:S(2)}, u32[]{:S(2)}) collective-permute-start(bf16[64,2048]{1,0:T(8,128)(2,1)S(1)} %collective-permute-done.10), channel_id=1, source_target_pairs={{2,4},{3,5},{4,6},{5,7},{10,12},{11,13},{12,14},{13,15},{18,20},{1... | collective-permute-start | bytes 786440 | tf_op jit(solution)/shard_map/ppermute | solution.py:94
  40.0 3.6 %collective-permute-start.5 = (s32[4,128]{1,0:T(4,128)S(1)}, s32[4,128]{1,0:T(4,128)S(1)}, u32[]{:S(2)}, u32[]{:S(2)}) collective-permute-start(s32[4,128]{1,0:T(4,128)S(1)} %bitcast.18), channel_id=1, source_target_pairs={{0,6},{1,7},{2,0},{3,1},{4,2},{5,3},{6,4},{7,5},{8,14},{9,15},{10,... | collective-permute-start | bytes 6152 | tf_op jit(solution)/shard_map/ppermute | solution.py:94
  40.1 4.2 %collective-permute-start = (bf16[128,2048]{1,0:T(8,128)(2,1)S(1)}, bf16[128,2048]{1,0:T(8,128)(2,1)S(1)}, u32[]{:S(2)}, u32[]{:S(2)}) collective-permute-start(bf16[128,2048]{1,0:T(8,128)(2,1)S(1)} %copy-done.2), channel_id=1, source_target_pairs={{0,1},{1,0},{2,3},{3,2},{4,5},{5,4},{6,7},{7,6},{8,9},{9,8},{10,11... | collective-permute-start | bytes 1572872 | tf_op jit(solution)/shard_map/ppermute | solution.py:95
  40.2 9.0 %collective-permute-start.12 = (bf16[128,2048]{1,0:T(8,128)(2,1)S(1)}, bf16[128,2048]{1,0:T(8,128)(2,1)S(1)}, u32[]{:S(2)}, u32[]{:S(2)}) collective-permute-start(bf16[128,2048]{1,0:T(8,128)(2,1)S(1)} %constant_dynamic-update-slice_fusion.refs_0_), channel_id=1, source_target_pairs={{0,1},{1,0},{2,3},{3,2},{4,5},{5,4},{6,7},{7,6},{8,9},{9,8},{10,11... | collective-permute-start | bytes 1572872 | tf_op jit(solution)/shard_map/ppermute | solution.py:95
  40.6 10.8 %collective-permute-start.4 = (bf16[128,2048]{1,0:T(8,128)(2,1)S(1)}, bf16[128,2048]{1,0:T(8,128)(2,1)S(1)}, u32[]{:S(2)}, u32[]{:S(2)}) collective-permute-start(bf16[128,2048]{1,0:T(8,128)(2,1)S(1)} %collective-permute-done.3.refs_0_), channel_id=1, source_target_pairs={{0,1},{1,0},{2,3},{3,2},{4,5},{5,4},{6,7},{7,6},{8,9},{9,8},{10,11... | collective-permute-start | bytes 1572872 | tf_op jit(solution)/shard_map/ppermute | solution.py:95
  41.9 1.7 %collective-permute-start.1 = (s32[4,128]{1,0:T(4,128)S(1)}, s32[4,128]{1,0:T(4,128)S(1)}, u32[]{:S(2)}, u32[]{:S(2)}) collective-permute-start(s32[4,128]{1,0:T(4,128)S(1)} %bitcast.19), channel_id=1, source_target_pairs={{0,1},{1,0},{2,3},{3,2},{4,5},{5,4},{6,7},{7,6},{8,9},{9,8},{10,11... | collective-permute-start | bytes 6152 | tf_op jit(solution)/shard_map/ppermute | solution.py:95
  43.6 13.5 %collective-permute-start.18 = (bf16[128,2048]{1,0:T(8,128)(2,1)S(1)}, bf16[128,2048]{1,0:T(8,128)(2,1)S(1)}, u32[]{:S(2)}, u32[]{:S(2)}) collective-permute-start(bf16[128,2048]{1,0:T(8,128)(2,1)S(1)} %maximum_add_fusion.refs_0_), channel_id=1, source_target_pairs={{0,1},{1,0},{2,3},{3,2},{4,5},{5,4},{6,7},{7,6},{8,9},{9,8},{10,11... | collective-permute-start | bytes 1572872 | tf_op jit(solution)/shard_map/ppermute | solution.py:95
  43.7 5.4 %collective-permute-start.8 = (s32[12,128]{1,0:T(8,128)S(1)}, s32[12,128]{1,0:T(8,128)S(1)}, u32[]{:S(2)}, u32[]{:S(2)}) collective-permute-start(s32[12,128]{1,0:T(8,128)S(1)} %pad_add_fusion.refs_2_.refs_1_), channel_id=1, source_target_pairs={{0,1},{1,0},{2,3},{3,2},{4,5},{5,4},{6,7},{7,6},{8,9},{9,8},{10,11... | collective-permute-start | bytes 18440 | tf_op jit(solution)/shard_map/ppermute | solution.py:95
  44.2 1.6 %copy-start.1 = (bf16[1,2048,512]{2,1,0:T(8,128)(2,1)S(1)}, bf16[1,2048,512]{2,1,0:T(8,128)(2,1)}, u32[]{:S(2)}) copy-start(bf16[1,2048,512]{2,1,0:T(8,128)(2,1)} %param.7) | copy-start | bytes 6291460
  47.5 12.4 %collective-permute-start.2 = (bf16[256,512]{1,0:T(8,128)(2,1)S(1)}, bf16[256,512]{1,0:T(8,128)(2,1)}, u32[]{:S(2)}, u32[]{:S(2)}) collective-permute-start(bf16[256,512]{1,0:T(8,128)(2,1)S(1)} %hidden.5.refs_0_), channel_id=1, source_target_pairs={{0,8},{8,0},{1,9},{9,1},{2,10},{10,2},{3,11},{11,3},{4,12},{12,4},... | collective-permute-start | bytes 786440 | tf_op jit(solution)/shard_map/ppermute | solution.py:96
  50.8 11.7 %collective-permute-start.13 = (bf16[256,512]{1,0:T(8,128)(2,1)S(1)}, bf16[256,512]{1,0:T(8,128)(2,1)}, u32[]{:S(2)}, u32[]{:S(2)}) collective-permute-start(bf16[256,512]{1,0:T(8,128)(2,1)S(1)} %hidden.7.refs_4_), channel_id=1, source_target_pairs={{0,8},{8,0},{1,9},{9,1},{2,10},{10,2},{3,11},{11,3},{4,12},{12,4},... | collective-permute-start | bytes 786440 | tf_op jit(solution)/shard_map/ppermute | solution.py:96
  53.9 14.2 %collective-permute-start.9 = (bf16[256,512]{1,0:T(8,128)(2,1)}, bf16[256,512]{1,0:T(8,128)(2,1)S(1)}, u32[]{:S(2)}, u32[]{:S(2)}) collective-permute-start(bf16[256,512]{1,0:T(8,128)(2,1)} %hidden.6.refs_2_), channel_id=1, source_target_pairs={{0,8},{8,0},{1,9},{9,1},{2,10},{10,2},{3,11},{11,3},{4,12},{12,4},... | collective-permute-start | bytes 786440 | tf_op jit(solution)/shard_map/ppermute | solution.py:96
  56.5 14.3 %collective-permute-start.17 = (bf16[128,512]{1,0:T(8,128)(2,1)S(1)}, bf16[128,512]{1,0:T(8,128)(2,1)S(1)}, u32[]{:S(2)}, u32[]{:S(2)}) collective-permute-start(bf16[128,512]{1,0:T(8,128)(2,1)S(1)} %hidden.8.refs_0_), channel_id=1, source_target_pairs={{0,8},{8,0},{1,9},{9,1},{2,10},{10,2},{3,11},{11,3},{4,12},{12,4},... | collective-permute-start | bytes 393224 | tf_op jit(solution)/shard_map/ppermute | solution.py:96
  58.4 14.3 %collective-permute-start.19 = (bf16[128,512]{1,0:T(8,128)(2,1)S(1)}, bf16[128,512]{1,0:T(8,128)(2,1)S(1)}, u32[]{:S(2)}, u32[]{:S(2)}) collective-permute-start(bf16[128,512]{1,0:T(8,128)(2,1)S(1)} %hidden.9.refs_2_), channel_id=1, source_target_pairs={{0,8},{8,0},{1,9},{9,1},{2,10},{10,2},{3,11},{11,3},{4,12},{12,4},... | collective-permute-start | bytes 393224 | tf_op jit(solution)/shard_map/ppermute | solution.py:96

commit v3 on v2

--- a/solution.py
+++ b/solution.py
@@ -13,16 +13,16 @@
 CHIPS_DENSE = 4
 
 
-def hidden_kernel(me_ref, gate_ref, up_ref, *refs, at, top):
+def hidden_kernel(me_ref, gate_ref, up_ref, *refs, at, top, first):
     hidden_ref = refs[-1]
     count = len(refs) // 2
     pieces, names = refs[:count], refs[count:-1]
     hw = gate_ref.shape[1]
     width = 256
     member = []
-    for name in names:
+    for piece, name in zip(pieces, names):
         hit = (name[at * top : (at + 1) * top, :] == me_ref[0]).astype(jnp.float32)
-        member.append(jnp.max(hit.T, axis=1, keepdims=True))
+        member.append(jnp.max(hit.T[first : first + piece.shape[0], :], axis=1, keepdims=True))
     member = jnp.concatenate(member, axis=0)
     x = jnp.concatenate([piece[...] for piece in pieces], axis=0)
 
@@ -37,16 +37,16 @@
     lax.fori_loop(0, hw // width, step, 0)
 
 
-def hidden_of(me, pieces, names, at, top, gate_w, up_w):
+def hidden_of(me, pieces, names, at, top, first, gate_w, up_w):
     rows = sum(piece.shape[0] for piece in pieces)
     model, hw = gate_w.shape
     return pl.pallas_call(
-        functools.partial(hidden_kernel, at=at, top=top),
+        functools.partial(hidden_kernel, at=at, top=top, first=first),
         in_specs=[pl.BlockSpec(memory_space=pltpu.SMEM)]
         + [pl.BlockSpec(memory_space=pltpu.VMEM)] * (2 + 2 * len(pieces)),
         out_specs=pl.BlockSpec(memory_space=pltpu.VMEM),
         out_shape=jax.ShapeDtypeStruct((rows, hw), jnp.bfloat16),
-        compiler_params=pltpu.CompilerParams(vmem_limit_bytes=24 << 20),
+        compiler_params=pltpu.CompilerParams(vmem_limit_bytes=6 << 20),
         cost_estimate=pl.CostEstimate(
             flops=2 * rows * model * 2 * hw,
             bytes_accessed=2 * (rows * model + 2 * model * hw) + 2 * rows * hw,
@@ -73,7 +73,7 @@
         in_specs=[pl.BlockSpec(memory_space=pltpu.VMEM)] * len(hiddens),
         out_specs=pl.BlockSpec(memory_space=pltpu.VMEM),
         out_shape=jax.ShapeDtypeStruct((hw, hw), jnp.float32),
-        compiler_params=pltpu.CompilerParams(vmem_limit_bytes=24 << 20),
+        compiler_params=pltpu.CompilerParams(vmem_limit_bytes=6 << 20),
         cost_estimate=pl.CostEstimate(
             flops=2 * rows * hw * hw,
             bytes_accessed=2 * rows * hw + 4 * hw * hw,
@@ -99,10 +99,11 @@
     names = routes.T
     above = move(tokens, ring(-1))
     half = tokens.shape[0] // 2
-    below, on_up = [], []
+    below, on_up, on_down = [], [], []
     for i in range(2):
         below.append(move(tokens[i * half : (i + 1) * half], ring(1)))
-    on_down = move(above, [(2, 1), (1, 0)])
+    for i in range(2):
+        on_down.append(move(above[i * half : (i + 1) * half], [(2, 1), (1, 0)]))
     for i in range(2):
         on_up.append(move(below[i], [(1, 2), (2, 3)]))
     below = jnp.concatenate(below, axis=0)
@@ -117,16 +118,20 @@
     for slot, own in enumerate([tokens, above, below]):
         other = swap(own)
         who, at = ((names, other_names), 0) if slot == 0 else ((moved, other_moved), slot - 1)
-        hidden = hidden_of(me, (own, other), who, at, top, gate_w, up_w)
+        hidden = hidden_of(me, (own, other), who, at, top, 0, gate_w, up_w)
         hiddens.append([hidden] + [turn(hidden, s) for s in range(1, data_ranks)])
     early = partial_gram(sum(hiddens, []))
 
-    last = jnp.concatenate(on_up, axis=0) + on_down
-    other = swap(last)
     late = []
-    for piece, who in ((last, moved), (other, other_moved)):
-        hidden = hidden_of(me, (piece,), (who,), 2, top, gate_w, up_w)
-        late += [hidden] + [turn(hidden, s) for s in range(1, data_ranks)]
+    slot = 3
+    for i in range(2):
+        last = on_up[i] + on_down[i]
+        other = swap(last)
+        pieces = [((last, other), (moved, other_moved))] if i == 0 else [((last,), (moved,)), ((other,), (other_moved,))]
+        for piece, who in pieces:
+            hidden = hidden_of(me, piece, who, 2, top, i * half, gate_w, up_w)
+            late += [hidden] + [turn(hidden, s) for s in range(1, data_ranks)]
+            slot += 1
     return early, late
 
 
@@ -279,7 +284,7 @@
         out_specs=pl.BlockSpec(memory_space=pltpu.VMEM),
         out_shape=jax.ShapeDtypeStruct((size // data_ranks, size), jnp.float32),
         scratch_shapes=[pltpu.VMEM((size, size), jnp.float32)] * 2,
-        compiler_params=pltpu.CompilerParams(vmem_limit_bytes=24 << 20),
+        compiler_params=pltpu.CompilerParams(vmem_limit_bytes=6 << 20),
         name="factor",
     )(rank, early, *late)
 

time: 85.6 us -> 88.7 us (1.036)
  waiting for transfers between devices: 36.1 us -> 15.1 us
  starting transfers between devices: 20.4 us -> 34.4 us
  Pallas kernels: 23.1 us -> 29.6 us
  local copies, waits for them, and re-layouts: 4.45 us -> 7.74 us
    ppermute x9 -> x10, starting transfers between devices: 12.9 us -> 26.7 us  [gathered(): move = lambda x, pairs: lax.ppermute(x, 'expert', between_chips(pairs))]
    ppermute x9 -> x10, waiting for transfers between devices: 25.4 us -> 11.9 us  [gathered(): move = lambda x, pairs: lax.ppermute(x, 'expert', between_chips(pairs))]
    ppermute x5 -> x6, waiting for transfers between devices: 10.6 us -> 3.22 us  [gathered(): lax.ppermute(x, 'dp', [(r, (r + s) % data_ranks) for r in range(data_rank...]
    pallas_call x5 -> x6, Pallas kernels: 8.3 us -> 14.8 us  [hidden_of(): pl.pallas_call(functools.partial(hidden_kernel, at=at, top=top, first=fir...]
    unnamed x9 -> x19, local copies, waits for them, and re-layouts: 1.62 us -> 4.87 us
    ppermute x5 -> x6, starting transfers between devices: 5.8 us -> 6.34 us  [gathered(): lax.ppermute(x, 'dp', [(r, (r + s) % data_ranks) for r in range(data_rank...]
  transfers between devices with their start and end apart: 20 -> 23, of which waited for: 9 -> 6; matrix products, arithmetic and copies ran while one was open for 5% -> 5% of each run, Pallas kernels for 12% -> 19%
where the time goes in v3:
time: 88.7 us; the launch traced here: 88.2 us
  starting transfers between devices  34.4 us (39%)
  Pallas kernels  29.6 us (33%)
  waiting for transfers between devices  15.1 us (17%)
  local copies, waits for them, and re-layouts  7.74 us (9%)
  other arithmetic  1.09 us (1%)
    ppermute x10, starting transfers between devices, gathered(): move = lambda x, pairs: lax.ppermute(x, 'expert', between_chips(pairs))  26.7 us
    pallas_call x6, Pallas kernels, hidden_of(): pl.pallas_call(functools.partial(hidden_kernel, at=at, top=top, first=fir...  14.8 us
    pallas_call x1, Pallas kernels, factor_rows(): pl.pallas_call(functools.partial(factor_kernel, rows_mean=rows_mean), in_...  12.6 us
    ppermute x10, waiting for transfers between devices, gathered(): move = lambda x, pairs: lax.ppermute(x, 'expert', between_chips(pairs))  11.9 us
    ppermute x6, starting transfers between devices, gathered(): lax.ppermute(x, 'dp', [(r, (r + s) % data_ranks) for r in range(data_rank...  6.34 us
    unnamed x19, local copies, waits for them, and re-layouts  4.87 us
    ppermute x6, waiting for transfers between devices, gathered(): lax.ppermute(x, 'dp', [(r, (r + s) % data_ranks) for r in range(data_rank...  3.22 us
    pallas_call x1, Pallas kernels, partial_gram(): pl.pallas_call(gram_kernel, in_specs=[pl.BlockSpec(memory_space=pltpu.VME...  2.18 us
  transfers between devices with their start and end apart: 23, of which 6 were waited for; matrix products, arithmetic and copies ran while one was open for 5% of the time, Pallas kernels for 19%

profile of v3, /device:TPU:0, one launch (start us, length us, event | category | flops | bytes accessed | tf_op | source)
XLA Modules:
  0.0 88.2 jit_solution(12383993820566675730)
XLA Ops:
  0.0 1.2 %fusion.1 = (bf16[64,2048]{1,0:T(8,128)(2,1)S(1)}, bf16[64,2048]{1,0:T(8,128)(2,1)S(1)}) fusion(bf16[128,2048]{1,0:T(8,128)(2,1)} %refs_0_.1), kind=kLoop, calls=%fused_computation.4 | loop fusion | bytes 1048576 | tf_op jit(solution)/shard_map/slice | solution.py:104
  1.2 3.1 %collective-permute-start.10 = (bf16[64,2048]{1,0:T(8,128)(2,1)S(1)}, bf16[64,2048]{1,0:T(8,128)(2,1)}, u32[]{:S(2)}, u32[]{:S(2)}) collective-permute-start(bf16[64,2048]{1,0:T(8,128)(2,1)S(1)} %get-tuple-element.8), channel_id=1, source_target_pairs={{0,2},{1,3},{2,4},{3,5},{4,6},{5,7},{6,0},{7,1},{8,10},{9,11},{10,... | collective-permute-start | bytes 786440 | tf_op jit(solution)/shard_map/ppermute | solution.py:94
  4.3 2.1 %collective-permute-start.3 = (bf16[128,2048]{1,0:T(8,128)(2,1)}, bf16[128,2048]{1,0:T(8,128)(2,1)S(1)}, u32[]{:S(2)}, u32[]{:S(2)}) collective-permute-start(bf16[128,2048]{1,0:T(8,128)(2,1)} %refs_0_.1), channel_id=1, source_target_pairs={{0,6},{1,7},{2,0},{3,1},{4,2},{5,3},{6,4},{7,5},{8,14},{9,15},{10,... | collective-permute-start | bytes 1572872 | tf_op jit(solution)/shard_map/ppermute | solution.py:94
  6.4 2.5 %collective-permute-start.7 = (s32[4,128]{1,0:T(4,128)}, s32[4,128]{1,0:T(4,128)S(1)}, u32[]{:S(2)}, u32[]{:S(2)}) collective-permute-start(s32[4,128]{1,0:T(4,128)} %bitcast.18), channel_id=1, source_target_pairs={{0,4},{1,5},{2,6},{3,7},{4,0},{5,1},{6,2},{7,3},{8,12},{9,13},{10,... | collective-permute-start | bytes 6152 | tf_op jit(solution)/shard_map/ppermute | solution.py:94
  8.9 1.9 %collective-permute-start.6 = (s32[4,128]{1,0:T(4,128)}, s32[4,128]{1,0:T(4,128)S(1)}, u32[]{:S(2)}, u32[]{:S(2)}) collective-permute-start(s32[4,128]{1,0:T(4,128)} %bitcast.19), channel_id=1, source_target_pairs={{0,2},{1,3},{2,4},{3,5},{4,6},{5,7},{6,0},{7,1},{8,10},{9,11},{10,... | collective-permute-start | bytes 6152 | tf_op jit(solution)/shard_map/ppermute | solution.py:94
  10.8 2.9 %collective-permute-done.10 = bf16[64,2048]{1,0:T(8,128)(2,1)} collective-permute-done((bf16[64,2048]{1,0:T(8,128)(2,1)S(1)}, bf16[64,2048]{1,0:T(8,128)(2,1)}, u32[]{:S(2)}, u32[]{:S(2)}) %collective-permute-start.10) | collective-permute-done | bytes 262176 | tf_op jit(solution)/shard_map/ppermute | solution.py:94
  13.7 13.2 %collective-permute-start.5 = (s32[4,128]{1,0:T(4,128)}, s32[4,128]{1,0:T(4,128)S(1)}, u32[]{:S(2)}, u32[]{:S(2)}) collective-permute-start(s32[4,128]{1,0:T(4,128)} %bitcast.20), channel_id=1, source_target_pairs={{0,6},{1,7},{2,0},{3,1},{4,2},{5,3},{6,4},{7,5},{8,14},{9,15},{10,... | collective-permute-start | bytes 6152 | tf_op jit(solution)/shard_map/ppermute | solution.py:94
  26.9 1.7 %constant_dynamic-update-slice_fusion.1 = bf16[128,2048]{1,0:T(8,128)(2,1)} fusion(bf16[64,2048]{1,0:T(8,128)(2,1)} %collective-permute-done.10), kind=kLoop, calls=%fused_computation.2 | loop fusion | bytes 524288
  33.1 1.3 %collective-permute-start.15 = (bf16[64,2048]{1,0:T(8,128)(2,1)}, bf16[64,2048]{1,0:T(8,128)(2,1)}, u32[]{:S(2)}, u32[]{:S(2)}) collective-permute-start(bf16[64,2048]{1,0:T(8,128)(2,1)} %get-tuple-element.6), channel_id=1, source_target_pairs={{4,2},{5,3},{2,0},{3,1},{12,10},{13,11},{10,8},{11,9},{20,18},{21,... | collective-permute-start | bytes 786440 | tf_op jit(solution)/shard_map/ppermute | solution.py:94
  35.1 1.3 %collective-permute-start.19 = (bf16[64,2048]{1,0:T(8,128)(2,1)}, bf16[64,2048]{1,0:T(8,128)(2,1)S(1)}, u32[]{:S(2)}, u32[]{:S(2)}) collective-permute-start(bf16[64,2048]{1,0:T(8,128)(2,1)} %get-tuple-element.5), channel_id=1, source_target_pairs={{4,2},{5,3},{2,0},{3,1},{12,10},{13,11},{10,8},{11,9},{20,18},{21,... | collective-permute-start | bytes 786440 | tf_op jit(solution)/shard_map/ppermute | solution.py:94
  36.4 7.9 %collective-permute-done.15 = bf16[64,2048]{1,0:T(8,128)(2,1)} collective-permute-done((bf16[64,2048]{1,0:T(8,128)(2,1)}, bf16[64,2048]{1,0:T(8,128)(2,1)}, u32[]{:S(2)}, u32[]{:S(2)}) %collective-permute-start.15) | collective-permute-done | bytes 262176 | tf_op jit(solution)/shard_map/ppermute | solution.py:94
  44.3 1.6 %copy-done.1 = bf16[1,2048,512]{2,1,0:T(8,128)(2,1)S(1)} copy-done((bf16[1,2048,512]{2,1,0:T(8,128)(2,1)S(1)}, bf16[1,2048,512]{2,1,0:T(8,128)(2,1)}, u32[]{:S(2)}) %copy-start.1) | copy-done | bytes 2097176
  45.9 3.0 %hidden.6.refs_0_ = bf16[256,512]{1,0:T(8,128)(2,1)S(1)} custom-call(s32[1]{0:T(128)} %bitcast.1.me_ref, bf16[2048,512]{1,0:T(8,128)(2,1)S(1)} %bitcast.6, bf16[2048,512]{1,0:T(8,128)(2,1)S(1)} %bitcast.12, bf16[128,2048]{1,0:T(8,128)(2,1)S(1)} %copy-done.4, bf16[128,2048]{1,0:T(8,128)(2,1)} %collective-permute-done.refs_1_, s32[4,128]{1,0:T(4,128)S(1)} %bitcast.22, ...), custom_call_target="tpu_custom_call" | custom-call | flops 1073741824 | bytes 5505024 | tf_op jit(solution)/shard_map/hidden/pallas_call | solution.py:43
  49.9 1.6 %collective-permute-start.2 = (bf16[256,512]{1,0:T(8,128)(2,1)S(1)}, bf16[256,512]{1,0:T(8,128)(2,1)}, u32[]{:S(2)}, u32[]{:S(2)}) collective-permute-start(bf16[256,512]{1,0:T(8,128)(2,1)S(1)} %hidden.6.refs_0_), channel_id=1, source_target_pairs={{0,8},{8,0},{1,9},{9,1},{2,10},{10,2},{3,11},{11,3},{4,12},{12,4},... | collective-permute-start | bytes 786440 | tf_op jit(solution)/shard_map/ppermute | solution.py:96
  51.7 3.7 %hidden.8.refs_4_ = bf16[256,512]{1,0:T(8,128)(2,1)} custom-call(s32[1]{0:T(128)} %bitcast.1.me_ref, bf16[2048,512]{1,0:T(8,128)(2,1)S(1)} %bitcast.7, bf16[2048,512]{1,0:T(8,128)(2,1)S(1)} %bitcast.13, bf16[128,2048]{1,0:T(8,128)(2,1)} %constant_dynamic-update-slice_fusion.refs_0_, bf16[128,2048]{1,0:T(8,128)(2,1)} %collective-permute-done.12.refs_1_, ...), custom_call_target="tpu_custom_call" | custom-call | flops 1073741824 | bytes 5505024 | tf_op jit(solution)/shard_map/hidden/pallas_call | solution.py:43
  56.1 3.5 %hidden.7.refs_2_ = bf16[256,512]{1,0:T(8,128)(2,1)} custom-call(s32[1]{0:T(128)} %bitcast.1.me_ref, bf16[2048,512]{1,0:T(8,128)(2,1)S(1)} %bitcast.8, bf16[2048,512]{1,0:T(8,128)(2,1)S(1)} %bitcast.14, bf16[128,2048]{1,0:T(8,128)(2,1)S(1)} %collective-permute-done.3.refs_0_, bf16[128,2048]{1,0:T(8,128)(2,1)} %collective-permute-done.4.refs_1_, ...), custom_call_target="tpu_custom_call" | custom-call | flops 1073741824 | bytes 5505024 | tf_op jit(solution)/shard_map/hidden/pallas_call | solution.py:43
  59.6 1.5 %collective-permute-start.9 = (bf16[256,512]{1,0:T(8,128)(2,1)}, bf16[256,512]{1,0:T(8,128)(2,1)S(1)}, u32[]{:S(2)}, u32[]{:S(2)}) collective-permute-start(bf16[256,512]{1,0:T(8,128)(2,1)} %hidden.7.refs_2_), channel_id=1, source_target_pairs={{0,8},{8,0},{1,9},{9,1},{2,10},{10,2},{3,11},{11,3},{4,12},{12,4},... | collective-permute-start | bytes 786440 | tf_op jit(solution)/shard_map/ppermute | solution.py:96
  62.9 1.6 %copy-done.3 = bf16[1,2048,512]{2,1,0:T(8,128)(2,1)S(1)} copy-done((bf16[1,2048,512]{2,1,0:T(8,128)(2,1)S(1)}, bf16[1,2048,512]{2,1,0:T(8,128)(2,1)}, u32[]{:S(2)}) %copy-start.3) | copy-done | bytes 2097176
  64.4 1.2 %hidden.10.refs_2_ = bf16[64,512]{1,0:T(8,128)(2,1)S(1)} custom-call(s32[1]{0:T(128)} %bitcast.1.me_ref, bf16[2048,512]{1,0:T(8,128)(2,1)S(1)} %bitcast.10, bf16[2048,512]{1,0:T(8,128)(2,1)S(1)} %bitcast.16, bf16[64,2048]{1,0:T(8,128)(2,1)S(1)} %add.7.refs_0_, s32[12,128]{1,0:T(8,128)S(1)} %pad_add_fusion.refs_2_.refs_1_), custom_call_target="tpu_custom_call" | custom-call | flops 268435456 | bytes 4521984 | tf_op jit(solution)/shard_map/hidden/pallas_call | solution.py:43
  65.6 1.6 %collective-permute-start.20 = (bf16[64,512]{1,0:T(8,128)(2,1)S(1)}, bf16[64,512]{1,0:T(8,128)(2,1)S(1)}, u32[]{:S(2)}, u32[]{:S(2)}) collective-permute-start(bf16[64,512]{1,0:T(8,128)(2,1)S(1)} %hidden.10.refs_2_), channel_id=1, source_target_pairs={{0,8},{8,0},{1,9},{9,1},{2,10},{10,2},{3,11},{11,3},{4,12},{12,4},... | collective-permute-start | bytes 196616 | tf_op jit(solution)/shard_map/ppermute | solution.py:96
  67.2 2.3 %hidden.11.refs_4_ = bf16[64,512]{1,0:T(8,128)(2,1)S(1)} custom-call(s32[1]{0:T(128)} %bitcast.1.me_ref, bf16[2048,512]{1,0:T(8,128)(2,1)S(1)} %bitcast.11, bf16[2048,512]{1,0:T(8,128)(2,1)S(1)} %bitcast.17, bf16[64,2048]{1,0:T(8,128)(2,1)} %collective-permute-done.21.refs_0_, s32[12,128]{1,0:T(8,128)S(1)} %collective-permute-done.8.refs_3_.refs_1_), custom_call_target="tpu_custom_call" | custom-call | flops 268435456 | bytes 4521984 | tf_op jit(solution)/shard_map/hidden/pallas_call | solution.py:43
  70.4 2.2 %partial_gram.1.early_ref = f32[512,512]{1,0:T(8,128)S(1)} custom-call(bf16[256,512]{1,0:T(8,128)(2,1)S(1)} %hidden.6.refs_0_, bf16[256,512]{1,0:T(8,128)(2,1)} %collective-permute-done.2.refs_1_, bf16[256,512]{1,0:T(8,128)(2,1)} %hidden.7.refs_2_, bf16[256,512]{1,0:T(8,128)(2,1)S(1)} %collective-permute-done.9.refs_3_, bf16[256,512]{1,0:T(8,128)(2,1)} %hidden.8.refs_4_, ...), custom_call_target="tpu_custom_call" | custom-call | flops 805306368 | bytes 2621440 | tf_op jit(solution)/shard_map/partial_gram/pallas_call | solution.py:71
  72.6 2.0 %collective-permute-done.20.refs_3_ = bf16[64,512]{1,0:T(8,128)(2,1)S(1)} collective-permute-done((bf16[64,512]{1,0:T(8,128)(2,1)S(1)}, bf16[64,512]{1,0:T(8,128)(2,1)S(1)}, u32[]{:S(2)}, u32[]{:S(2)}) %collective-permute-start.20) | collective-permute-done | bytes 65568 | tf_op jit(solution)/shard_map/ppermute | solution.py:96
  75.6 12.6 %factor.1 = f32[256,512]{1,0:T(8,128)} custom-call(s32[1]{0:T(128)} %bitcast.rank_ref, f32[512,512]{1,0:T(8,128)S(1)} %partial_gram.1.early_ref, bf16[128,512]{1,0:T(8,128)(2,1)S(1)} %hidden.9.refs_0_, bf16[128,512]{1,0:T(8,128)(2,1)S(1)} %collective-permute-done.17.refs_1_, bf16[64,512]{1,0:T(8,128)(2,1)S(1)} %hidden.10.refs_2_, ...), custom_call_target="tpu_custom_call" | custom-call | tf_op jit(solution)/shard_map/factor/pallas_call | solution.py:281
  (55 shorter events, 10.7 us)
Async XLA Ops:
  0.0 44.3 %copy-start = (bf16[1,2048,512]{2,1,0:T(8,128)(2,1)S(1)}, bf16[1,2048,512]{2,1,0:T(8,128)(2,1)}, u32[]{:S(2)}) copy-start(bf16[1,2048,512]{2,1,0:T(8,128)(2,1)} %param.6) | copy-start | bytes 6291460
  1.2 12.4 %collective-permute-start.10 = (bf16[64,2048]{1,0:T(8,128)(2,1)S(1)}, bf16[64,2048]{1,0:T(8,128)(2,1)}, u32[]{:S(2)}, u32[]{:S(2)}) collective-permute-start(bf16[64,2048]{1,0:T(8,128)(2,1)S(1)} %get-tuple-element.8), channel_id=1, source_target_pairs={{0,2},{1,3},{2,4},{3,5},{4,6},{5,7},{6,0},{7,1},{8,10},{9,11},{10,... | collective-permute-start | bytes 786440 | tf_op jit(solution)/shard_map/ppermute | solution.py:94
  4.3 27.3 %collective-permute-start.3 = (bf16[128,2048]{1,0:T(8,128)(2,1)}, bf16[128,2048]{1,0:T(8,128)(2,1)S(1)}, u32[]{:S(2)}, u32[]{:S(2)}) collective-permute-start(bf16[128,2048]{1,0:T(8,128)(2,1)} %refs_0_.1), channel_id=1, source_target_pairs={{0,6},{1,7},{2,0},{3,1},{4,2},{5,3},{6,4},{7,5},{8,14},{9,15},{10,... | collective-permute-start | bytes 1572872 | tf_op jit(solution)/shard_map/ppermute | solution.py:94
  6.4 23.2 %collective-permute-start.11 = (bf16[64,2048]{1,0:T(8,128)(2,1)S(1)}, bf16[64,2048]{1,0:T(8,128)(2,1)S(1)}, u32[]{:S(2)}, u32[]{:S(2)}) collective-permute-start(bf16[64,2048]{1,0:T(8,128)(2,1)S(1)} %get-tuple-element.7), channel_id=1, source_target_pairs={{0,2},{1,3},{2,4},{3,5},{4,6},{5,7},{6,0},{7,1},{8,10},{9,11},{10,... | collective-permute-start | bytes 786440 | tf_op jit(solution)/shard_map/ppermute | solution.py:94
  6.4 24.0 %collective-permute-start.7 = (s32[4,128]{1,0:T(4,128)}, s32[4,128]{1,0:T(4,128)S(1)}, u32[]{:S(2)}, u32[]{:S(2)}) collective-permute-start(s32[4,128]{1,0:T(4,128)} %bitcast.18), channel_id=1, source_target_pairs={{0,4},{1,5},{2,6},{3,7},{4,0},{5,1},{6,2},{7,3},{8,12},{9,13},{10,... | collective-permute-start | bytes 6152 | tf_op jit(solution)/shard_map/ppermute | solution.py:94
  8.9 21.9 %collective-permute-start.6 = (s32[4,128]{1,0:T(4,128)}, s32[4,128]{1,0:T(4,128)S(1)}, u32[]{:S(2)}, u32[]{:S(2)}) collective-permute-start(s32[4,128]{1,0:T(4,128)} %bitcast.19), channel_id=1, source_target_pairs={{0,2},{1,3},{2,4},{3,5},{4,6},{5,7},{6,0},{7,1},{8,10},{9,11},{10,... | collective-permute-start | bytes 6152 | tf_op jit(solution)/shard_map/ppermute | solution.py:94
  13.7 17.3 %collective-permute-start.5 = (s32[4,128]{1,0:T(4,128)}, s32[4,128]{1,0:T(4,128)S(1)}, u32[]{:S(2)}, u32[]{:S(2)}) collective-permute-start(s32[4,128]{1,0:T(4,128)} %bitcast.20), channel_id=1, source_target_pairs={{0,6},{1,7},{2,0},{3,1},{4,2},{5,3},{6,4},{7,5},{8,14},{9,15},{10,... | collective-permute-start | bytes 6152 | tf_op jit(solution)/shard_map/ppermute | solution.py:94
  29.7 3.4 %collective-permute-start.1 = (s32[4,128]{1,0:T(4,128)}, s32[4,128]{1,0:T(4,128)S(1)}, u32[]{:S(2)}, u32[]{:S(2)}) collective-permute-start(s32[4,128]{1,0:T(4,128)} %bitcast.21), channel_id=1, source_target_pairs={{0,1},{1,0},{2,3},{3,2},{4,5},{5,4},{6,7},{7,6},{8,9},{9,8},{10,11... | collective-permute-start | bytes 6152 | tf_op jit(solution)/shard_map/ppermute | solution.py:95
  30.4 4.6 %collective-permute-start = (bf16[128,2048]{1,0:T(8,128)(2,1)S(1)}, bf16[128,2048]{1,0:T(8,128)(2,1)}, u32[]{:S(2)}, u32[]{:S(2)}) collective-permute-start(bf16[128,2048]{1,0:T(8,128)(2,1)S(1)} %copy-done.4), channel_id=1, source_target_pairs={{0,1},{1,0},{2,3},{3,2},{4,5},{5,4},{6,7},{7,6},{8,9},{9,8},{10,11... | collective-permute-start | bytes 1572872 | tf_op jit(solution)/shard_map/ppermute | solution.py:95
  30.9 20.6 %collective-permute-start.12 = (bf16[128,2048]{1,0:T(8,128)(2,1)}, bf16[128,2048]{1,0:T(8,128)(2,1)}, u32[]{:S(2)}, u32[]{:S(2)}) collective-permute-start(bf16[128,2048]{1,0:T(8,128)(2,1)} %constant_dynamic-update-slice_fusion.refs_0_), channel_id=1, source_target_pairs={{0,1},{1,0},{2,3},{3,2},{4,5},{5,4},{6,7},{7,6},{8,9},{9,8},{10,11... | collective-permute-start | bytes 1572872 | tf_op jit(solution)/shard_map/ppermute | solution.py:95
  31.0 3.4 %collective-permute-start.14 = (bf16[64,2048]{1,0:T(8,128)(2,1)}, bf16[64,2048]{1,0:T(8,128)(2,1)S(1)}, u32[]{:S(2)}, u32[]{:S(2)}) collective-permute-start(bf16[64,2048]{1,0:T(8,128)(2,1)} %collective-permute-done.10), channel_id=1, source_target_pairs={{2,4},{3,5},{4,6},{5,7},{10,12},{11,13},{12,14},{13,15},{18,20},{1... | collective-permute-start | bytes 786440 | tf_op jit(solution)/shard_map/ppermute | solution.py:94
  31.7 24.4 %collective-permute-start.4 = (bf16[128,2048]{1,0:T(8,128)(2,1)S(1)}, bf16[128,2048]{1,0:T(8,128)(2,1)}, u32[]{:S(2)}, u32[]{:S(2)}) collective-permute-start(bf16[128,2048]{1,0:T(8,128)(2,1)S(1)} %collective-permute-done.3.refs_0_), channel_id=1, source_target_pairs={{0,1},{1,0},{2,3},{3,2},{4,5},{5,4},{6,7},{7,6},{8,9},{9,8},{10,11... | collective-permute-start | bytes 1572872 | tf_op jit(solution)/shard_map/ppermute | solution.py:95
  33.1 11.3 %collective-permute-start.15 = (bf16[64,2048]{1,0:T(8,128)(2,1)}, bf16[64,2048]{1,0:T(8,128)(2,1)}, u32[]{:S(2)}, u32[]{:S(2)}) collective-permute-start(bf16[64,2048]{1,0:T(8,128)(2,1)} %get-tuple-element.6), channel_id=1, source_target_pairs={{4,2},{5,3},{2,0},{3,1},{12,10},{13,11},{10,8},{11,9},{20,18},{21,... | collective-permute-start | bytes 786440 | tf_op jit(solution)/shard_map/ppermute | solution.py:94
  34.4 21.0 %collective-permute-start.18 = (bf16[64,2048]{1,0:T(8,128)(2,1)}, bf16[64,2048]{1,0:T(8,128)(2,1)S(1)}, u32[]{:S(2)}, u32[]{:S(2)}) collective-permute-start(bf16[64,2048]{1,0:T(8,128)(2,1)} %copy-done.8), channel_id=1, source_target_pairs={{2,4},{3,5},{4,6},{5,7},{10,12},{11,13},{12,14},{13,15},{18,20},{1... | collective-permute-start | bytes 786440 | tf_op jit(solution)/shard_map/ppermute | solution.py:94
  35.1 20.9 %collective-permute-start.19 = (bf16[64,2048]{1,0:T(8,128)(2,1)}, bf16[64,2048]{1,0:T(8,128)(2,1)S(1)}, u32[]{:S(2)}, u32[]{:S(2)}) collective-permute-start(bf16[64,2048]{1,0:T(8,128)(2,1)} %get-tuple-element.5), channel_id=1, source_target_pairs={{4,2},{5,3},{2,0},{3,1},{12,10},{13,11},{10,8},{11,9},{20,18},{21,... | collective-permute-start | bytes 786440 | tf_op jit(solution)/shard_map/ppermute | solution.py:94
  44.3 5.6 %collective-permute-start.8 = (s32[12,128]{1,0:T(8,128)S(1)}, s32[12,128]{1,0:T(8,128)S(1)}, u32[]{:S(2)}, u32[]{:S(2)}) collective-permute-start(s32[12,128]{1,0:T(8,128)S(1)} %pad_add_fusion.refs_2_.refs_1_), channel_id=1, source_target_pairs={{0,1},{1,0},{2,3},{3,2},{4,5},{5,4},{6,7},{7,6},{8,9},{9,8},{10,11... | collective-permute-start | bytes 18440 | tf_op jit(solution)/shard_map/ppermute | solution.py:95
  49.9 19.6 %collective-permute-start.2 = (bf16[256,512]{1,0:T(8,128)(2,1)S(1)}, bf16[256,512]{1,0:T(8,128)(2,1)}, u32[]{:S(2)}, u32[]{:S(2)}) collective-permute-start(bf16[256,512]{1,0:T(8,128)(2,1)S(1)} %hidden.6.refs_0_), channel_id=1, source_target_pairs={{0,8},{8,0},{1,9},{9,1},{2,10},{10,2},{3,11},{11,3},{4,12},{12,4},... | collective-permute-start | bytes 786440 | tf_op jit(solution)/shard_map/ppermute | solution.py:96
  51.5 9.6 %collective-permute-start.16 = (bf16[64,2048]{1,0:T(8,128)(2,1)S(1)}, bf16[64,2048]{1,0:T(8,128)(2,1)S(1)}, u32[]{:S(2)}, u32[]{:S(2)}) collective-permute-start(bf16[64,2048]{1,0:T(8,128)(2,1)S(1)} %add.6.refs_0_), channel_id=1, source_target_pairs={{0,1},{1,0},{2,3},{3,2},{4,5},{5,4},{6,7},{7,6},{8,9},{9,8},{10,11... | collective-permute-start | bytes 786440 | tf_op jit(solution)/shard_map/ppermute | solution.py:95
  55.4 14.8 %collective-permute-start.13 = (bf16[256,512]{1,0:T(8,128)(2,1)}, bf16[256,512]{1,0:T(8,128)(2,1)}, u32[]{:S(2)}, u32[]{:S(2)}) collective-permute-start(bf16[256,512]{1,0:T(8,128)(2,1)} %hidden.8.refs_4_), channel_id=1, source_target_pairs={{0,8},{8,0},{1,9},{9,1},{2,10},{10,2},{3,11},{11,3},{4,12},{12,4},... | collective-permute-start | bytes 786440 | tf_op jit(solution)/shard_map/ppermute | solution.py:96
  56.0 9.6 %collective-permute-start.21 = (bf16[64,2048]{1,0:T(8,128)(2,1)S(1)}, bf16[64,2048]{1,0:T(8,128)(2,1)}, u32[]{:S(2)}, u32[]{:S(2)}) collective-permute-start(bf16[64,2048]{1,0:T(8,128)(2,1)S(1)} %add.7.refs_0_), channel_id=1, source_target_pairs={{0,1},{1,0},{2,3},{3,2},{4,5},{5,4},{6,7},{7,6},{8,9},{9,8},{10,11... | collective-permute-start | bytes 786440 | tf_op jit(solution)/shard_map/ppermute | solution.py:95
  59.6 10.8 %collective-permute-start.9 = (bf16[256,512]{1,0:T(8,128)(2,1)}, bf16[256,512]{1,0:T(8,128)(2,1)S(1)}, u32[]{:S(2)}, u32[]{:S(2)}) collective-permute-start(bf16[256,512]{1,0:T(8,128)(2,1)} %hidden.7.refs_2_), channel_id=1, source_target_pairs={{0,8},{8,0},{1,9},{9,1},{2,10},{10,2},{3,11},{11,3},{4,12},{12,4},... | collective-permute-start | bytes 786440 | tf_op jit(solution)/shard_map/ppermute | solution.py:96
  62.3 13.3 %collective-permute-start.17 = (bf16[128,512]{1,0:T(8,128)(2,1)S(1)}, bf16[128,512]{1,0:T(8,128)(2,1)S(1)}, u32[]{:S(2)}, u32[]{:S(2)}) collective-permute-start(bf16[128,512]{1,0:T(8,128)(2,1)S(1)} %hidden.9.refs_0_), channel_id=1, source_target_pairs={{0,8},{8,0},{1,9},{9,1},{2,10},{10,2},{3,11},{11,3},{4,12},{12,4},... | collective-permute-start | bytes 393224 | tf_op jit(solution)/shard_map/ppermute | solution.py:96
  65.6 9.0 %collective-permute-start.20 = (bf16[64,512]{1,0:T(8,128)(2,1)S(1)}, bf16[64,512]{1,0:T(8,128)(2,1)S(1)}, u32[]{:S(2)}, u32[]{:S(2)}) collective-permute-start(bf16[64,512]{1,0:T(8,128)(2,1)S(1)} %hidden.10.refs_2_), channel_id=1, source_target_pairs={{0,8},{8,0},{1,9},{9,1},{2,10},{10,2},{3,11},{11,3},{4,12},{12,4},... | collective-permute-start | bytes 196616 | tf_op jit(solution)/shard_map/ppermute | solution.py:96
  69.5 6.0 %collective-permute-start.22 = (bf16[64,512]{1,0:T(8,128)(2,1)S(1)}, bf16[64,512]{1,0:T(8,128)(2,1)S(1)}, u32[]{:S(2)}, u32[]{:S(2)}) collective-permute-start(bf16[64,512]{1,0:T(8,128)(2,1)S(1)} %hidden.11.refs_4_), channel_id=1, source_target_pairs={{0,8},{8,0},{1,9},{9,1},{2,10},{10,2},{3,11},{11,3},{4,12},{12,4},... | collective-permute-start | bytes 196616 | tf_op jit(solution)/shard_map/ppermute | solution.py:96
  (8 other events, 98.7 us)

commit v4 on v2

--- a/solution.py
+++ b/solution.py
@@ -26,15 +26,12 @@
     member = jnp.concatenate(member, axis=0)
     x = jnp.concatenate([piece[...] for piece in pieces], axis=0)
 
-    def step(i, carry):
-        columns = pl.ds(pl.multiple_of(i * width, width), width)
+    for i in range(hw // width):
+        columns = slice(i * width, (i + 1) * width)
         gate = jnp.dot(x, gate_ref[:, columns], preferred_element_type=jnp.float32)
         up = jnp.dot(x, up_ref[:, columns], preferred_element_type=jnp.float32)
         value = gate / (1.0 + jnp.exp(-gate)) * up
         hidden_ref[:, columns] = jnp.where(member > 0, value, 0.0).astype(jnp.bfloat16)
-        return carry
-
-    lax.fori_loop(0, hw // width, step, 0)
 
 
 def hidden_of(me, pieces, names, at, top, gate_w, up_w):
@@ -195,11 +192,9 @@
     return jnp.dot(left.T.astype(jnp.bfloat16), right, preferred_element_type=jnp.float32)
 
 
-def outer_of_many(a, b):
-    left, right = three_parts(a.T), three_parts(b)
-    left = jnp.concatenate([left[i].astype(jnp.bfloat16) for i, _ in PRODUCTS], axis=1)
-    right = jnp.concatenate([right[j].astype(jnp.bfloat16) for _, j in PRODUCTS], axis=0)
-    return jnp.dot(left, right, preferred_element_type=jnp.float32)
+def stacked_parts(a, side, axis):
+    parts = [part.astype(jnp.bfloat16) for part in three_parts(a)]
+    return jnp.concatenate([parts[product[side]] for product in PRODUCTS], axis=axis)
 
 
 def factor_panel(rows, column, sublane):
@@ -263,9 +258,13 @@
             if after < block:
                 done = jnp.concatenate(done, axis=0)
                 rest_ref[base + after : end, base:] -= outer_of_few(done[:, :block], done)[after:, :]
+        if end < size:
+            right = stacked_parts(out_ref[base:end, end:], 1, 0)
         for to in range(end, size, block):
-            right = out_ref[base:end, to:]
-            rest_ref[to : to + block, to:] -= outer_of_many(right[:, :block], right)
+            left = stacked_parts(out_ref[base:end, to : to + block].T, 0, 1)
+            rest_ref[to : to + block, to:] -= jnp.dot(
+                left, right[:, to - end :], preferred_element_type=jnp.float32
+            )
     count = my_rows_ref.shape[0]
     my_rows_ref[...] = out_ref[pl.ds(pl.multiple_of(rank_ref[0] * count, count), count), :]
 

time: 85.6 us -> 85.4 us (level)
  Pallas kernels: 23.1 us -> 21.1 us
  waiting for transfers between devices: 36.1 us -> 37.8 us
    pallas_call x5, Pallas kernels: 8.3 us -> 6.24 us  [hidden_of(): pl.pallas_call(functools.partial(hidden_kernel, at=at, top=top), in_specs...]
    ppermute x5, waiting for transfers between devices: 10.6 us -> 12.3 us  [gathered(): lax.ppermute(x, 'dp', [(r, (r + s) % data_ranks) for r in range(data_rank...]
  transfers between devices with their start and end apart: 20 -> 20, of which waited for: 9 -> 9; matrix products, arithmetic and copies ran while one was open for 5% -> 5% of each run, Pallas kernels for 12% -> 10%
where the time goes in v4:
time: 85.4 us; the launch traced here: 85.1 us
  waiting for transfers between devices  37.8 us (44%)
  Pallas kernels  21.1 us (25%)
  starting transfers between devices  20.4 us (24%)
  local copies, waits for them, and re-layouts  4.45 us (5%)
  other arithmetic  1.18 us (1%)
    ppermute x9, waiting for transfers between devices, gathered(): move = lambda x, pairs: lax.ppermute(x, 'expert', between_chips(pairs))  25.4 us
    ppermute x9, starting transfers between devices, gathered(): move = lambda x, pairs: lax.ppermute(x, 'expert', between_chips(pairs))  12.9 us
    pallas_call x1, Pallas kernels, factor_rows(): pl.pallas_call(functools.partial(factor_kernel, rows_mean=rows_mean), in_...  12.8 us
    ppermute x5, waiting for transfers between devices, gathered(): lax.ppermute(x, 'dp', [(r, (r + s) % data_ranks) for r in range(data_rank...  12.3 us
    pallas_call x5, Pallas kernels, hidden_of(): pl.pallas_call(functools.partial(hidden_kernel, at=at, top=top), in_specs...  6.24 us
    ppermute x5, starting transfers between devices, gathered(): lax.ppermute(x, 'dp', [(r, (r + s) % data_ranks) for r in range(data_rank...  5.8 us
    pallas_call x1, Pallas kernels, partial_gram(): pl.pallas_call(gram_kernel, in_specs=[pl.BlockSpec(memory_space=pltpu.VME...  2.1 us
    slice x1, local copies, waits for them, and re-layouts, gathered(): below.append(move(tokens[i * half:(i + 1) * half], ring(1)))  1.86 us
  transfers between devices with their start and end apart: 20, of which 9 were waited for; matrix products, arithmetic and copies ran while one was open for 5% of the time, Pallas kernels for 10%

profile of v4, /device:TPU:0, one launch (start us, length us, event | category | flops | bytes accessed | tf_op | source)
XLA Modules:
  0.0 85.1 jit_solution(5366545941969850301)
XLA Ops:
  0.0 5.1 %collective-permute-start.3 = (bf16[128,2048]{1,0:T(8,128)(2,1)}, bf16[128,2048]{1,0:T(8,128)(2,1)S(1)}, u32[]{:S(2)}, u32[]{:S(2)}) collective-permute-start(bf16[128,2048]{1,0:T(8,128)(2,1)} %refs_0_.1), channel_id=1, source_target_pairs={{0,6},{1,7},{2,0},{3,1},{4,2},{5,3},{6,4},{7,5},{8,14},{9,15},{10,... | collective-permute-start | bytes 1572872 | tf_op jit(solution)/shard_map/ppermute | solution.py:91
  5.1 1.9 %fusion = (bf16[64,2048]{1,0:T(8,128)(2,1)}, bf16[64,2048]{1,0:T(8,128)(2,1)}) fusion(bf16[128,2048]{1,0:T(8,128)(2,1)} %refs_0_.1), kind=kLoop, calls=%fused_computation.4 | loop fusion | bytes 1048576 | tf_op jit(solution)/shard_map/slice | solution.py:101
  7.3 10.5 %collective-permute-done.3.refs_0_ = bf16[128,2048]{1,0:T(8,128)(2,1)S(1)} collective-permute-done((bf16[128,2048]{1,0:T(8,128)(2,1)}, bf16[128,2048]{1,0:T(8,128)(2,1)S(1)}, u32[]{:S(2)}, u32[]{:S(2)}) %collective-permute-start.3) | collective-permute-done | bytes 524320 | tf_op jit(solution)/shard_map/ppermute | solution.py:91
  17.8 1.3 %collective-permute-start.16 = (bf16[128,2048]{1,0:T(8,128)(2,1)S(1)}, bf16[128,2048]{1,0:T(8,128)(2,1)}, u32[]{:S(2)}, u32[]{:S(2)}) collective-permute-start(bf16[128,2048]{1,0:T(8,128)(2,1)S(1)} %collective-permute-done.3.refs_0_), channel_id=1, source_target_pairs={{4,2},{5,3},{2,0},{3,1},{12,10},{13,11},{10,8},{11,9},{20,18},{21,... | collective-permute-start | bytes 1572872 | tf_op jit(solution)/shard_map/ppermute | solution.py:91
  19.1 2.2 %collective-permute-start.7 = (s32[4,128]{1,0:T(4,128)}, s32[4,128]{1,0:T(4,128)S(1)}, u32[]{:S(2)}, u32[]{:S(2)}) collective-permute-start(s32[4,128]{1,0:T(4,128)} %bitcast.16), channel_id=1, source_target_pairs={{0,4},{1,5},{2,6},{3,7},{4,0},{5,1},{6,2},{7,3},{8,12},{9,13},{10,... | collective-permute-start | bytes 6152 | tf_op jit(solution)/shard_map/ppermute | solution.py:91
  21.3 2.7 %collective-permute-start.6 = (s32[4,128]{1,0:T(4,128)}, s32[4,128]{1,0:T(4,128)S(1)}, u32[]{:S(2)}, u32[]{:S(2)}) collective-permute-start(s32[4,128]{1,0:T(4,128)} %bitcast.17), channel_id=1, source_target_pairs={{0,2},{1,3},{2,4},{3,5},{4,6},{5,7},{6,0},{7,1},{8,10},{9,11},{10,... | collective-permute-start | bytes 6152 | tf_op jit(solution)/shard_map/ppermute | solution.py:91
  25.1 3.7 %collective-permute-done.10 = bf16[64,2048]{1,0:T(8,128)(2,1)S(1)} collective-permute-done((bf16[64,2048]{1,0:T(8,128)(2,1)}, bf16[64,2048]{1,0:T(8,128)(2,1)S(1)}, u32[]{:S(2)}, u32[]{:S(2)}) %collective-permute-start.10) | collective-permute-done | bytes 262176 | tf_op jit(solution)/shard_map/ppermute | solution.py:91
  29.5 1.0 %constant_dynamic-update-slice_fusion.refs_0_ = bf16[128,2048]{1,0:T(8,128)(2,1)S(1)} fusion(bf16[128,2048]{1,0:T(8,128)(2,1)S(1)} %constant_dynamic-update-slice_fusion.1, bf16[64,2048]{1,0:T(8,128)(2,1)} %collective-permute-done.11), kind=kLoop, calls=%fused_computation.2 | loop fusion | bytes 524288 | tf_op jit(solution)/shard_map/concatenate | solution.py:105
  30.5 9.6 %collective-permute-done.7 = s32[4,128]{1,0:T(4,128)S(1)} collective-permute-done((s32[4,128]{1,0:T(4,128)}, s32[4,128]{1,0:T(4,128)S(1)}, u32[]{:S(2)}, u32[]{:S(2)}) %collective-permute-start.7) | collective-permute-done | bytes 2080 | tf_op jit(solution)/shard_map/ppermute | solution.py:91
  40.7 1.2 %maximum_add_fusion.refs_0_ = bf16[128,2048]{1,0:T(8,128)(2,1)S(1)} fusion(bf16[128,2048]{1,0:T(8,128)(2,1)} %collective-permute-done.16, bf16[64,2048]{1,0:T(8,128)(2,1)S(1)} %collective-permute-done.15, bf16[64,2048]{1,0:T(8,128)(2,1)S(1)} %collective-permute-done.14), kind=kLoop, calls=%fused_computation | loop fusion | flops 1572864 | bytes 1572864 | tf_op jit(solution)/shard_map/add | solution.py:121
  42.4 1.2 %collective-permute-done.5 = s32[4,128]{1,0:T(4,128)S(1)} collective-permute-done((s32[4,128]{1,0:T(4,128)S(1)}, s32[4,128]{1,0:T(4,128)S(1)}, u32[]{:S(2)}, u32[]{:S(2)}) %collective-permute-start.5) | collective-permute-done | bytes 2080 | tf_op jit(solution)/shard_map/ppermute | solution.py:91
  44.2 1.6 %copy-done.1 = bf16[1,2048,512]{2,1,0:T(8,128)(2,1)S(1)} copy-done((bf16[1,2048,512]{2,1,0:T(8,128)(2,1)S(1)}, bf16[1,2048,512]{2,1,0:T(8,128)(2,1)}, u32[]{:S(2)}) %copy-start.1) | copy-done | bytes 2097176
  45.8 1.3 %hidden.5.refs_0_ = bf16[256,512]{1,0:T(8,128)(2,1)S(1)} custom-call(s32[1]{0:T(128)} %bitcast.1.me_ref, bf16[2048,512]{1,0:T(8,128)(2,1)S(1)} %bitcast.6, bf16[2048,512]{1,0:T(8,128)(2,1)S(1)} %bitcast.11, bf16[128,2048]{1,0:T(8,128)(2,1)S(1)} %copy-done.2, bf16[128,2048]{1,0:T(8,128)(2,1)S(1)} %collective-permute-done.refs_1_, s32[4,128]{1,0:T(4,128)S(1)} %bitcast.20, ...), custom_call_target="tpu_custom_call" | custom-call | flops 1073741824 | bytes 5505024 | tf_op jit(solution)/shard_map/hidden/pallas_call | solution.py:40
  47.2 1.6 %collective-permute-start.2 = (bf16[256,512]{1,0:T(8,128)(2,1)S(1)}, bf16[256,512]{1,0:T(8,128)(2,1)}, u32[]{:S(2)}, u32[]{:S(2)}) collective-permute-start(bf16[256,512]{1,0:T(8,128)(2,1)S(1)} %hidden.5.refs_0_), channel_id=1, source_target_pairs={{0,8},{8,0},{1,9},{9,1},{2,10},{10,2},{3,11},{11,3},{4,12},{12,4},... | collective-permute-start | bytes 786440 | tf_op jit(solution)/shard_map/ppermute | solution.py:93
  48.7 1.4 %hidden.7.refs_4_ = bf16[256,512]{1,0:T(8,128)(2,1)S(1)} custom-call(s32[1]{0:T(128)} %bitcast.1.me_ref, bf16[2048,512]{1,0:T(8,128)(2,1)S(1)} %bitcast.7, bf16[2048,512]{1,0:T(8,128)(2,1)S(1)} %bitcast.12, bf16[128,2048]{1,0:T(8,128)(2,1)S(1)} %constant_dynamic-update-slice_fusion.refs_0_, bf16[128,2048]{1,0:T(8,128)(2,1)S(1)} %collective-permute-done.12.refs_1_, ...), custom_call_target="tpu_custom_call" | custom-call | flops 1073741824 | bytes 5505024 | tf_op jit(solution)/shard_map/hidden/pallas_call | solution.py:40
  50.7 2.1 %hidden.6.refs_2_ = bf16[256,512]{1,0:T(8,128)(2,1)} custom-call(s32[1]{0:T(128)} %bitcast.1.me_ref, bf16[2048,512]{1,0:T(8,128)(2,1)S(1)} %bitcast.8, bf16[2048,512]{1,0:T(8,128)(2,1)S(1)} %bitcast.13, bf16[128,2048]{1,0:T(8,128)(2,1)S(1)} %collective-permute-done.3.refs_0_, bf16[128,2048]{1,0:T(8,128)(2,1)S(1)} %collective-permute-done.4.refs_1_, ...), custom_call_target="tpu_custom_call" | custom-call | flops 1073741824 | bytes 5505024 | tf_op jit(solution)/shard_map/hidden/pallas_call | solution.py:40
  52.7 1.5 %collective-permute-start.9 = (bf16[256,512]{1,0:T(8,128)(2,1)}, bf16[256,512]{1,0:T(8,128)(2,1)S(1)}, u32[]{:S(2)}, u32[]{:S(2)}) collective-permute-start(bf16[256,512]{1,0:T(8,128)(2,1)} %hidden.6.refs_2_), channel_id=1, source_target_pairs={{0,8},{8,0},{1,9},{9,1},{2,10},{10,2},{3,11},{11,3},{4,12},{12,4},... | collective-permute-start | bytes 786440 | tf_op jit(solution)/shard_map/ppermute | solution.py:93
  55.6 0.8 hidden.9.refs_2_
  56.4 1.6 %collective-permute-start.19 = (bf16[128,512]{1,0:T(8,128)(2,1)S(1)}, bf16[128,512]{1,0:T(8,128)(2,1)S(1)}, u32[]{:S(2)}, u32[]{:S(2)}) collective-permute-start(bf16[128,512]{1,0:T(8,128)(2,1)S(1)} %hidden.9.refs_2_), channel_id=1, source_target_pairs={{0,8},{8,0},{1,9},{9,1},{2,10},{10,2},{3,11},{11,3},{4,12},{12,4},... | collective-permute-start | bytes 393224 | tf_op jit(solution)/shard_map/ppermute | solution.py:93
  57.9 4.2 %collective-permute-done.13.refs_5_ = bf16[256,512]{1,0:T(8,128)(2,1)} collective-permute-done((bf16[256,512]{1,0:T(8,128)(2,1)S(1)}, bf16[256,512]{1,0:T(8,128)(2,1)}, u32[]{:S(2)}, u32[]{:S(2)}) %collective-permute-start.13) | collective-permute-done | bytes 262176 | tf_op jit(solution)/shard_map/ppermute | solution.py:93
  62.1 5.5 %collective-permute-done.9.refs_3_ = bf16[256,512]{1,0:T(8,128)(2,1)S(1)} collective-permute-done((bf16[256,512]{1,0:T(8,128)(2,1)}, bf16[256,512]{1,0:T(8,128)(2,1)S(1)}, u32[]{:S(2)}, u32[]{:S(2)}) %collective-permute-start.9) | collective-permute-done | bytes 262176 | tf_op jit(solution)/shard_map/ppermute | solution.py:93
  67.6 2.1 %partial_gram.1.early_ref = f32[512,512]{1,0:T(8,128)S(1)} custom-call(bf16[256,512]{1,0:T(8,128)(2,1)S(1)} %hidden.5.refs_0_, bf16[256,512]{1,0:T(8,128)(2,1)} %collective-permute-done.2.refs_1_, bf16[256,512]{1,0:T(8,128)(2,1)} %hidden.6.refs_2_, bf16[256,512]{1,0:T(8,128)(2,1)S(1)} %collective-permute-done.9.refs_3_, bf16[256,512]{1,0:T(8,128)(2,1)S(1)} %hidden.7.refs_4_, ...), custom_call_target="tpu_custom_call" | custom-call | flops 805306368 | bytes 2621440 | tf_op jit(solution)/shard_map/partial_gram/pallas_call | solution.py:68
  70.5 1.9 %collective-permute-done.19.refs_3_ = bf16[128,512]{1,0:T(8,128)(2,1)S(1)} collective-permute-done((bf16[128,512]{1,0:T(8,128)(2,1)S(1)}, bf16[128,512]{1,0:T(8,128)(2,1)S(1)}, u32[]{:S(2)}, u32[]{:S(2)}) %collective-permute-start.19) | collective-permute-done | bytes 131104 | tf_op jit(solution)/shard_map/ppermute | solution.py:93
  72.3 12.8 %factor.1 = f32[256,512]{1,0:T(8,128)} custom-call(s32[1]{0:T(128)} %bitcast.rank_ref, f32[512,512]{1,0:T(8,128)S(1)} %partial_gram.1.early_ref, bf16[128,512]{1,0:T(8,128)(2,1)S(1)} %hidden.8.refs_0_, bf16[128,512]{1,0:T(8,128)(2,1)S(1)} %collective-permute-done.17.refs_1_, bf16[128,512]{1,0:T(8,128)(2,1)S(1)} %hidden.9.refs_2_, ...), custom_call_target="tpu_custom_call" | custom-call | tf_op jit(solution)/shard_map/factor/pallas_call | solution.py:275
  (36 shorter events, 6.4 us)
Async XLA Ops:
  0.0 40.1 %copy-start.2 = (bf16[128,2048]{1,0:T(8,128)(2,1)S(1)}, bf16[128,2048]{1,0:T(8,128)(2,1)}, u32[]{:S(2)}) copy-start(bf16[128,2048]{1,0:T(8,128)(2,1)} %refs_0_.1) | copy-start | bytes 1572868
  0.0 40.0 %copy-start.3 = (s32[128,4]{0,1:T(4,128)S(1)}, s32[128,4]{0,1:T(4,128)}, u32[]{:S(2)}) copy-start(s32[128,4]{0,1:T(4,128)} %param.5) | copy-start | bytes 6148
  0.0 44.2 %copy-start = (bf16[1,2048,512]{2,1,0:T(8,128)(2,1)S(1)}, bf16[1,2048,512]{2,1,0:T(8,128)(2,1)}, u32[]{:S(2)}) copy-start(bf16[1,2048,512]{2,1,0:T(8,128)(2,1)} %param.6) | copy-start | bytes 6291460
  0.0 17.8 %collective-permute-start.3 = (bf16[128,2048]{1,0:T(8,128)(2,1)}, bf16[128,2048]{1,0:T(8,128)(2,1)S(1)}, u32[]{:S(2)}, u32[]{:S(2)}) collective-permute-start(bf16[128,2048]{1,0:T(8,128)(2,1)} %refs_0_.1), channel_id=1, source_target_pairs={{0,6},{1,7},{2,0},{3,1},{4,2},{5,3},{6,4},{7,5},{8,14},{9,15},{10,... | collective-permute-start | bytes 1572872 | tf_op jit(solution)/shard_map/ppermute | solution.py:91
  7.0 17.4 %collective-permute-start.11 = (bf16[64,2048]{1,0:T(8,128)(2,1)}, bf16[64,2048]{1,0:T(8,128)(2,1)}, u32[]{:S(2)}, u32[]{:S(2)}) collective-permute-start(bf16[64,2048]{1,0:T(8,128)(2,1)} %get-tuple-element.5), channel_id=1, source_target_pairs={{0,2},{1,3},{2,4},{3,5},{4,6},{5,7},{6,0},{7,1},{8,10},{9,11},{10,... | collective-permute-start | bytes 786440 | tf_op jit(solution)/shard_map/ppermute | solution.py:91
  7.0 21.8 %collective-permute-start.10 = (bf16[64,2048]{1,0:T(8,128)(2,1)}, bf16[64,2048]{1,0:T(8,128)(2,1)S(1)}, u32[]{:S(2)}, u32[]{:S(2)}) collective-permute-start(bf16[64,2048]{1,0:T(8,128)(2,1)} %get-tuple-element.6), channel_id=1, source_target_pairs={{0,2},{1,3},{2,4},{3,5},{4,6},{5,7},{6,0},{7,1},{8,10},{9,11},{10,... | collective-permute-start | bytes 786440 | tf_op jit(solution)/shard_map/ppermute | solution.py:91
  17.8 22.8 %collective-permute-start.16 = (bf16[128,2048]{1,0:T(8,128)(2,1)S(1)}, bf16[128,2048]{1,0:T(8,128)(2,1)}, u32[]{:S(2)}, u32[]{:S(2)}) collective-permute-start(bf16[128,2048]{1,0:T(8,128)(2,1)S(1)} %collective-permute-done.3.refs_0_), channel_id=1, source_target_pairs={{4,2},{5,3},{2,0},{3,1},{12,10},{13,11},{10,8},{11,9},{20,18},{21,... | collective-permute-start | bytes 1572872 | tf_op jit(solution)/shard_map/ppermute | solution.py:91
  19.1 20.9 %collective-permute-start.7 = (s32[4,128]{1,0:T(4,128)}, s32[4,128]{1,0:T(4,128)S(1)}, u32[]{:S(2)}, u32[]{:S(2)}) collective-permute-start(s32[4,128]{1,0:T(4,128)} %bitcast.16), channel_id=1, source_target_pairs={{0,4},{1,5},{2,6},{3,7},{4,0},{5,1},{6,2},{7,3},{8,12},{9,13},{10,... | collective-permute-start | bytes 6152 | tf_op jit(solution)/shard_map/ppermute | solution.py:91
  21.3 20.6 %collective-permute-start.6 = (s32[4,128]{1,0:T(4,128)}, s32[4,128]{1,0:T(4,128)S(1)}, u32[]{:S(2)}, u32[]{:S(2)}) collective-permute-start(s32[4,128]{1,0:T(4,128)} %bitcast.17), channel_id=1, source_target_pairs={{0,2},{1,3},{2,4},{3,5},{4,6},{5,7},{6,0},{7,1},{8,10},{9,11},{10,... | collective-permute-start | bytes 6152 | tf_op jit(solution)/shard_map/ppermute | solution.py:91
  24.4 15.6 %collective-permute-start.15 = (bf16[64,2048]{1,0:T(8,128)(2,1)}, bf16[64,2048]{1,0:T(8,128)(2,1)S(1)}, u32[]{:S(2)}, u32[]{:S(2)}) collective-permute-start(bf16[64,2048]{1,0:T(8,128)(2,1)} %collective-permute-done.11), channel_id=1, source_target_pairs={{2,4},{3,5},{4,6},{5,7},{10,12},{11,13},{12,14},{13,15},{18,20},{1... | collective-permute-start | bytes 786440 | tf_op jit(solution)/shard_map/ppermute | solution.py:91
  28.8 11.3 %collective-permute-start.14 = (bf16[64,2048]{1,0:T(8,128)(2,1)S(1)}, bf16[64,2048]{1,0:T(8,128)(2,1)S(1)}, u32[]{:S(2)}, u32[]{:S(2)}) collective-permute-start(bf16[64,2048]{1,0:T(8,128)(2,1)S(1)} %collective-permute-done.10), channel_id=1, source_target_pairs={{2,4},{3,5},{4,6},{5,7},{10,12},{11,13},{12,14},{13,15},{18,20},{1... | collective-permute-start | bytes 786440 | tf_op jit(solution)/shard_map/ppermute | solution.py:91
  40.0 3.6 %collective-permute-start.5 = (s32[4,128]{1,0:T(4,128)S(1)}, s32[4,128]{1,0:T(4,128)S(1)}, u32[]{:S(2)}, u32[]{:S(2)}) collective-permute-start(s32[4,128]{1,0:T(4,128)S(1)} %bitcast.18), channel_id=1, source_target_pairs={{0,6},{1,7},{2,0},{3,1},{4,2},{5,3},{6,4},{7,5},{8,14},{9,15},{10,... | collective-permute-start | bytes 6152 | tf_op jit(solution)/shard_map/ppermute | solution.py:91
  40.1 4.2 %collective-permute-start = (bf16[128,2048]{1,0:T(8,128)(2,1)S(1)}, bf16[128,2048]{1,0:T(8,128)(2,1)S(1)}, u32[]{:S(2)}, u32[]{:S(2)}) collective-permute-start(bf16[128,2048]{1,0:T(8,128)(2,1)S(1)} %copy-done.2), channel_id=1, source_target_pairs={{0,1},{1,0},{2,3},{3,2},{4,5},{5,4},{6,7},{7,6},{8,9},{9,8},{10,11... | collective-permute-start | bytes 1572872 | tf_op jit(solution)/shard_map/ppermute | solution.py:92
  40.2 8.6 %collective-permute-start.12 = (bf16[128,2048]{1,0:T(8,128)(2,1)S(1)}, bf16[128,2048]{1,0:T(8,128)(2,1)S(1)}, u32[]{:S(2)}, u32[]{:S(2)}) collective-permute-start(bf16[128,2048]{1,0:T(8,128)(2,1)S(1)} %constant_dynamic-update-slice_fusion.refs_0_), channel_id=1, source_target_pairs={{0,1},{1,0},{2,3},{3,2},{4,5},{5,4},{6,7},{7,6},{8,9},{9,8},{10,11... | collective-permute-start | bytes 1572872 | tf_op jit(solution)/shard_map/ppermute | solution.py:92
  40.6 10.0 %collective-permute-start.4 = (bf16[128,2048]{1,0:T(8,128)(2,1)S(1)}, bf16[128,2048]{1,0:T(8,128)(2,1)S(1)}, u32[]{:S(2)}, u32[]{:S(2)}) collective-permute-start(bf16[128,2048]{1,0:T(8,128)(2,1)S(1)} %collective-permute-done.3.refs_0_), channel_id=1, source_target_pairs={{0,1},{1,0},{2,3},{3,2},{4,5},{5,4},{6,7},{7,6},{8,9},{9,8},{10,11... | collective-permute-start | bytes 1572872 | tf_op jit(solution)/shard_map/ppermute | solution.py:92
  41.9 1.7 %collective-permute-start.1 = (s32[4,128]{1,0:T(4,128)S(1)}, s32[4,128]{1,0:T(4,128)S(1)}, u32[]{:S(2)}, u32[]{:S(2)}) collective-permute-start(s32[4,128]{1,0:T(4,128)S(1)} %bitcast.19), channel_id=1, source_target_pairs={{0,1},{1,0},{2,3},{3,2},{4,5},{5,4},{6,7},{7,6},{8,9},{9,8},{10,11... | collective-permute-start | bytes 6152 | tf_op jit(solution)/shard_map/ppermute | solution.py:92
  43.6 12.0 %collective-permute-start.18 = (bf16[128,2048]{1,0:T(8,128)(2,1)S(1)}, bf16[128,2048]{1,0:T(8,128)(2,1)S(1)}, u32[]{:S(2)}, u32[]{:S(2)}) collective-permute-start(bf16[128,2048]{1,0:T(8,128)(2,1)S(1)} %maximum_add_fusion.refs_0_), channel_id=1, source_target_pairs={{0,1},{1,0},{2,3},{3,2},{4,5},{5,4},{6,7},{7,6},{8,9},{9,8},{10,11... | collective-permute-start | bytes 1572872 | tf_op jit(solution)/shard_map/ppermute | solution.py:92
  43.7 5.1 %collective-permute-start.8 = (s32[12,128]{1,0:T(8,128)S(1)}, s32[12,128]{1,0:T(8,128)S(1)}, u32[]{:S(2)}, u32[]{:S(2)}) collective-permute-start(s32[12,128]{1,0:T(8,128)S(1)} %pad_add_fusion.refs_2_.refs_1_), channel_id=1, source_target_pairs={{0,1},{1,0},{2,3},{3,2},{4,5},{5,4},{6,7},{7,6},{8,9},{9,8},{10,11... | collective-permute-start | bytes 18440 | tf_op jit(solution)/shard_map/ppermute | solution.py:92
  44.2 1.6 %copy-start.1 = (bf16[1,2048,512]{2,1,0:T(8,128)(2,1)S(1)}, bf16[1,2048,512]{2,1,0:T(8,128)(2,1)}, u32[]{:S(2)}) copy-start(bf16[1,2048,512]{2,1,0:T(8,128)(2,1)} %param.7) | copy-start | bytes 6291460
  47.2 10.7 %collective-permute-start.2 = (bf16[256,512]{1,0:T(8,128)(2,1)S(1)}, bf16[256,512]{1,0:T(8,128)(2,1)}, u32[]{:S(2)}, u32[]{:S(2)}) collective-permute-start(bf16[256,512]{1,0:T(8,128)(2,1)S(1)} %hidden.5.refs_0_), channel_id=1, source_target_pairs={{0,8},{8,0},{1,9},{9,1},{2,10},{10,2},{3,11},{11,3},{4,12},{12,4},... | collective-permute-start | bytes 786440 | tf_op jit(solution)/shard_map/ppermute | solution.py:93
  50.1 12.0 %collective-permute-start.13 = (bf16[256,512]{1,0:T(8,128)(2,1)S(1)}, bf16[256,512]{1,0:T(8,128)(2,1)}, u32[]{:S(2)}, u32[]{:S(2)}) collective-permute-start(bf16[256,512]{1,0:T(8,128)(2,1)S(1)} %hidden.7.refs_4_), channel_id=1, source_target_pairs={{0,8},{8,0},{1,9},{9,1},{2,10},{10,2},{3,11},{11,3},{4,12},{12,4},... | collective-permute-start | bytes 786440 | tf_op jit(solution)/shard_map/ppermute | solution.py:93
  52.7 14.9 %collective-permute-start.9 = (bf16[256,512]{1,0:T(8,128)(2,1)}, bf16[256,512]{1,0:T(8,128)(2,1)S(1)}, u32[]{:S(2)}, u32[]{:S(2)}) collective-permute-start(bf16[256,512]{1,0:T(8,128)(2,1)} %hidden.6.refs_2_), channel_id=1, source_target_pairs={{0,8},{8,0},{1,9},{9,1},{2,10},{10,2},{3,11},{11,3},{4,12},{12,4},... | collective-permute-start | bytes 786440 | tf_op jit(solution)/shard_map/ppermute | solution.py:93
  55.0 15.5 %collective-permute-start.17 = (bf16[128,512]{1,0:T(8,128)(2,1)S(1)}, bf16[128,512]{1,0:T(8,128)(2,1)S(1)}, u32[]{:S(2)}, u32[]{:S(2)}) collective-permute-start(bf16[128,512]{1,0:T(8,128)(2,1)S(1)} %hidden.8.refs_0_), channel_id=1, source_target_pairs={{0,8},{8,0},{1,9},{9,1},{2,10},{10,2},{3,11},{11,3},{4,12},{12,4},... | collective-permute-start | bytes 393224 | tf_op jit(solution)/shard_map/ppermute | solution.py:93
  56.4 16.0 %collective-permute-start.19 = (bf16[128,512]{1,0:T(8,128)(2,1)S(1)}, bf16[128,512]{1,0:T(8,128)(2,1)S(1)}, u32[]{:S(2)}, u32[]{:S(2)}) collective-permute-start(bf16[128,512]{1,0:T(8,128)(2,1)S(1)} %hidden.9.refs_2_), channel_id=1, source_target_pairs={{0,8},{8,0},{1,9},{9,1},{2,10},{10,2},{3,11},{11,3},{4,12},{12,4},... | collective-permute-start | bytes 393224 | tf_op jit(solution)/shard_map/ppermute | solution.py:93

commit v5 on v4

--- a/solution.py
+++ b/solution.py
@@ -58,16 +58,17 @@
     return lax.dot_general(h, h, (((0,), (0,)), ((), ())), preferred_element_type=jnp.float32)
 
 
-def gram_kernel(*refs):
-    refs[-1][...] = gram_of(refs[:-1])
-
-
-def partial_gram(hiddens):
+def gram_kernel(*refs, count):
+    gram = gram_of(refs[:count])
+    refs[-1][...] = gram if len(refs) == count + 1 else refs[count][...] + gram
+
+
+def partial_gram(hiddens, *total):
     rows = sum(hidden.shape[0] for hidden in hiddens)
     hw = hiddens[0].shape[1]
     return pl.pallas_call(
-        gram_kernel,
-        in_specs=[pl.BlockSpec(memory_space=pltpu.VMEM)] * len(hiddens),
+        functools.partial(gram_kernel, count=len(hiddens)),
+        in_specs=[pl.BlockSpec(memory_space=pltpu.VMEM)] * (len(hiddens) + len(total)),
         out_specs=pl.BlockSpec(memory_space=pltpu.VMEM),
         out_shape=jax.ShapeDtypeStruct((hw, hw), jnp.float32),
         compiler_params=pltpu.CompilerParams(vmem_limit_bytes=24 << 20),
@@ -77,7 +78,7 @@
             transcendentals=0,
         ),
         name="partial_gram",
-    )(*hiddens)
+    )(*hiddens, *total)
 
 
 def between_chips(pairs):
@@ -123,8 +124,9 @@
     late = []
     for piece, who in ((last, moved), (other, other_moved)):
         hidden = hidden_of(me, (piece,), (who,), 2, top, gate_w, up_w)
-        late += [hidden] + [turn(hidden, s) for s in range(1, data_ranks)]
-    return early, late
+        late.append([hidden] + [turn(hidden, s) for s in range(1, data_ranks)])
+    early = partial_gram(late[0] + late[1][:1], early)
+    return early, late[1][1:]
 
 
 def packed_grams(tokens, routes, gate_w, up_w, capacity):
@@ -234,12 +236,17 @@
     size = early_ref.shape[0]
     block, group, groups = 128, 8, 4
     panel = group * groups
-    row = lax.broadcasted_iota(jnp.int32, (size, size), 0)
-    col = lax.broadcasted_iota(jnp.int32, (size, size), 1)
-    gram = early_ref[...]
-    if late_refs:
-        gram = gram + gram_of(late_refs)
-    rest_ref[...] = gram / rows_mean + jnp.where(row == col, RIDGE, 0.0)
+    late = jnp.concatenate([ref[...] for ref in late_refs], axis=0) if late_refs else None
+    for base in range(0, size, block):
+        corner = slice(base, base + block)
+        gram = early_ref[corner, base:]
+        if late is not None:
+            gram = gram + lax.dot_general(
+                late[:, corner], late[:, base:], (((0,), (0,)), ((), ())), preferred_element_type=jnp.float32
+            )
+        row = lax.broadcasted_iota(jnp.int32, gram.shape, 0)
+        col = lax.broadcasted_iota(jnp.int32, gram.shape, 1)
+        rest_ref[corner, base:] = gram / rows_mean + jnp.where(row == col, RIDGE, 0.0)
     for base in range(0, size, block):
         width = size - base
         end = base + block

time: 85.4 us -> 85.2 us (level)
    pallas_call x1 -> x2, Pallas kernels: 2.1 us -> 2.56 us  [partial_gram(): pl.pallas_call(functools.partial(gram_kernel, count=len(hiddens)), in_spe...]
where the time goes in v5:
time: 85.2 us; the launch traced here: 84.9 us
  waiting for transfers between devices  37.3 us (44%)
  Pallas kernels  21.4 us (25%)
  starting transfers between devices  20.4 us (24%)
  local copies, waits for them, and re-layouts  4.45 us (5%)
  other arithmetic  1.18 us (1%)
    ppermute x9, waiting for transfers between devices, gathered(): move = lambda x, pairs: lax.ppermute(x, 'expert', between_chips(pairs))  25.4 us
    ppermute x9, starting transfers between devices, gathered(): move = lambda x, pairs: lax.ppermute(x, 'expert', between_chips(pairs))  12.9 us
    pallas_call x1, Pallas kernels, factor_rows(): pl.pallas_call(functools.partial(factor_kernel, rows_mean=rows_mean), in_...  12.6 us
    ppermute x5, waiting for transfers between devices, gathered(): lax.ppermute(x, 'dp', [(r, (r + s) % data_ranks) for r in range(data_rank...  11.8 us
    pallas_call x5, Pallas kernels, hidden_of(): pl.pallas_call(functools.partial(hidden_kernel, at=at, top=top), in_specs...  6.24 us
    ppermute x5, starting transfers between devices, gathered(): lax.ppermute(x, 'dp', [(r, (r + s) % data_ranks) for r in range(data_rank...  5.8 us
    pallas_call x2, Pallas kernels, partial_gram(): pl.pallas_call(functools.partial(gram_kernel, count=len(hiddens)), in_spe...  2.56 us
    slice x1, local copies, waits for them, and re-layouts, gathered(): below.append(move(tokens[i * half:(i + 1) * half], ring(1)))  1.86 us
  transfers between devices with their start and end apart: 20, of which 9 were waited for; matrix products, arithmetic and copies ran while one was open for 5% of the time, Pallas kernels for 10%

profile of v5, /device:TPU:0, one launch (start us, length us, event | category | flops | bytes accessed | tf_op | source)
XLA Modules:
  0.0 84.9 jit_solution(1695304312650262653)
XLA Ops:
  0.0 5.1 %collective-permute-start.4 = (bf16[128,2048]{1,0:T(8,128)(2,1)}, bf16[128,2048]{1,0:T(8,128)(2,1)S(1)}, u32[]{:S(2)}, u32[]{:S(2)}) collective-permute-start(bf16[128,2048]{1,0:T(8,128)(2,1)} %refs_0_.1), channel_id=1, source_target_pairs={{0,6},{1,7},{2,0},{3,1},{4,2},{5,3},{6,4},{7,5},{8,14},{9,15},{10,... | collective-permute-start | bytes 1572872 | tf_op jit(solution)/shard_map/ppermute | solution.py:92
  5.1 1.9 %fusion = (bf16[64,2048]{1,0:T(8,128)(2,1)}, bf16[64,2048]{1,0:T(8,128)(2,1)}) fusion(bf16[128,2048]{1,0:T(8,128)(2,1)} %refs_0_.1), kind=kLoop, calls=%fused_computation.4 | loop fusion | bytes 1048576 | tf_op jit(solution)/shard_map/slice | solution.py:102
  7.3 10.5 %collective-permute-done.4.refs_0_ = bf16[128,2048]{1,0:T(8,128)(2,1)S(1)} collective-permute-done((bf16[128,2048]{1,0:T(8,128)(2,1)}, bf16[128,2048]{1,0:T(8,128)(2,1)S(1)}, u32[]{:S(2)}, u32[]{:S(2)}) %collective-permute-start.4) | collective-permute-done | bytes 524320 | tf_op jit(solution)/shard_map/ppermute | solution.py:92
  17.8 1.3 %collective-permute-start.5 = (bf16[128,2048]{1,0:T(8,128)(2,1)S(1)}, bf16[128,2048]{1,0:T(8,128)(2,1)}, u32[]{:S(2)}, u32[]{:S(2)}) collective-permute-start(bf16[128,2048]{1,0:T(8,128)(2,1)S(1)} %collective-permute-done.4.refs_0_), channel_id=1, source_target_pairs={{4,2},{5,3},{2,0},{3,1},{12,10},{13,11},{10,8},{11,9},{20,18},{21,... | collective-permute-start | bytes 1572872 | tf_op jit(solution)/shard_map/ppermute | solution.py:92
  19.1 2.2 %collective-permute-start.8 = (s32[4,128]{1,0:T(4,128)}, s32[4,128]{1,0:T(4,128)S(1)}, u32[]{:S(2)}, u32[]{:S(2)}) collective-permute-start(s32[4,128]{1,0:T(4,128)} %bitcast.16), channel_id=1, source_target_pairs={{0,4},{1,5},{2,6},{3,7},{4,0},{5,1},{6,2},{7,3},{8,12},{9,13},{10,... | collective-permute-start | bytes 6152 | tf_op jit(solution)/shard_map/ppermute | solution.py:92
  21.3 2.7 %collective-permute-start.7 = (s32[4,128]{1,0:T(4,128)}, s32[4,128]{1,0:T(4,128)S(1)}, u32[]{:S(2)}, u32[]{:S(2)}) collective-permute-start(s32[4,128]{1,0:T(4,128)} %bitcast.17), channel_id=1, source_target_pairs={{0,2},{1,3},{2,4},{3,5},{4,6},{5,7},{6,0},{7,1},{8,10},{9,11},{10,... | collective-permute-start | bytes 6152 | tf_op jit(solution)/shard_map/ppermute | solution.py:92
  25.1 3.7 %collective-permute-done = bf16[64,2048]{1,0:T(8,128)(2,1)S(1)} collective-permute-done((bf16[64,2048]{1,0:T(8,128)(2,1)}, bf16[64,2048]{1,0:T(8,128)(2,1)S(1)}, u32[]{:S(2)}, u32[]{:S(2)}) %collective-permute-start) | collective-permute-done | bytes 262176 | tf_op jit(solution)/shard_map/ppermute | solution.py:92
  29.5 1.0 %constant_dynamic-update-slice_fusion.refs_0_ = bf16[128,2048]{1,0:T(8,128)(2,1)S(1)} fusion(bf16[128,2048]{1,0:T(8,128)(2,1)S(1)} %constant_dynamic-update-slice_fusion.1, bf16[64,2048]{1,0:T(8,128)(2,1)} %collective-permute-done.2), kind=kLoop, calls=%fused_computation.2 | loop fusion | bytes 524288 | tf_op jit(solution)/shard_map/concatenate | solution.py:106
  30.5 9.6 %collective-permute-done.8 = s32[4,128]{1,0:T(4,128)S(1)} collective-permute-done((s32[4,128]{1,0:T(4,128)}, s32[4,128]{1,0:T(4,128)S(1)}, u32[]{:S(2)}, u32[]{:S(2)}) %collective-permute-start.8) | collective-permute-done | bytes 2080 | tf_op jit(solution)/shard_map/ppermute | solution.py:92
  40.7 1.2 %maximum_add_fusion.refs_0_ = bf16[128,2048]{1,0:T(8,128)(2,1)S(1)} fusion(bf16[128,2048]{1,0:T(8,128)(2,1)} %collective-permute-done.5, bf16[64,2048]{1,0:T(8,128)(2,1)S(1)} %collective-permute-done.3, bf16[64,2048]{1,0:T(8,128)(2,1)S(1)} %collective-permute-done.1), kind=kLoop, calls=%fused_computation | loop fusion | flops 1572864 | bytes 1572864 | tf_op jit(solution)/shard_map/add | solution.py:122
  42.4 1.2 %collective-permute-done.6 = s32[4,128]{1,0:T(4,128)S(1)} collective-permute-done((s32[4,128]{1,0:T(4,128)S(1)}, s32[4,128]{1,0:T(4,128)S(1)}, u32[]{:S(2)}, u32[]{:S(2)}) %collective-permute-start.6) | collective-permute-done | bytes 2080 | tf_op jit(solution)/shard_map/ppermute | solution.py:92
  44.2 1.6 %copy-done.1 = bf16[1,2048,512]{2,1,0:T(8,128)(2,1)S(1)} copy-done((bf16[1,2048,512]{2,1,0:T(8,128)(2,1)S(1)}, bf16[1,2048,512]{2,1,0:T(8,128)(2,1)}, u32[]{:S(2)}) %copy-start.1) | copy-done | bytes 2097176
  45.8 1.3 %hidden.7.refs_0_ = bf16[256,512]{1,0:T(8,128)(2,1)S(1)} custom-call(s32[1]{0:T(128)} %bitcast.1.me_ref, bf16[2048,512]{1,0:T(8,128)(2,1)S(1)} %bitcast.6, bf16[2048,512]{1,0:T(8,128)(2,1)S(1)} %bitcast.11, bf16[128,2048]{1,0:T(8,128)(2,1)S(1)} %copy-done.2, bf16[128,2048]{1,0:T(8,128)(2,1)S(1)} %collective-permute-done.12.refs_1_, s32[4,128]{1,0:T(4,128)S(1)} %bitcast.20, ...), custom_call_target="tpu_custom_call" | custom-call | flops 1073741824 | bytes 5505024 | tf_op jit(solution)/shard_map/hidden/pallas_call | solution.py:40
  47.2 1.6 %collective-permute-start.14 = (bf16[256,512]{1,0:T(8,128)(2,1)S(1)}, bf16[256,512]{1,0:T(8,128)(2,1)}, u32[]{:S(2)}, u32[]{:S(2)}) collective-permute-start(bf16[256,512]{1,0:T(8,128)(2,1)S(1)} %hidden.7.refs_0_), channel_id=1, source_target_pairs={{0,8},{8,0},{1,9},{9,1},{2,10},{10,2},{3,11},{11,3},{4,12},{12,4},... | collective-permute-start | bytes 786440 | tf_op jit(solution)/shard_map/ppermute | solution.py:94
  48.7 1.4 %hidden.9.refs_4_ = bf16[256,512]{1,0:T(8,128)(2,1)S(1)} custom-call(s32[1]{0:T(128)} %bitcast.1.me_ref, bf16[2048,512]{1,0:T(8,128)(2,1)S(1)} %bitcast.7, bf16[2048,512]{1,0:T(8,128)(2,1)S(1)} %bitcast.12, bf16[128,2048]{1,0:T(8,128)(2,1)S(1)} %constant_dynamic-update-slice_fusion.refs_0_, bf16[128,2048]{1,0:T(8,128)(2,1)S(1)} %collective-permute-done.17.refs_1_, ...), custom_call_target="tpu_custom_call" | custom-call | flops 1073741824 | bytes 5505024 | tf_op jit(solution)/shard_map/hidden/pallas_call | solution.py:40
  50.7 2.1 %hidden.8.refs_2_ = bf16[256,512]{1,0:T(8,128)(2,1)} custom-call(s32[1]{0:T(128)} %bitcast.1.me_ref, bf16[2048,512]{1,0:T(8,128)(2,1)S(1)} %bitcast.8, bf16[2048,512]{1,0:T(8,128)(2,1)S(1)} %bitcast.13, bf16[128,2048]{1,0:T(8,128)(2,1)S(1)} %collective-permute-done.4.refs_0_, bf16[128,2048]{1,0:T(8,128)(2,1)S(1)} %collective-permute-done.15.refs_1_, ...), custom_call_target="tpu_custom_call" | custom-call | flops 1073741824 | bytes 5505024 | tf_op jit(solution)/shard_map/hidden/pallas_call | solution.py:40
  52.7 1.5 %collective-permute-start.16 = (bf16[256,512]{1,0:T(8,128)(2,1)}, bf16[256,512]{1,0:T(8,128)(2,1)S(1)}, u32[]{:S(2)}, u32[]{:S(2)}) collective-permute-start(bf16[256,512]{1,0:T(8,128)(2,1)} %hidden.8.refs_2_), channel_id=1, source_target_pairs={{0,8},{8,0},{1,9},{9,1},{2,10},{10,2},{3,11},{11,3},{4,12},{12,4},... | collective-permute-start | bytes 786440 | tf_op jit(solution)/shard_map/ppermute | solution.py:94
  55.6 0.8 hidden.6.refs_2_
  56.4 1.6 %collective-permute-start.19 = (bf16[128,512]{1,0:T(8,128)(2,1)S(1)}, bf16[128,512]{1,0:T(8,128)(2,1)S(1)}, u32[]{:S(2)}, u32[]{:S(2)}) collective-permute-start(bf16[128,512]{1,0:T(8,128)(2,1)S(1)} %hidden.6.refs_2_), channel_id=1, source_target_pairs={{0,8},{8,0},{1,9},{9,1},{2,10},{10,2},{3,11},{11,3},{4,12},{12,4},... | collective-permute-start | bytes 393224 | tf_op jit(solution)/shard_map/ppermute | solution.py:94
  57.9 4.2 %collective-permute-done.18.refs_5_ = bf16[256,512]{1,0:T(8,128)(2,1)} collective-permute-done((bf16[256,512]{1,0:T(8,128)(2,1)S(1)}, bf16[256,512]{1,0:T(8,128)(2,1)}, u32[]{:S(2)}, u32[]{:S(2)}) %collective-permute-start.18) | collective-permute-done | bytes 262176 | tf_op jit(solution)/shard_map/ppermute | solution.py:94
  62.1 5.5 %collective-permute-done.16.refs_3_ = bf16[256,512]{1,0:T(8,128)(2,1)S(1)} collective-permute-done((bf16[256,512]{1,0:T(8,128)(2,1)}, bf16[256,512]{1,0:T(8,128)(2,1)S(1)}, u32[]{:S(2)}, u32[]{:S(2)}) %collective-permute-start.16) | collective-permute-done | bytes 262176 | tf_op jit(solution)/shard_map/ppermute | solution.py:94
  67.6 2.1 %partial_gram.2.refs_3_ = f32[512,512]{1,0:T(8,128)S(1)} custom-call(bf16[256,512]{1,0:T(8,128)(2,1)S(1)} %hidden.7.refs_0_, bf16[256,512]{1,0:T(8,128)(2,1)} %collective-permute-done.14.refs_1_, bf16[256,512]{1,0:T(8,128)(2,1)} %hidden.8.refs_2_, bf16[256,512]{1,0:T(8,128)(2,1)S(1)} %collective-permute-done.16.refs_3_, bf16[256,512]{1,0:T(8,128)(2,1)S(1)} %hidden.9.refs_4_, ...), custom_call_target="tpu_custom_call" | custom-call | flops 805306368 | bytes 2621440 | tf_op jit(solution)/shard_map/partial_gram/pallas_call | solution.py:69
  70.9 1.4 %collective-permute-done.19.refs_0_ = bf16[128,512]{1,0:T(8,128)(2,1)S(1)} collective-permute-done((bf16[128,512]{1,0:T(8,128)(2,1)S(1)}, bf16[128,512]{1,0:T(8,128)(2,1)S(1)}, u32[]{:S(2)}, u32[]{:S(2)}) %collective-permute-start.19) | collective-permute-done | bytes 131104 | tf_op jit(solution)/shard_map/ppermute | solution.py:94
  72.3 12.6 %factor.1 = f32[256,512]{1,0:T(8,128)} custom-call(s32[1]{0:T(128)} %bitcast.rank_ref, f32[512,512]{1,0:T(8,128)S(1)} %partial_gram.3.early_ref, bf16[128,512]{1,0:T(8,128)(2,1)S(1)} %collective-permute-done.19.refs_0_), custom_call_target="tpu_custom_call" | custom-call | tf_op jit(solution)/shard_map/factor/pallas_call | solution.py:282
  (37 shorter events, 6.9 us)
Async XLA Ops:
  0.0 40.1 %copy-start.2 = (bf16[128,2048]{1,0:T(8,128)(2,1)S(1)}, bf16[128,2048]{1,0:T(8,128)(2,1)}, u32[]{:S(2)}) copy-start(bf16[128,2048]{1,0:T(8,128)(2,1)} %refs_0_.1) | copy-start | bytes 1572868
  0.0 40.0 %copy-start.3 = (s32[128,4]{0,1:T(4,128)S(1)}, s32[128,4]{0,1:T(4,128)}, u32[]{:S(2)}) copy-start(s32[128,4]{0,1:T(4,128)} %param.5) | copy-start | bytes 6148
  0.0 44.2 %copy-start = (bf16[1,2048,512]{2,1,0:T(8,128)(2,1)S(1)}, bf16[1,2048,512]{2,1,0:T(8,128)(2,1)}, u32[]{:S(2)}) copy-start(bf16[1,2048,512]{2,1,0:T(8,128)(2,1)} %param.6) | copy-start | bytes 6291460
  0.0 17.8 %collective-permute-start.4 = (bf16[128,2048]{1,0:T(8,128)(2,1)}, bf16[128,2048]{1,0:T(8,128)(2,1)S(1)}, u32[]{:S(2)}, u32[]{:S(2)}) collective-permute-start(bf16[128,2048]{1,0:T(8,128)(2,1)} %refs_0_.1), channel_id=1, source_target_pairs={{0,6},{1,7},{2,0},{3,1},{4,2},{5,3},{6,4},{7,5},{8,14},{9,15},{10,... | collective-permute-start | bytes 1572872 | tf_op jit(solution)/shard_map/ppermute | solution.py:92
  7.0 17.4 %collective-permute-start.2 = (bf16[64,2048]{1,0:T(8,128)(2,1)}, bf16[64,2048]{1,0:T(8,128)(2,1)}, u32[]{:S(2)}, u32[]{:S(2)}) collective-permute-start(bf16[64,2048]{1,0:T(8,128)(2,1)} %get-tuple-element.6), channel_id=1, source_target_pairs={{0,2},{1,3},{2,4},{3,5},{4,6},{5,7},{6,0},{7,1},{8,10},{9,11},{10,... | collective-permute-start | bytes 786440 | tf_op jit(solution)/shard_map/ppermute | solution.py:92
  7.0 21.8 %collective-permute-start = (bf16[64,2048]{1,0:T(8,128)(2,1)}, bf16[64,2048]{1,0:T(8,128)(2,1)S(1)}, u32[]{:S(2)}, u32[]{:S(2)}) collective-permute-start(bf16[64,2048]{1,0:T(8,128)(2,1)} %get-tuple-element.5), channel_id=1, source_target_pairs={{0,2},{1,3},{2,4},{3,5},{4,6},{5,7},{6,0},{7,1},{8,10},{9,11},{10,... | collective-permute-start | bytes 786440 | tf_op jit(solution)/shard_map/ppermute | solution.py:92
  17.8 22.8 %collective-permute-start.5 = (bf16[128,2048]{1,0:T(8,128)(2,1)S(1)}, bf16[128,2048]{1,0:T(8,128)(2,1)}, u32[]{:S(2)}, u32[]{:S(2)}) collective-permute-start(bf16[128,2048]{1,0:T(8,128)(2,1)S(1)} %collective-permute-done.4.refs_0_), channel_id=1, source_target_pairs={{4,2},{5,3},{2,0},{3,1},{12,10},{13,11},{10,8},{11,9},{20,18},{21,... | collective-permute-start | bytes 1572872 | tf_op jit(solution)/shard_map/ppermute | solution.py:92
  19.1 20.9 %collective-permute-start.8 = (s32[4,128]{1,0:T(4,128)}, s32[4,128]{1,0:T(4,128)S(1)}, u32[]{:S(2)}, u32[]{:S(2)}) collective-permute-start(s32[4,128]{1,0:T(4,128)} %bitcast.16), channel_id=1, source_target_pairs={{0,4},{1,5},{2,6},{3,7},{4,0},{5,1},{6,2},{7,3},{8,12},{9,13},{10,... | collective-permute-start | bytes 6152 | tf_op jit(solution)/shard_map/ppermute | solution.py:92
  21.3 20.6 %collective-permute-start.7 = (s32[4,128]{1,0:T(4,128)}, s32[4,128]{1,0:T(4,128)S(1)}, u32[]{:S(2)}, u32[]{:S(2)}) collective-permute-start(s32[4,128]{1,0:T(4,128)} %bitcast.17), channel_id=1, source_target_pairs={{0,2},{1,3},{2,4},{3,5},{4,6},{5,7},{6,0},{7,1},{8,10},{9,11},{10,... | collective-permute-start | bytes 6152 | tf_op jit(solution)/shard_map/ppermute | solution.py:92
  24.4 15.6 %collective-permute-start.3 = (bf16[64,2048]{1,0:T(8,128)(2,1)}, bf16[64,2048]{1,0:T(8,128)(2,1)S(1)}, u32[]{:S(2)}, u32[]{:S(2)}) collective-permute-start(bf16[64,2048]{1,0:T(8,128)(2,1)} %collective-permute-done.2), channel_id=1, source_target_pairs={{2,4},{3,5},{4,6},{5,7},{10,12},{11,13},{12,14},{13,15},{18,20},{1... | collective-permute-start | bytes 786440 | tf_op jit(solution)/shard_map/ppermute | solution.py:92
  28.8 11.3 %collective-permute-start.1 = (bf16[64,2048]{1,0:T(8,128)(2,1)S(1)}, bf16[64,2048]{1,0:T(8,128)(2,1)S(1)}, u32[]{:S(2)}, u32[]{:S(2)}) collective-permute-start(bf16[64,2048]{1,0:T(8,128)(2,1)S(1)} %collective-permute-done), channel_id=1, source_target_pairs={{2,4},{3,5},{4,6},{5,7},{10,12},{11,13},{12,14},{13,15},{18,20},{1... | collective-permute-start | bytes 786440 | tf_op jit(solution)/shard_map/ppermute | solution.py:92
  40.0 3.6 %collective-permute-start.6 = (s32[4,128]{1,0:T(4,128)S(1)}, s32[4,128]{1,0:T(4,128)S(1)}, u32[]{:S(2)}, u32[]{:S(2)}) collective-permute-start(s32[4,128]{1,0:T(4,128)S(1)} %bitcast.18), channel_id=1, source_target_pairs={{0,6},{1,7},{2,0},{3,1},{4,2},{5,3},{6,4},{7,5},{8,14},{9,15},{10,... | collective-permute-start | bytes 6152 | tf_op jit(solution)/shard_map/ppermute | solution.py:92
  40.1 4.2 %collective-permute-start.12 = (bf16[128,2048]{1,0:T(8,128)(2,1)S(1)}, bf16[128,2048]{1,0:T(8,128)(2,1)S(1)}, u32[]{:S(2)}, u32[]{:S(2)}) collective-permute-start(bf16[128,2048]{1,0:T(8,128)(2,1)S(1)} %copy-done.2), channel_id=1, source_target_pairs={{0,1},{1,0},{2,3},{3,2},{4,5},{5,4},{6,7},{7,6},{8,9},{9,8},{10,11... | collective-permute-start | bytes 1572872 | tf_op jit(solution)/shard_map/ppermute | solution.py:93
  40.2 8.6 %collective-permute-start.17 = (bf16[128,2048]{1,0:T(8,128)(2,1)S(1)}, bf16[128,2048]{1,0:T(8,128)(2,1)S(1)}, u32[]{:S(2)}, u32[]{:S(2)}) collective-permute-start(bf16[128,2048]{1,0:T(8,128)(2,1)S(1)} %constant_dynamic-update-slice_fusion.refs_0_), channel_id=1, source_target_pairs={{0,1},{1,0},{2,3},{3,2},{4,5},{5,4},{6,7},{7,6},{8,9},{9,8},{10,11... | collective-permute-start | bytes 1572872 | tf_op jit(solution)/shard_map/ppermute | solution.py:93
  40.6 10.0 %collective-permute-start.15 = (bf16[128,2048]{1,0:T(8,128)(2,1)S(1)}, bf16[128,2048]{1,0:T(8,128)(2,1)S(1)}, u32[]{:S(2)}, u32[]{:S(2)}) collective-permute-start(bf16[128,2048]{1,0:T(8,128)(2,1)S(1)} %collective-permute-done.4.refs_0_), channel_id=1, source_target_pairs={{0,1},{1,0},{2,3},{3,2},{4,5},{5,4},{6,7},{7,6},{8,9},{9,8},{10,11... | collective-permute-start | bytes 1572872 | tf_op jit(solution)/shard_map/ppermute | solution.py:93
  41.9 1.7 %collective-permute-start.13 = (s32[4,128]{1,0:T(4,128)S(1)}, s32[4,128]{1,0:T(4,128)S(1)}, u32[]{:S(2)}, u32[]{:S(2)}) collective-permute-start(s32[4,128]{1,0:T(4,128)S(1)} %bitcast.19), channel_id=1, source_target_pairs={{0,1},{1,0},{2,3},{3,2},{4,5},{5,4},{6,7},{7,6},{8,9},{9,8},{10,11... | collective-permute-start | bytes 6152 | tf_op jit(solution)/shard_map/ppermute | solution.py:93
  43.6 12.0 %collective-permute-start.10 = (bf16[128,2048]{1,0:T(8,128)(2,1)S(1)}, bf16[128,2048]{1,0:T(8,128)(2,1)S(1)}, u32[]{:S(2)}, u32[]{:S(2)}) collective-permute-start(bf16[128,2048]{1,0:T(8,128)(2,1)S(1)} %maximum_add_fusion.refs_0_), channel_id=1, source_target_pairs={{0,1},{1,0},{2,3},{3,2},{4,5},{5,4},{6,7},{7,6},{8,9},{9,8},{10,11... | collective-permute-start | bytes 1572872 | tf_op jit(solution)/shard_map/ppermute | solution.py:93
  43.7 5.1 %collective-permute-start.11 = (s32[12,128]{1,0:T(8,128)S(1)}, s32[12,128]{1,0:T(8,128)S(1)}, u32[]{:S(2)}, u32[]{:S(2)}) collective-permute-start(s32[12,128]{1,0:T(8,128)S(1)} %pad_add_fusion.refs_1_.refs_2_), channel_id=1, source_target_pairs={{0,1},{1,0},{2,3},{3,2},{4,5},{5,4},{6,7},{7,6},{8,9},{9,8},{10,11... | collective-permute-start | bytes 18440 | tf_op jit(solution)/shard_map/ppermute | solution.py:93
  44.2 1.6 %copy-start.1 = (bf16[1,2048,512]{2,1,0:T(8,128)(2,1)S(1)}, bf16[1,2048,512]{2,1,0:T(8,128)(2,1)}, u32[]{:S(2)}) copy-start(bf16[1,2048,512]{2,1,0:T(8,128)(2,1)} %param.7) | copy-start | bytes 6291460
  47.2 10.7 %collective-permute-start.14 = (bf16[256,512]{1,0:T(8,128)(2,1)S(1)}, bf16[256,512]{1,0:T(8,128)(2,1)}, u32[]{:S(2)}, u32[]{:S(2)}) collective-permute-start(bf16[256,512]{1,0:T(8,128)(2,1)S(1)} %hidden.7.refs_0_), channel_id=1, source_target_pairs={{0,8},{8,0},{1,9},{9,1},{2,10},{10,2},{3,11},{11,3},{4,12},{12,4},... | collective-permute-start | bytes 786440 | tf_op jit(solution)/shard_map/ppermute | solution.py:94
  50.1 12.0 %collective-permute-start.18 = (bf16[256,512]{1,0:T(8,128)(2,1)S(1)}, bf16[256,512]{1,0:T(8,128)(2,1)}, u32[]{:S(2)}, u32[]{:S(2)}) collective-permute-start(bf16[256,512]{1,0:T(8,128)(2,1)S(1)} %hidden.9.refs_4_), channel_id=1, source_target_pairs={{0,8},{8,0},{1,9},{9,1},{2,10},{10,2},{3,11},{11,3},{4,12},{12,4},... | collective-permute-start | bytes 786440 | tf_op jit(solution)/shard_map/ppermute | solution.py:94
  52.7 14.9 %collective-permute-start.16 = (bf16[256,512]{1,0:T(8,128)(2,1)}, bf16[256,512]{1,0:T(8,128)(2,1)S(1)}, u32[]{:S(2)}, u32[]{:S(2)}) collective-permute-start(bf16[256,512]{1,0:T(8,128)(2,1)} %hidden.8.refs_2_), channel_id=1, source_target_pairs={{0,8},{8,0},{1,9},{9,1},{2,10},{10,2},{3,11},{11,3},{4,12},{12,4},... | collective-permute-start | bytes 786440 | tf_op jit(solution)/shard_map/ppermute | solution.py:94
  55.0 15.5 %collective-permute-start.9 = (bf16[128,512]{1,0:T(8,128)(2,1)S(1)}, bf16[128,512]{1,0:T(8,128)(2,1)S(1)}, u32[]{:S(2)}, u32[]{:S(2)}) collective-permute-start(bf16[128,512]{1,0:T(8,128)(2,1)S(1)} %hidden.5.refs_0_), channel_id=1, source_target_pairs={{0,8},{8,0},{1,9},{9,1},{2,10},{10,2},{3,11},{11,3},{4,12},{12,4},... | collective-permute-start | bytes 393224 | tf_op jit(solution)/shard_map/ppermute | solution.py:94
  56.4 16.0 %collective-permute-start.19 = (bf16[128,512]{1,0:T(8,128)(2,1)S(1)}, bf16[128,512]{1,0:T(8,128)(2,1)S(1)}, u32[]{:S(2)}, u32[]{:S(2)}) collective-permute-start(bf16[128,512]{1,0:T(8,128)(2,1)S(1)} %hidden.6.refs_2_), channel_id=1, source_target_pairs={{0,8},{8,0},{1,9},{9,1},{2,10},{10,2},{3,11},{11,3},{4,12},{12,4},... | collective-permute-start | bytes 393224 | tf_op jit(solution)/shard_map/ppermute | solution.py:94
